TPU v7x, 512 devices: a whole 4x8x8 slice. The times are simulated.
512 devices in a mesh: sec: 4 (over z_lo), gx: 8 (over z_hi, x), gy: 16 (over y, core).
Axes of the slice: x: 4, y: 8, z: 8 (z_hi: 2, z_lo: 4; z = z_hi * 4 + z_lo), core: 2. Of those that a mesh axis runs over, the one named last changes fastest.
Arguments:
- soil_class: int32 [256, 4096], P('gx', 'gy'), may hold values from 0 to 11
- geology_class: int32 [256, 4096], P('gx', 'gy'), may hold values from 0 to 15
- land_mask: int32 [256, 4096], P('gx', 'gy'), may hold values 0 or 1
- river_mask: int32 [256, 4096], P('gx', 'gy'), may hold values 0 or 1
- elevation: float32 [256, 4096], P('gx', 'gy'), may hold values from -6 to 6
- roughness: float32 [256, 4096], P('gx', 'gy'), may hold values from 0.02 to 0.11
- rainfall: float32 [256, 4096], P('gx', 'gy'), may hold values from 0.05 to 1
- potential_evap: float32 [256, 4096], P('gx', 'gy'), may hold values from 0.05 to 0.5
- surface_head: float32 [256, 4096], P('gx', 'gy'), may hold values from -3 to 3
- pressure: float32 [8, 256, 4096], P('sec', 'gx', 'gy'), may hold values from -6 to 6
- storage: float32 [8, 256, 4096], P('sec', 'gx', 'gy'), may hold values from 0.2 to 2
- soil_embed: bfloat16 [12, 128], replicated, may hold values from -4 to 4
- geology_embed: bfloat16 [16, 128], replicated, may hold values from -4 to 4
- conv_weight: bfloat16 [3, 3, 128, 128], replicated, may hold values from -0.1875 to 0.1875
- out_weight: bfloat16 [128, 8], replicated, may hold values from -0.5 to 0.5
Outputs:
- pressure_out: float32 [8, 256, 4096], P('sec', 'gx', 'gy')
- head_out: float32 [256, 4096], P('gx', 'gy')
All inputs are finite; a program needn't handle non-finite values. No bound on the sum of `land_mask` or of `river_mask` on one device may be relied on, other than what follows from the above.
Results may differ from a plain program's by a relative error of at most 0.0041.
Values sent between devices are 32-bit elements; how exact they have to be, the bound alone decides.
No kernel may reach another device: no remote copies, remote signals or barrier semaphores. Data moves between devices by JAX's collectives and lax.ppermute only.
A program may use at most 64 MiB of HBM per device.

v0:
```python
import jax
import jax.numpy as jnp
from jax import lax
from jax.sharding import PartitionSpec as P

SWEEPS = 4
CYCLES = 4


infil_rate = 0.3
lateral = 1.0
vertical = 0.5


def padded(block, sides, width):
    for axis, dim in sides:
        count = lax.axis_size(axis)
        forward = [(i, i + 1) for i in range(count - 1)]
        backward = [(target, source) for source, target in forward]
        low = lax.ppermute(
            lax.slice_in_dim(block, block.shape[dim] - width, None, axis=dim), axis, forward
        )
        high = lax.ppermute(lax.slice_in_dim(block, 0, width, axis=dim), axis, backward)
        block = jnp.concatenate([low, block, high], axis=dim)
    return block


def spread(value, axis, root):
    mine = lax.axis_index(axis) == root
    return lax.psum(jnp.where(mine, value, jnp.zeros_like(value)), axis)


def infiltration(land_frac, top_cond, surface, top_press):
    return land_frac * (infil_rate * top_cond / (1.0 + top_cond)) * (surface - top_press)


def evaporation_loss(land_frac, potential, top_press):
    return land_frac * potential * jax.nn.sigmoid(top_press)


def surface_flux(level_pad, rough_pad):
    centre_level = level_pad[1:-1, 1:-1]
    centre_rough = rough_pad[1:-1, 1:-1]
    total = jnp.zeros_like(centre_level)
    pairs = (
        (level_pad[2:, 1:-1], rough_pad[2:, 1:-1]),
        (level_pad[:-2, 1:-1], rough_pad[:-2, 1:-1]),
        (level_pad[1:-1, 2:], rough_pad[1:-1, 2:]),
        (level_pad[1:-1, :-2], rough_pad[1:-1, :-2]),
    )
    for near_level, near_rough in pairs:
        total = total + 0.5 * (centre_rough + near_rough) * (near_level - centre_level)
    return total


def shifted(values):
    return [
        (values[:-2, 1:-1, 1:-1], vertical),
        (values[2:, 1:-1, 1:-1], vertical),
        (values[1:-1, :-2, 1:-1], lateral),
        (values[1:-1, 2:, 1:-1], lateral),
        (values[1:-1, 1:-1, 2:], lateral),
        (values[1:-1, 1:-1, :-2], lateral),
    ]


def jacobi_sweep(press_pad, cond_pad, rhs_mid, store_mid):
    cond_mid = cond_pad[1:-1, 1:-1, 1:-1]
    diagonal = store_mid
    total = rhs_mid
    for (near_press, factor), (near_cond, unused) in zip(shifted(press_pad), shifted(cond_pad)):
        face = factor * 0.5 * (cond_mid + near_cond)
        diagonal = diagonal + face
        total = total + face * near_press
    return total / diagonal


def tile_features(soil_class, geology_class, soil_embed, geology_embed):
    soil_onehot = (
        soil_class[:, :, None] == jnp.arange(soil_embed.shape[0], dtype=jnp.int32)
    ).astype(jnp.bfloat16)
    geology_onehot = (
        geology_class[:, :, None] == jnp.arange(geology_embed.shape[0], dtype=jnp.int32)
    ).astype(jnp.bfloat16)
    total = jnp.einsum("xys,sc->xyc", soil_onehot, soil_embed, preferred_element_type=jnp.float32)
    total = total + jnp.einsum(
        "xys,sc->xyc", geology_onehot, geology_embed, preferred_element_type=jnp.float32
    )
    return total.astype(jnp.bfloat16)


def conv_relu(features_pad, kernel):
    convolved = lax.conv_general_dilated(
        features_pad[None],
        kernel,
        (1, 1),
        "VALID",
        dimension_numbers=("NHWC", "HWIO", "NCHW"),
        preferred_element_type=jnp.float32,
    )[0]
    return jax.nn.relu(convolved).astype(jnp.bfloat16)


def shards(
    soil_class,
    geology_class,
    land_mask,
    river_mask,
    elevation,
    roughness,
    rainfall,
    potential_evap,
    surface_head,
    pressure,
    storage,
    soil_embed,
    geology_embed,
    conv_weight,
    out_weight,
):
    sec_count = lax.axis_size("sec")
    sec_index = lax.axis_index("sec")
    layers_dev, tile_rows, tile_cols = pressure.shape
    class_pad = (
        padded(jnp.stack((soil_class + 1, geology_class + 1)), (("gx", 1), ("gy", 2)), 1) - 1
    )
    features_pad = tile_features(class_pad[0], class_pad[1], soil_embed, geology_embed)
    hidden = conv_relu(features_pad, conv_weight)
    own_out = lax.dynamic_slice_in_dim(out_weight, sec_index * layers_dev, layers_dev, 1)
    logits = jnp.einsum("cxy,cl->lxy", hidden, own_out, preferred_element_type=jnp.float32)
    conduct = jnp.exp(logits)
    depth = 1
    coeff_pad = padded(jnp.stack((conduct, storage)), (("sec", 1), ("gx", 2), ("gy", 3)), depth)
    cond_pad = coeff_pad[0]
    top_cond = spread(conduct[0], "sec", 0)
    land_frac = land_mask.astype(jnp.float32)
    river_frac = river_mask.astype(jnp.float32)
    rough = land_frac * (1.0 + river_frac) * roughness
    rough_pad = padded(rough, (("gx", 0), ("gy", 1)), 1)
    strip_rows = tile_rows // sec_count
    first_row = sec_index * strip_rows

    def strip_of(values):
        return lax.dynamic_slice_in_dim(values, first_row, strip_rows, 0)

    strip_land = strip_of(land_frac)
    strip_rain = strip_of(rainfall)
    strip_potential = strip_of(potential_evap)
    strip_cond = strip_of(top_cond)
    strip_rough = lax.dynamic_slice_in_dim(rough_pad, first_row, strip_rows + 2, 0)
    layer_ids = sec_index * layers_dev + jnp.arange(layers_dev, dtype=jnp.int32)
    top_layer = (layer_ids == 0).astype(jnp.float32)[:, None, None]
    surface = surface_head
    press = pressure
    for cycle in range(CYCLES):
        top_press = spread(press[0], "sec", 0)
        level_pad = padded(surface + elevation, (("gx", 0), ("gy", 1)), 1)
        level_strip = lax.dynamic_slice_in_dim(level_pad, first_row, strip_rows + 2, 0)
        flux = surface_flux(level_strip, strip_rough)
        old_strip = strip_of(surface)
        top_strip = strip_of(top_press)
        infil = infiltration(strip_land, strip_cond, old_strip, top_strip)
        evap = evaporation_loss(strip_land, strip_potential, top_strip)
        new_strip = old_strip + strip_land * (strip_rain - infil + flux)
        source_strip = infil - evap
        surface, source = (
            lax.all_gather(new_strip, "sec", axis=0, tiled=True),
            lax.all_gather(source_strip, "sec", axis=0, tiled=True),
        )
        rhs = storage * press + top_layer * source[None]
        for sweep in range(SWEEPS):
            press_pad = padded(press, (("sec", 0), ("gx", 1), ("gy", 2)), 1)
            press = jacobi_sweep(press_pad, cond_pad, rhs, storage)
    return (press, surface)


def solution(mesh):
    in_specs = (
        P("gx", "gy"),
        P("gx", "gy"),
        P("gx", "gy"),
        P("gx", "gy"),
        P("gx", "gy"),
        P("gx", "gy"),
        P("gx", "gy"),
        P("gx", "gy"),
        P("gx", "gy"),
        P("sec", "gx", "gy"),
        P("sec", "gx", "gy"),
        P(),
        P(),
        P(),
        P(),
    )
    out_specs = (P("sec", "gx", "gy"), P("gx", "gy"))
    return jax.shard_map(shards, mesh=mesh, in_specs=in_specs, out_specs=out_specs, check_vma=False)
```

profile of v0, /device:TPU:30, one launch (start us, length us, event | category | flops | bytes accessed | tf_op | source)
XLA Modules:
  0.0 815.6 jit_solution(7540490617223454841)
XLA Ops:
  8.0 10.8 %collective-permute-start = (s32[2,1,256]{2,1,0:T(1,128)S(1)}, s32[2,1,256]{2,1,0:T(1,128)S(1)}, u32[]{:S(2)}, u32[]{:S(2)}) collective-permute-start(s32[2,1,256]{2,1,0:T(1,128)S(1)} %get-tuple-element.138), channel_id=1, source_target_pairs={{0,16},{16,32},{32,48},{48,64},{64,80},{80,96},{96,112},{1,17},{17... | collective-permute-start | bytes 6152 | tf_op jit(solution)/shard_map/ppermute | solution.py:20
  21.6 9.9 %collective-permute-start.38 = (f32[1,256]{1,0:T(1,128)S(1)}, f32[1,256]{1,0:T(1,128)S(1)}, u32[]{:S(2)}, u32[]{:S(2)}) collective-permute-start(f32[1,256]{1,0:T(1,128)S(1)} %get-tuple-element.161), channel_id=1, source_target_pairs={{0,16},{16,32},{32,48},{48,64},{64,80},{80,96},{96,112},{1,17},{17... | collective-permute-start | bytes 3080 | tf_op jit(solution)/shard_map/ppermute | solution.py:20
  34.3 9.9 %collective-permute-start.34 = (f32[1,256]{1,0:T(1,128)S(1)}, f32[1,256]{1,0:T(1,128)S(1)}, u32[]{:S(2)}, u32[]{:S(2)}) collective-permute-start(f32[1,256]{1,0:T(1,128)S(1)} %get-tuple-element.159), channel_id=1, source_target_pairs={{0,16},{16,32},{32,48},{48,64},{64,80},{80,96},{96,112},{1,17},{17... | collective-permute-start | bytes 3080 | tf_op jit(solution)/shard_map/ppermute | solution.py:20
  61.3 4.8 collective-permute-start.36
  85.2 5.4 maximum_convert_fusion
  97.5 8.7 %collective-permute-start.12 = (f32[4,1,256]{2,1,0:T(1,128)S(1)}, f32[4,1,256]{2,1,0:T(1,128)S(1)}, u32[]{:S(2)}, u32[]{:S(2)}) collective-permute-start(f32[4,1,256]{2,1,0:T(1,128)S(1)} %get-tuple-element.91), channel_id=1, source_target_pairs={{0,16},{16,32},{32,48},{48,64},{64,80},{80,96},{96,112},{1,17},{17... | collective-permute-start | bytes 12296 | tf_op jit(solution)/shard_map/ppermute | solution.py:20
  108.2 4.5 collective-permute-start.4
  124.3 6.8 collective-permute-start.6
  133.0 39.1 %all-reduce.3.cloned.1.call-done = (f32[32,256]{1,0:T(8,128)}, f32[32,256]{1,0:T(8,128)}) async-done(((f32[32,256]{1,0:T(8,128)}, f32[32,256]{1,0:T(8,128)}), (f32[32,256]{1,0:T(8,128)}, f32[32,256]{1,0:T(8,128)})) %all-reduce.3.cloned.1.call-update) | async-done | bytes 65552 | tf_op jit(solution)/shard_map/psum | solution.py:30
  179.4 13.1 %all_gather.24 = f32[32,256]{1,0:T(8,128)S(1)} all-gather(f32[8,256]{1,0:T(8,128)S(1)} %get-tuple-element.21), channel_id=1, replica_groups=mesh['sec'=4,'gx'=8,'gy'=16] {'sec'}, dimensions={0}, use_global_device_ids=true | all-gather | bytes 40960 | tf_op jit(solution)/shard_map/all_gather | solution.py:168
  200.2 6.9 collective-permute-start.18
  209.0 9.6 %collective-permute-done.19 = f32[4,1,256]{2,1,0:T(1,128)S(1)} collective-permute-done((f32[4,1,256]{2,1,0:T(1,128)S(1)}, f32[4,1,256]{2,1,0:T(1,128)S(1)}, u32[]{:S(2)}, u32[]{:S(2)}) %collective-permute-start.19) | collective-permute-done | bytes 4128 | tf_op jit(solution)/shard_map/ppermute | solution.py:23
  241.1 13.1 %all_gather.25 = f32[32,256]{1,0:T(8,128)S(1)} all-gather(f32[8,256]{1,0:T(8,128)S(1)} %get-tuple-element.8), channel_id=1, replica_groups=mesh['sec'=4,'gx'=8,'gy'=16] {'sec'}, dimensions={0}, use_global_device_ids=true | all-gather | bytes 40960 | tf_op jit(solution)/shard_map/all_gather | solution.py:167
  258.7 7.9 collective-permute-start.66
  272.4 5.8 collective-permute-done.67
  278.2 8.6 %collective-permute-start.30 = (f32[4,1,256]{2,1,0:T(1,128)S(1)}, f32[4,1,256]{2,1,0:T(1,128)S(1)}, u32[]{:S(2)}, u32[]{:S(2)}) collective-permute-start(f32[4,1,256]{2,1,0:T(1,128)S(1)} %get-tuple-element.83), channel_id=1, source_target_pairs={{0,16},{16,32},{32,48},{48,64},{64,80},{80,96},{96,112},{1,17},{17... | collective-permute-start | bytes 12296 | tf_op jit(solution)/shard_map/ppermute | solution.py:20
  288.8 4.4 collective-permute-start.68
  310.4 19.3 %psum.37 = f32[32,256]{1,0:T(8,128)S(1)} all-reduce(f32[32,256]{1,0:T(8,128)S(1)} %get-tuple-element.127), channel_id=1, replica_groups=mesh['sec'=4,'gx'=8,'gy'=16] {'sec'}, use_global_device_ids=true, to_apply=%region_2.3 | all-reduce | flops 8192 | bytes 65536 | tf_op jit(solution)/shard_map/psum | solution.py:30
  329.8 6.4 collective-permute-start.44
  338.3 9.5 %collective-permute-done.45 = f32[4,1,256]{2,1,0:T(1,128)S(1)} collective-permute-done((f32[4,1,256]{2,1,0:T(1,128)S(1)}, f32[4,1,256]{2,1,0:T(1,128)S(1)}, u32[]{:S(2)}, u32[]{:S(2)}) %collective-permute-start.45) | collective-permute-done | bytes 4128 | tf_op jit(solution)/shard_map/ppermute | solution.py:23
  352.2 13.2 %all_gather.26 = f32[32,256]{1,0:T(8,128)S(1)} all-gather(f32[8,256]{1,0:T(8,128)S(1)} %get-tuple-element.102), channel_id=1, replica_groups=mesh['sec'=4,'gx'=8,'gy'=16] {'sec'}, dimensions={0}, use_global_device_ids=true | all-gather | bytes 40960 | tf_op jit(solution)/shard_map/all_gather | solution.py:168
  378.5 7.6 collective-permute-done.51
  409.4 13.1 %all_gather.27 = f32[32,256]{1,0:T(8,128)S(1)} all-gather(f32[8,256]{1,0:T(8,128)S(1)} %get-tuple-element.101), channel_id=1, replica_groups=mesh['sec'=4,'gx'=8,'gy'=16] {'sec'}, dimensions={0}, use_global_device_ids=true | all-gather | bytes 40960 | tf_op jit(solution)/shard_map/all_gather | solution.py:167
  427.0 8.0 collective-permute-start.94
  439.7 6.8 collective-permute-done.95
  446.5 7.6 collective-permute-start.62
  456.1 7.7 collective-permute-start.96
  467.9 6.4 collective-permute-start.65
  480.0 18.3 %psum.38 = f32[32,256]{1,0:T(8,128)S(1)} all-reduce(f32[32,256]{1,0:T(8,128)S(1)} %get-tuple-element.118), channel_id=1, replica_groups=mesh['sec'=4,'gx'=8,'gy'=16] {'sec'}, use_global_device_ids=true, to_apply=%region_3.4 | all-reduce | flops 8192 | bytes 65536 | tf_op jit(solution)/shard_map/psum | solution.py:30
  498.4 8.2 %collective-permute-start.72 = (f32[4,1,256]{2,1,0:T(1,128)S(1)}, f32[4,1,256]{2,1,0:T(1,128)S(1)}, u32[]{:S(2)}, u32[]{:S(2)}) collective-permute-start(f32[4,1,256]{2,1,0:T(1,128)S(1)} %get-tuple-element.73), channel_id=1, source_target_pairs={{0,16},{16,32},{32,48},{48,64},{64,80},{80,96},{96,112},{1,17},{17... | collective-permute-start | bytes 12296 | tf_op jit(solution)/shard_map/ppermute | solution.py:20
  508.6 9.5 %collective-permute-done.73 = f32[4,1,256]{2,1,0:T(1,128)S(1)} collective-permute-done((f32[4,1,256]{2,1,0:T(1,128)S(1)}, f32[4,1,256]{2,1,0:T(1,128)S(1)}, u32[]{:S(2)}, u32[]{:S(2)}) %collective-permute-start.73) | collective-permute-done | bytes 4128 | tf_op jit(solution)/shard_map/ppermute | solution.py:23
  522.6 13.1 %all_gather.28 = f32[32,256]{1,0:T(8,128)S(1)} all-gather(f32[8,256]{1,0:T(8,128)S(1)} %get-tuple-element.100), channel_id=1, replica_groups=mesh['sec'=4,'gx'=8,'gy'=16] {'sec'}, dimensions={0}, use_global_device_ids=true | all-gather | bytes 40960 | tf_op jit(solution)/shard_map/all_gather | solution.py:168
  548.9 7.6 collective-permute-done.79
  579.7 13.1 %all_gather.29 = f32[32,256]{1,0:T(8,128)S(1)} all-gather(f32[8,256]{1,0:T(8,128)S(1)} %get-tuple-element.99), channel_id=1, replica_groups=mesh['sec'=4,'gx'=8,'gy'=16] {'sec'}, dimensions={0}, use_global_device_ids=true | all-gather | bytes 40960 | tf_op jit(solution)/shard_map/all_gather | solution.py:167
  597.4 7.9 collective-permute-start.122
  610.0 6.8 collective-permute-done.123
  616.8 7.6 collective-permute-start.90
  626.5 7.8 collective-permute-start.124
  638.2 6.4 collective-permute-start.93
  650.5 18.3 %psum.39 = f32[32,256]{1,0:T(8,128)S(1)} all-reduce(f32[32,256]{1,0:T(8,128)S(1)} %get-tuple-element.109), channel_id=1, replica_groups=mesh['sec'=4,'gx'=8,'gy'=16] {'sec'}, use_global_device_ids=true, to_apply=%region_4.5 | all-reduce | flops 8192 | bytes 65536 | tf_op jit(solution)/shard_map/psum | solution.py:30
  668.8 8.1 collective-permute-start.100
  679.0 9.5 %collective-permute-done.101 = f32[4,1,256]{2,1,0:T(1,128)S(1)} collective-permute-done((f32[4,1,256]{2,1,0:T(1,128)S(1)}, f32[4,1,256]{2,1,0:T(1,128)S(1)}, u32[]{:S(2)}, u32[]{:S(2)}) %collective-permute-start.101) | collective-permute-done | bytes 4128 | tf_op jit(solution)/shard_map/ppermute | solution.py:23
  693.0 13.1 %all_gather.30 = f32[32,256]{1,0:T(8,128)S(1)} all-gather(f32[8,256]{1,0:T(8,128)S(1)} %get-tuple-element.98), channel_id=1, replica_groups=mesh['sec'=4,'gx'=8,'gy'=16] {'sec'}, dimensions={0}, use_global_device_ids=true | all-gather | bytes 40960 | tf_op jit(solution)/shard_map/all_gather | solution.py:168
  719.2 7.6 collective-permute-done.107
  750.1 7.6 collective-permute-done.113
  779.3 7.6 collective-permute-done.119
  788.9 5.3 collective-permute-start.121
  794.2 13.2 %all_gather.31 = f32[32,256]{1,0:T(8,128)S(1)} all-gather(f32[8,256]{1,0:T(8,128)S(1)} %get-tuple-element.97), channel_id=1, replica_groups=mesh['sec'=4,'gx'=8,'gy'=16] {'sec'}, dimensions={0}, use_global_device_ids=true | all-gather | bytes 40960 | tf_op jit(solution)/shard_map/all_gather | solution.py:167
  (374 shorter events, 327.6 us)
Async XLA Ops:
  7.2 164.9 %all-reduce.3.cloned.1.call-start = ((), (), s32[]{:S(2)}) async-start(), calls=%async_computation | async-start | bytes 131072 | tf_op jit(solution)/shard_map/psum | solution.py:30
  8.0 58.1 %collective-permute-start = (s32[2,1,256]{2,1,0:T(1,128)S(1)}, s32[2,1,256]{2,1,0:T(1,128)S(1)}, u32[]{:S(2)}, u32[]{:S(2)}) collective-permute-start(s32[2,1,256]{2,1,0:T(1,128)S(1)} %get-tuple-element.138), channel_id=1, source_target_pairs={{0,16},{16,32},{32,48},{48,64},{64,80},{80,96},{96,112},{1,17},{17... | collective-permute-start | bytes 6152 | tf_op jit(solution)/shard_map/ppermute | solution.py:20
  18.9 49.2 %collective-permute-start.1 = (s32[2,1,256]{2,1,0:T(1,128)S(1)}, s32[2,1,256]{2,1,0:T(1,128)S(1)}, u32[]{:S(2)}, u32[]{:S(2)}) collective-permute-start(s32[2,1,256]{2,1,0:T(1,128)S(1)} %get-tuple-element.139), channel_id=1, source_target_pairs={{16,0},{32,16},{48,32},{64,48},{80,64},{96,80},{112,96},{17,1},{33... | collective-permute-start | bytes 6152 | tf_op jit(solution)/shard_map/ppermute | solution.py:23
  21.6 24.8 %collective-permute-start.38 = (f32[1,256]{1,0:T(1,128)S(1)}, f32[1,256]{1,0:T(1,128)S(1)}, u32[]{:S(2)}, u32[]{:S(2)}) collective-permute-start(f32[1,256]{1,0:T(1,128)S(1)} %get-tuple-element.161), channel_id=1, source_target_pairs={{0,16},{16,32},{32,48},{48,64},{64,80},{80,96},{96,112},{1,17},{17... | collective-permute-start | bytes 3080 | tf_op jit(solution)/shard_map/ppermute | solution.py:20
  31.6 16.8 %collective-permute-start.39 = (f32[1,256]{1,0:T(1,128)S(1)}, f32[1,256]{1,0:T(1,128)S(1)}, u32[]{:S(2)}, u32[]{:S(2)}) collective-permute-start(f32[1,256]{1,0:T(1,128)S(1)} %get-tuple-element.162), channel_id=1, source_target_pairs={{16,0},{32,16},{48,32},{64,48},{80,64},{96,80},{112,96},{17,1},{33... | collective-permute-start | bytes 3080 | tf_op jit(solution)/shard_map/ppermute | solution.py:23
  34.3 17.5 %collective-permute-start.34 = (f32[1,256]{1,0:T(1,128)S(1)}, f32[1,256]{1,0:T(1,128)S(1)}, u32[]{:S(2)}, u32[]{:S(2)}) collective-permute-start(f32[1,256]{1,0:T(1,128)S(1)} %get-tuple-element.159), channel_id=1, source_target_pairs={{0,16},{16,32},{32,48},{48,64},{64,80},{80,96},{96,112},{1,17},{17... | collective-permute-start | bytes 3080 | tf_op jit(solution)/shard_map/ppermute | solution.py:20
  48.3 49.1 %collective-permute-start.10 = (f32[1,32,256]{2,1,0:T(8,128)S(1)}, f32[1,32,256]{2,1,0:T(8,128)S(1)}, u32[]{:S(2)}, u32[]{:S(2)}) collective-permute-start(f32[1,32,256]{2,1,0:T(8,128)S(1)} %get-tuple-element.141), channel_id=1, source_target_pairs={{0,128},{128,256},{256,384},{1,129},{129,257},{257,385},{2,130},{1... | collective-permute-start | bytes 98312 | tf_op jit(solution)/shard_map/ppermute | solution.py:20
  59.9 37.6 %collective-permute-start.11 = (f32[1,32,256]{2,1,0:T(8,128)S(1)}, f32[1,32,256]{2,1,0:T(8,128)S(1)}, u32[]{:S(2)}, u32[]{:S(2)}) collective-permute-start(f32[1,32,256]{2,1,0:T(8,128)S(1)} %get-tuple-element.142), channel_id=1, source_target_pairs={{128,0},{256,128},{384,256},{129,1},{257,129},{385,257},{130,2},{2... | collective-permute-start | bytes 98312 | tf_op jit(solution)/shard_map/ppermute | solution.py:23
  97.5 16.6 %collective-permute-start.12 = (f32[4,1,256]{2,1,0:T(1,128)S(1)}, f32[4,1,256]{2,1,0:T(1,128)S(1)}, u32[]{:S(2)}, u32[]{:S(2)}) collective-permute-start(f32[4,1,256]{2,1,0:T(1,128)S(1)} %get-tuple-element.91), channel_id=1, source_target_pairs={{0,16},{16,32},{32,48},{48,64},{64,80},{80,96},{96,112},{1,17},{17... | collective-permute-start | bytes 12296 | tf_op jit(solution)/shard_map/ppermute | solution.py:20
  108.2 16.0 %collective-permute-start.4 = (f32[2,1,32,256]{3,2,1,0:T(8,128)S(1)}, f32[2,1,32,256]{3,2,1,0:T(8,128)S(1)}, u32[]{:S(2)}, u32[]{:S(2)}) collective-permute-start(f32[2,1,32,256]{3,2,1,0:T(8,128)S(1)} %get-tuple-element.89), channel_id=1, source_target_pairs={{0,128},{128,256},{256,384},{1,129},{129,257},{257,385},{2,130},{1... | collective-permute-start | bytes 196616 | tf_op jit(solution)/shard_map/ppermute | solution.py:20
  117.9 74.9 %collective-permute-start.14 = (f32[4,34,1]{2,1,0:T(8,128)S(1)}, f32[4,34,1]{2,1,0:T(8,128)S(1)}, u32[]{:S(2)}, u32[]{:S(2)}) collective-permute-start(f32[4,34,1]{2,1,0:T(8,128)S(1)} %get-tuple-element.57), channel_id=1, source_target_pairs={{1,0},{2,1},{3,2},{4,3},{5,4},{6,5},{7,6},{8,7},{9,8},{10,9},{11,1... | collective-permute-start | bytes 1640 | tf_op jit(solution)/shard_map/ppermute | solution.py:23
  119.9 72.9 %collective-permute-start.15 = (f32[4,34,1]{2,1,0:T(8,128)S(1)}, f32[4,34,1]{2,1,0:T(8,128)S(1)}, u32[]{:S(2)}, u32[]{:S(2)}) collective-permute-start(f32[4,34,1]{2,1,0:T(8,128)S(1)} %get-tuple-element.58), channel_id=1, source_target_pairs={{0,1},{1,2},{2,3},{3,4},{4,5},{5,6},{6,7},{7,8},{8,9},{9,10},{10,1... | collective-permute-start | bytes 1640 | tf_op jit(solution)/shard_map/ppermute | solution.py:20
  124.3 49.4 %collective-permute-start.6 = (f32[2,4,1,256]{3,2,1,0:T(1,128)S(1)}, f32[2,4,1,256]{3,2,1,0:T(1,128)S(1)}, u32[]{:S(2)}, u32[]{:S(2)}) collective-permute-start(f32[2,4,1,256]{3,2,1,0:T(1,128)S(1)} %get-tuple-element.25), channel_id=1, source_target_pairs={{0,16},{16,32},{32,48},{48,64},{64,80},{80,96},{96,112},{1,17},{17... | collective-permute-start | bytes 24584 | tf_op jit(solution)/shard_map/ppermute | solution.py:20
  131.1 42.6 %collective-permute-start.7 = (f32[2,4,1,256]{3,2,1,0:T(1,128)S(1)}, f32[2,4,1,256]{3,2,1,0:T(1,128)S(1)}, u32[]{:S(2)}, u32[]{:S(2)}) collective-permute-start(f32[2,4,1,256]{3,2,1,0:T(1,128)S(1)} %get-tuple-element.26), channel_id=1, source_target_pairs={{16,0},{32,16},{48,32},{64,48},{80,64},{96,80},{112,96},{17,1},{33... | collective-permute-start | bytes 24584 | tf_op jit(solution)/shard_map/ppermute | solution.py:23
  173.9 18.7 %collective-permute-start.8 = (f32[2,4,34,1]{3,2,1,0:T(8,128)S(1)}, f32[2,4,34,1]{3,2,1,0:T(8,128)S(1)}, u32[]{:S(2)}, u32[]{:S(2)}) collective-permute-start(f32[2,4,34,1]{3,2,1,0:T(8,128)S(1)} %get-tuple-element.23), channel_id=1, source_target_pairs={{0,1},{1,2},{2,3},{3,4},{4,5},{5,6},{6,7},{7,8},{8,9},{9,10},{10,1... | collective-permute-start | bytes 3272 | tf_op jit(solution)/shard_map/ppermute | solution.py:20
  175.8 16.8 %collective-permute-start.9 = (f32[2,4,34,1]{3,2,1,0:T(8,128)S(1)}, f32[2,4,34,1]{3,2,1,0:T(8,128)S(1)}, u32[]{:S(2)}, u32[]{:S(2)}) collective-permute-start(f32[2,4,34,1]{3,2,1,0:T(8,128)S(1)} %get-tuple-element.24), channel_id=1, source_target_pairs={{1,0},{2,1},{3,2},{4,3},{5,4},{6,5},{7,6},{8,7},{9,8},{10,9},{11,1... | collective-permute-start | bytes 3272 | tf_op jit(solution)/shard_map/ppermute | solution.py:23
  235.2 19.0 %collective-permute-start.24 = (f32[4,1,256]{2,1,0:T(1,128)S(1)}, f32[4,1,256]{2,1,0:T(1,128)S(1)}, u32[]{:S(2)}, u32[]{:S(2)}) collective-permute-start(f32[4,1,256]{2,1,0:T(1,128)S(1)} %get-tuple-element.85), channel_id=1, source_target_pairs={{0,16},{16,32},{32,48},{48,64},{64,80},{80,96},{96,112},{1,17},{17... | collective-permute-start | bytes 12296 | tf_op jit(solution)/shard_map/ppermute | solution.py:20
  237.1 17.1 %collective-permute-start.25 = (f32[4,1,256]{2,1,0:T(1,128)S(1)}, f32[4,1,256]{2,1,0:T(1,128)S(1)}, u32[]{:S(2)}, u32[]{:S(2)}) collective-permute-start(f32[4,1,256]{2,1,0:T(1,128)S(1)} %get-tuple-element.86), channel_id=1, source_target_pairs={{16,0},{32,16},{48,32},{64,48},{80,64},{96,80},{112,96},{17,1},{33... | collective-permute-start | bytes 12296 | tf_op jit(solution)/shard_map/ppermute | solution.py:23
  254.3 14.4 %collective-permute-start.26 = (f32[4,34,1]{2,1,0:T(8,128)S(1)}, f32[4,34,1]{2,1,0:T(8,128)S(1)}, u32[]{:S(2)}, u32[]{:S(2)}) collective-permute-start(f32[4,34,1]{2,1,0:T(8,128)S(1)} %get-tuple-element.53), channel_id=1, source_target_pairs={{1,0},{2,1},{3,2},{4,3},{5,4},{6,5},{7,6},{8,7},{9,8},{10,9},{11,1... | collective-permute-start | bytes 1640 | tf_op jit(solution)/shard_map/ppermute | solution.py:23
  258.7 13.7 %collective-permute-start.66 = (f32[1,256]{1,0:T(1,128)S(1)}, f32[1,256]{1,0:T(1,128)S(1)}, u32[]{:S(2)}, u32[]{:S(2)}) collective-permute-start(f32[1,256]{1,0:T(1,128)S(1)} %get-tuple-element.157), channel_id=1, source_target_pairs={{0,16},{16,32},{32,48},{48,64},{64,80},{80,96},{96,112},{1,17},{17... | collective-permute-start | bytes 3080 | tf_op jit(solution)/shard_map/ppermute | solution.py:20
  278.2 16.9 %collective-permute-start.30 = (f32[4,1,256]{2,1,0:T(1,128)S(1)}, f32[4,1,256]{2,1,0:T(1,128)S(1)}, u32[]{:S(2)}, u32[]{:S(2)}) collective-permute-start(f32[4,1,256]{2,1,0:T(1,128)S(1)} %get-tuple-element.83), channel_id=1, source_target_pairs={{0,16},{16,32},{32,48},{48,64},{64,80},{80,96},{96,112},{1,17},{17... | collective-permute-start | bytes 12296 | tf_op jit(solution)/shard_map/ppermute | solution.py:20
  288.8 14.8 %collective-permute-start.68 = (f32[34,1]{1,0:T(8,128)S(1)}, f32[34,1]{1,0:T(8,128)S(1)}, u32[]{:S(2)}, u32[]{:S(2)}) collective-permute-start(f32[34,1]{1,0:T(8,128)S(1)} %get-tuple-element.148), channel_id=1, source_target_pairs={{0,1},{1,2},{2,3},{3,4},{4,5},{5,6},{6,7},{7,8},{8,9},{9,10},{10,1... | collective-permute-start | bytes 416 | tf_op jit(solution)/shard_map/ppermute | solution.py:20
  306.3 23.5 %collective-permute-start.42 = (f32[1,32,256]{2,1,0:T(8,128)S(1)}, f32[1,32,256]{2,1,0:T(8,128)S(1)}, u32[]{:S(2)}, u32[]{:S(2)}) collective-permute-start(f32[1,32,256]{2,1,0:T(8,128)S(1)} %get-tuple-element.128), channel_id=1, source_target_pairs={{0,128},{128,256},{256,384},{1,129},{129,257},{257,385},{2,130},{1... | collective-permute-start | bytes 98312 | tf_op jit(solution)/shard_map/ppermute | solution.py:20
  309.1 20.6 %collective-permute-start.43 = (f32[1,32,256]{2,1,0:T(8,128)S(1)}, f32[1,32,256]{2,1,0:T(8,128)S(1)}, u32[]{:S(2)}, u32[]{:S(2)}) collective-permute-start(f32[1,32,256]{2,1,0:T(8,128)S(1)} %get-tuple-element.129), channel_id=1, source_target_pairs={{128,0},{256,128},{384,256},{129,1},{257,129},{385,257},{130,2},{2... | collective-permute-start | bytes 98312 | tf_op jit(solution)/shard_map/ppermute | solution.py:23
  347.9 17.5 %collective-permute-start.46 = (f32[4,34,1]{2,1,0:T(8,128)S(1)}, f32[4,34,1]{2,1,0:T(8,128)S(1)}, u32[]{:S(2)}, u32[]{:S(2)}) collective-permute-start(f32[4,34,1]{2,1,0:T(8,128)S(1)} %get-tuple-element.49), channel_id=1, source_target_pairs={{1,0},{2,1},{3,2},{4,3},{5,4},{6,5},{7,6},{8,7},{9,8},{10,9},{11,1... | collective-permute-start | bytes 1640 | tf_op jit(solution)/shard_map/ppermute | solution.py:23
  349.8 15.6 %collective-permute-start.47 = (f32[4,34,1]{2,1,0:T(8,128)S(1)}, f32[4,34,1]{2,1,0:T(8,128)S(1)}, u32[]{:S(2)}, u32[]{:S(2)}) collective-permute-start(f32[4,34,1]{2,1,0:T(8,128)S(1)} %get-tuple-element.50), channel_id=1, source_target_pairs={{0,1},{1,2},{2,3},{3,4},{4,5},{5,6},{6,7},{7,8},{8,9},{9,10},{10,1... | collective-permute-start | bytes 1640 | tf_op jit(solution)/shard_map/ppermute | solution.py:20
  403.5 19.0 %collective-permute-start.56 = (f32[4,1,256]{2,1,0:T(1,128)S(1)}, f32[4,1,256]{2,1,0:T(1,128)S(1)}, u32[]{:S(2)}, u32[]{:S(2)}) collective-permute-start(f32[4,1,256]{2,1,0:T(1,128)S(1)} %get-tuple-element.77), channel_id=1, source_target_pairs={{0,16},{16,32},{32,48},{48,64},{64,80},{80,96},{96,112},{1,17},{17... | collective-permute-start | bytes 12296 | tf_op jit(solution)/shard_map/ppermute | solution.py:20
  405.4 17.1 %collective-permute-start.57 = (f32[4,1,256]{2,1,0:T(1,128)S(1)}, f32[4,1,256]{2,1,0:T(1,128)S(1)}, u32[]{:S(2)}, u32[]{:S(2)}) collective-permute-start(f32[4,1,256]{2,1,0:T(1,128)S(1)} %get-tuple-element.78), channel_id=1, source_target_pairs={{16,0},{32,16},{48,32},{64,48},{80,64},{96,80},{112,96},{17,1},{33... | collective-permute-start | bytes 12296 | tf_op jit(solution)/shard_map/ppermute | solution.py:23
  422.6 14.3 %collective-permute-start.58 = (f32[4,34,1]{2,1,0:T(8,128)S(1)}, f32[4,34,1]{2,1,0:T(8,128)S(1)}, u32[]{:S(2)}, u32[]{:S(2)}) collective-permute-start(f32[4,34,1]{2,1,0:T(8,128)S(1)} %get-tuple-element.45), channel_id=1, source_target_pairs={{1,0},{2,1},{3,2},{4,3},{5,4},{6,5},{7,6},{8,7},{9,8},{10,9},{11,1... | collective-permute-start | bytes 1640 | tf_op jit(solution)/shard_map/ppermute | solution.py:23
  427.0 12.7 %collective-permute-start.94 = (f32[1,256]{1,0:T(1,128)S(1)}, f32[1,256]{1,0:T(1,128)S(1)}, u32[]{:S(2)}, u32[]{:S(2)}) collective-permute-start(f32[1,256]{1,0:T(1,128)S(1)} %get-tuple-element.155), channel_id=1, source_target_pairs={{0,16},{16,32},{32,48},{48,64},{64,80},{80,96},{96,112},{1,17},{17... | collective-permute-start | bytes 3080 | tf_op jit(solution)/shard_map/ppermute | solution.py:20
  446.5 19.3 %collective-permute-start.62 = (f32[4,1,256]{2,1,0:T(1,128)S(1)}, f32[4,1,256]{2,1,0:T(1,128)S(1)}, u32[]{:S(2)}, u32[]{:S(2)}) collective-permute-start(f32[4,1,256]{2,1,0:T(1,128)S(1)} %get-tuple-element.75), channel_id=1, source_target_pairs={{0,16},{16,32},{32,48},{48,64},{64,80},{80,96},{96,112},{1,17},{17... | collective-permute-start | bytes 12296 | tf_op jit(solution)/shard_map/ppermute | solution.py:20
  456.1 18.1 %collective-permute-start.96 = (f32[34,1]{1,0:T(8,128)S(1)}, f32[34,1]{1,0:T(8,128)S(1)}, u32[]{:S(2)}, u32[]{:S(2)}) collective-permute-start(f32[34,1]{1,0:T(8,128)S(1)} %get-tuple-element.146), channel_id=1, source_target_pairs={{0,1},{1,2},{2,3},{3,4},{4,5},{5,6},{6,7},{7,8},{8,9},{9,10},{10,1... | collective-permute-start | bytes 416 | tf_op jit(solution)/shard_map/ppermute | solution.py:20
  475.3 23.0 %collective-permute-start.70 = (f32[1,32,256]{2,1,0:T(8,128)S(1)}, f32[1,32,256]{2,1,0:T(8,128)S(1)}, u32[]{:S(2)}, u32[]{:S(2)}) collective-permute-start(f32[1,32,256]{2,1,0:T(8,128)S(1)} %get-tuple-element.119), channel_id=1, source_target_pairs={{0,128},{128,256},{256,384},{1,129},{129,257},{257,385},{2,130},{1... | collective-permute-start | bytes 98312 | tf_op jit(solution)/shard_map/ppermute | solution.py:20
  478.7 19.6 %collective-permute-start.71 = (f32[1,32,256]{2,1,0:T(8,128)S(1)}, f32[1,32,256]{2,1,0:T(8,128)S(1)}, u32[]{:S(2)}, u32[]{:S(2)}) collective-permute-start(f32[1,32,256]{2,1,0:T(8,128)S(1)} %get-tuple-element.120), channel_id=1, source_target_pairs={{128,0},{256,128},{384,256},{129,1},{257,129},{385,257},{130,2},{2... | collective-permute-start | bytes 98312 | tf_op jit(solution)/shard_map/ppermute | solution.py:23
  518.2 17.5 %collective-permute-start.74 = (f32[4,34,1]{2,1,0:T(8,128)S(1)}, f32[4,34,1]{2,1,0:T(8,128)S(1)}, u32[]{:S(2)}, u32[]{:S(2)}) collective-permute-start(f32[4,34,1]{2,1,0:T(8,128)S(1)} %get-tuple-element.41), channel_id=1, source_target_pairs={{1,0},{2,1},{3,2},{4,3},{5,4},{6,5},{7,6},{8,7},{9,8},{10,9},{11,1... | collective-permute-start | bytes 1640 | tf_op jit(solution)/shard_map/ppermute | solution.py:23
  520.2 15.6 %collective-permute-start.75 = (f32[4,34,1]{2,1,0:T(8,128)S(1)}, f32[4,34,1]{2,1,0:T(8,128)S(1)}, u32[]{:S(2)}, u32[]{:S(2)}) collective-permute-start(f32[4,34,1]{2,1,0:T(8,128)S(1)} %get-tuple-element.42), channel_id=1, source_target_pairs={{0,1},{1,2},{2,3},{3,4},{4,5},{5,6},{6,7},{7,8},{8,9},{9,10},{10,1... | collective-permute-start | bytes 1640 | tf_op jit(solution)/shard_map/ppermute | solution.py:20
  573.9 19.0 %collective-permute-start.84 = (f32[4,1,256]{2,1,0:T(1,128)S(1)}, f32[4,1,256]{2,1,0:T(1,128)S(1)}, u32[]{:S(2)}, u32[]{:S(2)}) collective-permute-start(f32[4,1,256]{2,1,0:T(1,128)S(1)} %get-tuple-element.69), channel_id=1, source_target_pairs={{0,16},{16,32},{32,48},{48,64},{64,80},{80,96},{96,112},{1,17},{17... | collective-permute-start | bytes 12296 | tf_op jit(solution)/shard_map/ppermute | solution.py:20
  575.8 17.1 %collective-permute-start.85 = (f32[4,1,256]{2,1,0:T(1,128)S(1)}, f32[4,1,256]{2,1,0:T(1,128)S(1)}, u32[]{:S(2)}, u32[]{:S(2)}) collective-permute-start(f32[4,1,256]{2,1,0:T(1,128)S(1)} %get-tuple-element.70), channel_id=1, source_target_pairs={{16,0},{32,16},{48,32},{64,48},{80,64},{96,80},{112,96},{17,1},{33... | collective-permute-start | bytes 12296 | tf_op jit(solution)/shard_map/ppermute | solution.py:23
  593.0 14.2 %collective-permute-start.86 = (f32[4,34,1]{2,1,0:T(8,128)S(1)}, f32[4,34,1]{2,1,0:T(8,128)S(1)}, u32[]{:S(2)}, u32[]{:S(2)}) collective-permute-start(f32[4,34,1]{2,1,0:T(8,128)S(1)} %get-tuple-element.37), channel_id=1, source_target_pairs={{1,0},{2,1},{3,2},{4,3},{5,4},{6,5},{7,6},{8,7},{9,8},{10,9},{11,1... | collective-permute-start | bytes 1640 | tf_op jit(solution)/shard_map/ppermute | solution.py:23
  597.4 12.6 %collective-permute-start.122 = (f32[1,256]{1,0:T(1,128)S(1)}, f32[1,256]{1,0:T(1,128)S(1)}, u32[]{:S(2)}, u32[]{:S(2)}) collective-permute-start(f32[1,256]{1,0:T(1,128)S(1)} %get-tuple-element.153), channel_id=1, source_target_pairs={{0,16},{16,32},{32,48},{48,64},{64,80},{80,96},{96,112},{1,17},{17... | collective-permute-start | bytes 3080 | tf_op jit(solution)/shard_map/ppermute | solution.py:20
  616.8 19.3 %collective-permute-start.90 = (f32[4,1,256]{2,1,0:T(1,128)S(1)}, f32[4,1,256]{2,1,0:T(1,128)S(1)}, u32[]{:S(2)}, u32[]{:S(2)}) collective-permute-start(f32[4,1,256]{2,1,0:T(1,128)S(1)} %get-tuple-element.67), channel_id=1, source_target_pairs={{0,16},{16,32},{32,48},{48,64},{64,80},{80,96},{96,112},{1,17},{17... | collective-permute-start | bytes 12296 | tf_op jit(solution)/shard_map/ppermute | solution.py:20
  626.5 18.2 %collective-permute-start.124 = (f32[34,1]{1,0:T(8,128)S(1)}, f32[34,1]{1,0:T(8,128)S(1)}, u32[]{:S(2)}, u32[]{:S(2)}) collective-permute-start(f32[34,1]{1,0:T(8,128)S(1)} %get-tuple-element.144), channel_id=1, source_target_pairs={{0,1},{1,2},{2,3},{3,4},{4,5},{5,6},{6,7},{7,8},{8,9},{9,10},{10,1... | collective-permute-start | bytes 416 | tf_op jit(solution)/shard_map/ppermute | solution.py:20
  645.7 23.1 %collective-permute-start.98 = (f32[1,32,256]{2,1,0:T(8,128)S(1)}, f32[1,32,256]{2,1,0:T(8,128)S(1)}, u32[]{:S(2)}, u32[]{:S(2)}) collective-permute-start(f32[1,32,256]{2,1,0:T(8,128)S(1)} %get-tuple-element.110), channel_id=1, source_target_pairs={{0,128},{128,256},{256,384},{1,129},{129,257},{257,385},{2,130},{1... | collective-permute-start | bytes 98312 | tf_op jit(solution)/shard_map/ppermute | solution.py:20
  649.2 19.6 %collective-permute-start.99 = (f32[1,32,256]{2,1,0:T(8,128)S(1)}, f32[1,32,256]{2,1,0:T(8,128)S(1)}, u32[]{:S(2)}, u32[]{:S(2)}) collective-permute-start(f32[1,32,256]{2,1,0:T(8,128)S(1)} %get-tuple-element.111), channel_id=1, source_target_pairs={{128,0},{256,128},{384,256},{129,1},{257,129},{385,257},{130,2},{2... | collective-permute-start | bytes 98312 | tf_op jit(solution)/shard_map/ppermute | solution.py:23
  688.6 17.5 %collective-permute-start.102 = (f32[4,34,1]{2,1,0:T(8,128)S(1)}, f32[4,34,1]{2,1,0:T(8,128)S(1)}, u32[]{:S(2)}, u32[]{:S(2)}) collective-permute-start(f32[4,34,1]{2,1,0:T(8,128)S(1)} %get-tuple-element.33), channel_id=1, source_target_pairs={{1,0},{2,1},{3,2},{4,3},{5,4},{6,5},{7,6},{8,7},{9,8},{10,9},{11,1... | collective-permute-start | bytes 1640 | tf_op jit(solution)/shard_map/ppermute | solution.py:23
  690.5 15.6 %collective-permute-start.103 = (f32[4,34,1]{2,1,0:T(8,128)S(1)}, f32[4,34,1]{2,1,0:T(8,128)S(1)}, u32[]{:S(2)}, u32[]{:S(2)}) collective-permute-start(f32[4,34,1]{2,1,0:T(8,128)S(1)} %get-tuple-element.34), channel_id=1, source_target_pairs={{0,1},{1,2},{2,3},{3,4},{4,5},{5,6},{6,7},{7,8},{8,9},{9,10},{10,1... | collective-permute-start | bytes 1640 | tf_op jit(solution)/shard_map/ppermute | solution.py:20
  787.0 20.4 %collective-permute-start.120 = (f32[4,34,1]{2,1,0:T(8,128)S(1)}, f32[4,34,1]{2,1,0:T(8,128)S(1)}, u32[]{:S(2)}, u32[]{:S(2)}) collective-permute-start(f32[4,34,1]{2,1,0:T(8,128)S(1)} %get-tuple-element.27), channel_id=1, source_target_pairs={{1,0},{2,1},{3,2},{4,3},{5,4},{6,5},{7,6},{8,7},{9,8},{10,9},{11,1... | collective-permute-start | bytes 1640 | tf_op jit(solution)/shard_map/ppermute | solution.py:23
  788.9 18.5 %collective-permute-start.121 = (f32[4,34,1]{2,1,0:T(8,128)S(1)}, f32[4,34,1]{2,1,0:T(8,128)S(1)}, u32[]{:S(2)}, u32[]{:S(2)}) collective-permute-start(f32[4,34,1]{2,1,0:T(8,128)S(1)} %get-tuple-element.28), channel_id=1, source_target_pairs={{0,1},{1,2},{2,3},{3,4},{4,5},{5,6},{6,7},{7,8},{8,9},{9,10},{10,1... | collective-permute-start | bytes 1640 | tf_op jit(solution)/shard_map/ppermute | solution.py:20
  (87 other events, 952.7 us)
Sparse Core Ops, SparseCore 0:
  114.2 57.8 all-reduce.2
where the time goes:
time: 824 us; the launch traced here: 816 us
  starting transfers between devices  399 us (48%)
  waiting for transfers between devices  204 us (25%)
  blocking collectives  161 us (20%)
  between operations  16.3 us (2%)
  local copies, waits for them, and re-layouts  13.5 us (2%)
  other arithmetic  11.3 us (1%)
  matrix products  9.98 us (1%)
    ppermute x63, starting transfers between devices, padded(): lax.ppermute(lax.slice_in_dim(block, block.shape[dim] - width, None, axis...  270 us
    ppermute x63, waiting for transfers between devices, padded(): lax.ppermute(lax.slice_in_dim(block, 0, width, axis=dim), axis, backward)  146 us
    ppermute x63, starting transfers between devices, padded(): lax.ppermute(lax.slice_in_dim(block, 0, width, axis=dim), axis, backward)  129 us
    psum x3, blocking collectives, spread(): return lax.psum(jnp.where(mine, value, jnp.zeros_like(value)), axis)  55.9 us
    all_gather x4, blocking collectives, shards(): lax.all_gather(source_strip, 'sec', axis=0, tiled=True)  52.6 us
    all_gather x4, blocking collectives, shards(): lax.all_gather(new_strip, 'sec', axis=0, tiled=True)  52.6 us
    psum x1, waiting for transfers between devices, spread(): return lax.psum(jnp.where(mine, value, jnp.zeros_like(value)), axis)  39.1 us
    ppermute x63, waiting for transfers between devices, padded(): lax.ppermute(lax.slice_in_dim(block, block.shape[dim] - width, None, axis...  18.8 us
  transfers between devices with their start and end apart: 127, of which 44 were waited for; matrix products, arithmetic and copies ran while one was open for 4% of the time, Pallas kernels for 0%

commit v1 on v0

v1 whole, which is shorter than its diff:
```python
import functools

import jax
import jax.numpy as jnp
import numpy as np
from jax import lax
from jax.experimental import pallas as pl
from jax.experimental.pallas import tpu as pltpu
from jax.sharding import PartitionSpec as P

SWEEPS = 4
CYCLES = 4
HALO = SWEEPS * CYCLES
LANES = 128
CHUNK = 64
EDGE = (LANES - CHUNK) // 2
CROWS = 24
NSOIL = 12
NGEO = 16
KSOIL = 9 * NGEO
KROWS = 256

infil_rate = 0.3
lateral = 1.0
vertical = 0.5

VMEM = pl.BlockSpec(memory_space=pltpu.VMEM)
SMEM = pl.BlockSpec(memory_space=pltpu.SMEM)
f32 = jnp.float32
bf16 = jnp.bfloat16


def call(kernel, outs, n_in, scratch=(), smem=(), name=None):
    return pl.pallas_call(
        kernel,
        out_shape=outs,
        in_specs=[SMEM if i in smem else VMEM for i in range(n_in)],
        out_specs=jax.tree.map(lambda _: VMEM, outs),
        scratch_shapes=scratch,
        name=name,
    )


def swap_pairs(count, first):
    out = []
    for i in range(first, count - 1, 2):
        out += [(i, i + 1), (i + 1, i)]
    return out


def table_layout():
    sel = np.zeros((KROWS, NSOIL + NGEO), np.float32)
    tap = np.full((KROWS, LANES), -1, np.int32)
    for k in range(KSOIL):
        sel[k, NSOIL + k % NGEO] = 1
        tap[k] = k // NGEO
    for j in range(9 * NSOIL):
        sel[KSOIL + j, j % NSOIL] = 1
        tap[KSOIL + j] = j // NSOIL
    return sel, tap


def table_kernel(sel_ref, tap_ref, soil_ref, geo_ref, weight_ref, out_ref, table_ref, proj_ref):
    sel = sel_ref[...].astype(bf16)
    embed = jnp.dot(sel[:, :NSOIL], soil_ref[...], preferred_element_type=f32)
    embed = embed + jnp.dot(sel[:, NSOIL:], geo_ref[...], preferred_element_type=f32)
    tap = tap_ref[...]
    total = jnp.zeros((LANES, KROWS), f32)
    for t in range(9):
        mine = jnp.where(tap == t, embed, 0.0).astype(bf16)
        total = total + lax.dot_general(
            weight_ref[t], mine, (((0,), (1,)), ((), ())), preferred_element_type=f32
        )
    high = total.astype(bf16)
    table_ref[0:LANES, :] = high
    table_ref[LANES : 2 * LANES, :] = (total - high.astype(f32)).astype(bf16)
    eye = (
        lax.broadcasted_iota(jnp.int32, (LANES, LANES), 0)
        == lax.broadcasted_iota(jnp.int32, (LANES, LANES), 1)
    ).astype(f32).astype(bf16)
    proj_ref[...] = lax.dot_general(
        out_ref[...], eye, (((0,), (0,)), ((), ())), preferred_element_type=f32
    ).astype(bf16)


def columns(soil, geo, land, river, elev, rough, rain, evap, head):
    landf = land.astype(f32)
    conveyance = landf * (1.0 + river.astype(f32)) * rough
    return (
        [conveyance, rain, evap, elev, head],
        [(soil + 1).astype(f32), (geo + 1).astype(f32)],
    )


def pack_cols_kernel(
    par_ref, soil, geo, land, river, elev, rough, rain, evap, head, press, stor, a_ref, b_ref
):
    odd = par_ref[0] == 1
    plain, classes = columns(
        soil[...], geo[...], land[...], river[...], elev[...], rough[...], rain[...], evap[...], head[...]
    )
    plain = [press[0], press[1], stor[0], stor[1]] + plain
    width = plain[0].shape[1]
    lane = lax.broadcasted_iota(jnp.int32, (plain[0].shape[0], LANES), 1)

    def side(right):
        halves = []
        for half in range(2):
            acc = jnp.zeros((plain[0].shape[0], LANES), f32)
            items = []
            if half == 0:
                items = [(plain[i], 16, 16 * i) for i in range(8)]
            else:
                items = [(plain[8], 16, 0), (classes[0], 32, 32), (classes[1], 32, 64)]
            for value, wide, at in items:
                part = value[:, width - LANES :] if right else value[:, :LANES]
                start = LANES - wide if right else 0
                moved = part if start == at else pltpu.roll(part, (at - start) % LANES, 1)
                acc = jnp.where((lane >= at) & (lane < at + wide), moved, acc)
            halves.append(acc)
        return halves

    left, right = side(False), side(True)
    for half in range(2):
        cols = slice(half * LANES, (half + 1) * LANES)
        a_ref[:, cols] = jnp.where(odd, left[half], right[half])
        b_ref[:, cols] = jnp.where(odd, right[half], left[half])


def slice_kernel(
    par_ref, soil, geo, land, river, elev, rough, rain, evap, head, press, stor, a_ref, b_ref,
    z_ref, c_ref, work_ref,
):
    odd = par_ref[0] == 1
    plain, classes = columns(
        soil[...], geo[...], land[...], river[...], elev[...], rough[...], rain[...], evap[...], head[...]
    )
    plain = [press[0], press[1], stor[0], stor[1]] + plain
    rows, width = plain[0].shape
    lane = lax.broadcasted_iota(jnp.int32, (rows, LANES), 1)
    got_a, got_b = a_ref[...], b_ref[...]
    left = jnp.where(odd, got_a, got_b)
    right = jnp.where(odd, got_b, got_a)

    def slices(value, half, at, wide):
        cols = slice(half * LANES, (half + 1) * LANES)
        lo, hi = left[:, cols], right[:, cols]
        move = (EDGE - wide - at) % LANES
        lo = pltpu.roll(lo, move, 1) if move else lo
        move = (LANES - EDGE - at) % LANES
        hi = pltpu.roll(hi, move, 1) if move else hi
        first, last = value[:, :LANES], value[:, width - LANES :]
        low_r, high_r = pltpu.roll(first, EDGE, 1), pltpu.roll(last, EDGE, 1)
        low_l, high_l = pltpu.roll(first, LANES - EDGE, 1), pltpu.roll(last, LANES - EDGE, 1)
        zero = jnp.zeros_like(lo)
        return [
            jnp.where(lane < EDGE, jnp.where(lane >= EDGE - wide, lo, zero), low_r),
            jnp.where(lane < LANES - EDGE, low_l, high_l),
            jnp.where(lane < EDGE, low_r, high_r),
            jnp.where(lane < LANES - EDGE, high_l, jnp.where(lane < LANES - EDGE + wide, hi, zero)),
        ]

    for i in range(4):
        for d, part in enumerate(slices(plain[i], 0, 16 * i, 16)):
            z_ref[d, i] = part
    spots = [(0, 16 * i, 16) for i in range(4, 8)] + [(1, 0, 16), (1, 32, 32), (1, 64, 32)]
    for j, (value, (half, at, wide)) in enumerate(zip(plain[4:] + classes, spots)):
        for d, part in enumerate(slices(value, half, at, wide)):
            work_ref[d, j] = part
    c_ref[...] = work_ref[par_ref[1]]


def pack_rows_kernel(par_ref, z_ref, c_ref, a_ref, b_ref):
    odd = par_ref[0] == 1
    rows = z_ref.shape[2]
    low = jnp.where(odd, rows - HALO, 0)
    low_class = jnp.where(odd, rows - CROWS, 0)
    for ref, at, at_class in (
        (a_ref, low, low_class),
        (b_ref, (rows - HALO) - low, (rows - CROWS) - low_class),
    ):
        at = pl.multiple_of(at, 8)
        at_class = pl.multiple_of(at_class, 8)
        for s in range(4):
            for i in range(4):
                k = 8 * (i // 2) + 2 * s + i % 2
                ref[pl.ds(k * HALO, HALO), :] = z_ref[s, i, pl.ds(at, HALO), :]
        for j in range(5):
            ref[pl.ds((16 + j) * HALO, HALO), :] = c_ref[j, pl.ds(at, HALO), :]
        for j in range(2):
            ref[pl.ds(21 * HALO + j * CROWS, CROWS), :] = c_ref[5 + j, pl.ds(at_class, CROWS), :]


MSG_ROWS = 21 * HALO + 2 * CROWS


def main_kernel(
    par_ref, z_ref, c_ref, a_ref, b_ref, table_ref, proj_ref, out_ref,
    top_ref, bot_ref, shift_ref, cond_ref, press_ref, press2_ref, stor_ref, coef_ref, rhs_ref, flat_ref, src_ref,
):
    odd = par_ref[0] == 1
    rows = z_ref.shape[2]
    full = rows + 2 * HALO
    full_class = rows + 2 * CROWS
    top_ref[...] = jnp.where(odd, b_ref[...], a_ref[...])
    bot_ref[...] = jnp.where(odd, a_ref[...], b_ref[...])

    for j in range(2):
        at = 21 * HALO + j * CROWS
        value = jnp.concatenate([top_ref[at : at + CROWS, :], c_ref[5 + j], bot_ref[at : at + CROWS, :]], axis=0)
        for dx in (-1, 0, 1):
            shift_ref[(3 * j + dx + 1), :, :] = (pltpu.roll(value, (-dx) % LANES, 1) if dx else value) - 1.0

    for j in range(5):
        at = (16 + j) * HALO
        flat_ref[j, 0:HALO, :] = top_ref[at : at + HALO, :]
        flat_ref[j, HALO : HALO + rows, :] = c_ref[j]
        flat_ref[j, HALO + rows : full, :] = bot_ref[at : at + HALO, :]

    for f, ref in ((0, press_ref), (1, stor_ref)):
        for r in range(0, full, 8):
            parts = []
            for l in range(8):
                k = 8 * f + l
                if r < HALO:
                    part = top_ref[k * HALO + r : k * HALO + r + 8, :]
                elif r < HALO + rows:
                    part = z_ref[l // 2, 2 * f + l % 2, r - HALO : r - HALO + 8, :]
                else:
                    at = k * HALO + r - HALO - rows
                    part = bot_ref[at : at + 8, :]
                parts.append(part)
            ref[r : r + 8] = jnp.swapaxes(jnp.stack(parts), 0, 1)

    sub = lax.broadcasted_iota(jnp.int32, (8, LANES), 0)
    geo_low = sub.astype(f32)
    geo_high = geo_low + 8.0
    soil_mid = jnp.where(sub < 4, sub + 8, sub - 4).astype(f32)
    soil_late = (sub + 4).astype(f32)
    first4 = sub < 4

    def one_hot(row):
        def spread(kind, t):
            dy, dx = t // 3 - 1, t % 3
            return jnp.broadcast_to(shift_ref[3 * kind + dx, pl.ds(row + dy, 1), :], (8, LANES))

        tiles = []
        for t in range(9):
            value = spread(1, t)
            tiles += [value == geo_low, value == geo_high]
        soils = [spread(0, t) for t in range(9)]
        t = 0
        while t < 9:
            tiles.append(soils[t] == geo_low)
            if t + 1 < 9:
                tiles.append(jnp.where(first4, soils[t], soils[t + 1]) == soil_mid)
                tiles.append(soils[t + 1] == soil_late)
            else:
                tiles.append(jnp.where(first4, soils[t], -9.0) == soil_mid)
            t += 2
        pairs = [
            jnp.concatenate([jnp.where(a, 1.0, 0.0), jnp.where(b, 1.0, 0.0)], axis=0).astype(bf16)
            for a, b in zip(tiles[0::2], tiles[1::2])
        ]
        return jnp.concatenate(pairs, axis=0)

    table = table_ref[...]
    proj = proj_ref[...]

    def conduct_pair(i, carry):
        row = 2 * i
        at = row + CROWS - HALO
        hot = jnp.concatenate([one_hot(at), one_hot(at + 1)], axis=1)
        both = jnp.dot(table, hot, preferred_element_type=f32)
        hidden = jnp.maximum(both[:LANES] + both[LANES:], 0.0).astype(bf16)
        logits = jnp.dot(proj, hidden, preferred_element_type=f32)
        value = jnp.exp(logits)
        for k in range(2):
            inside = jnp.broadcast_to(shift_ref[1, pl.ds(at + k, 1), :], (8, LANES)) >= 0.0
            cond_ref[row + k] = jnp.where(inside, value[:, k * LANES : (k + 1) * LANES], 0.0)
        return carry

    lax.fori_loop(0, full // 2, conduct_pair, 0)

    def coefficients(r, carry):
        mid = cond_ref[r]
        north = 0.5 * lateral * (mid + cond_ref[r - 1])
        south = 0.5 * lateral * (mid + cond_ref[r + 1])
        east = 0.5 * lateral * (mid + pltpu.roll(mid, LANES - 1, 1))
        west = 0.5 * lateral * (mid + pltpu.roll(mid, 1, 1))
        up = 0.5 * vertical * (mid + jnp.where(sub > 0, pltpu.roll(mid, 1, 0), 0.0))
        down = 0.5 * vertical * (mid + jnp.where(sub < 7, pltpu.roll(mid, 7, 0), 0.0))
        store = stor_ref[r]
        diagonal = store + up + down + north + south + east + west
        live = store > 0.0
        inverse = jnp.where(live, 1.0, 0.0) / jnp.where(live, diagonal, 1.0)
        coef_ref[0, r] = jnp.where(sub > 0, up * inverse, 0.0)
        coef_ref[1, r] = jnp.where(sub < 7, down * inverse, 0.0)
        coef_ref[2, r] = north * inverse
        coef_ref[3, r] = south * inverse
        coef_ref[4, r] = east * inverse
        coef_ref[5, r] = west * inverse
        coef_ref[6, r] = store * inverse
        coef_ref[7, r] = jnp.where(sub == 0, inverse, 0.0)
        return carry

    lax.fori_loop(1, full - 1, coefficients, 0)

    rough, rain, evap, elev = flat_ref[0], flat_ref[1], flat_ref[2], flat_ref[3]
    head = flat_ref[4]
    land = jnp.where(rough > 0.0, 1.0, 0.0)

    def around(value):
        return (
            pltpu.roll(value, full - 1, 0),
            pltpu.roll(value, 1, 0),
            pltpu.roll(value, LANES - 1, 1),
            pltpu.roll(value, 1, 1),
        )

    faces = [0.5 * (rough + near) for near in around(rough)]
    top_cond = jnp.concatenate([cond_ref[r, 0:1, :] for r in range(full)], axis=0)
    rate = land * (infil_rate * top_cond / (1.0 + top_cond))
    loss = land * evap
    for cycle in range(CYCLES):
        top = jnp.concatenate([press_ref[r, 0:1, :] for r in range(full)], axis=0)
        level = head + elev
        flux = jnp.zeros_like(level)
        for face, near in zip(faces, around(level)):
            flux = flux + face * (near - level)
        infil = rate * (head - top)
        src_ref[...] = infil - loss * jax.nn.sigmoid(top)
        head = head + land * (rain - infil + flux)
        done = cycle * SWEEPS

        def right_side(r, carry):
            source = jnp.broadcast_to(src_ref[pl.ds(r, 1), :], (8, LANES))
            rhs_ref[r] = coef_ref[6, r] * press_ref[r] + coef_ref[7, r] * source
            return carry

        lax.fori_loop(done + 1, full - 1 - done, right_side, 0)
        for sweep in range(SWEEPS):
            old, new = (press_ref, press2_ref) if sweep % 2 == 0 else (press2_ref, press_ref)

            def one_row(r, carry):
                north, mid = carry
                south = old[r + 1]
                total = rhs_ref[r] + coef_ref[0, r] * pltpu.roll(mid, 1, 0)
                total = total + coef_ref[1, r] * pltpu.roll(mid, 7, 0)
                total = total + coef_ref[2, r] * north
                total = total + coef_ref[3, r] * south
                total = total + coef_ref[4, r] * pltpu.roll(mid, LANES - 1, 1)
                total = total + coef_ref[5, r] * pltpu.roll(mid, 1, 1)
                new[r] = total
                return mid, south

            first = done + sweep + 1
            lax.fori_loop(first, full - first, one_row, (old[first - 1], old[first]), unroll=2)

    lane = lax.broadcasted_iota(jnp.int32, (8, LANES), 1)
    for r in range(HALO, HALO + rows, 8):
        layers = jnp.swapaxes(press_ref[r : r + 8], 0, 1)
        for s in range(4):
            out_ref[s, 0, r - HALO : r - HALO + 8, :] = jnp.where(
                lane < CHUNK,
                pltpu.roll(layers[2 * s], LANES - EDGE, 1),
                pltpu.roll(layers[2 * s + 1], EDGE, 1),
            )
            out_ref[s, 1, r - HALO : r - HALO + 8, :] = pltpu.roll(head[r : r + 8], LANES - EDGE, 1)


def finish_kernel(z_ref, press_ref, head_ref):
    rows = z_ref.shape[2]
    lane = lax.broadcasted_iota(jnp.int32, (rows, LANES), 1)
    for d in range(0, 4, 2):
        cols = slice(d * CHUNK, d * CHUNK + LANES)
        a, b = z_ref[d, 0], z_ref[d + 1, 0]
        press_ref[0, :, cols] = jnp.where(lane < CHUNK, a, pltpu.roll(b, CHUNK, 1))
        press_ref[1, :, cols] = jnp.where(lane < CHUNK, pltpu.roll(a, CHUNK, 1), b)
        head_ref[:, cols] = jnp.where(lane < CHUNK, z_ref[d, 1], pltpu.roll(z_ref[d + 1, 1], CHUNK, 1))


def shards(
    soil_class, geology_class, land_mask, river_mask, elevation, roughness, rainfall, potential_evap,
    surface_head, pressure, storage, soil_embed, geology_embed, conv_weight, out_weight,
):
    rows, width = soil_class.shape
    sec = lax.axis_index("sec")
    gx = lax.axis_index("gx")
    gy = lax.axis_index("gy")
    n_gx, n_gy = lax.axis_size("gx"), lax.axis_size("gy")
    full = rows + 2 * HALO
    sds = jax.ShapeDtypeStruct
    raw = (
        soil_class, geology_class, land_mask, river_mask, elevation, roughness, rainfall,
        potential_evap, surface_head, pressure, storage,
    )
    par_y = jnp.stack([gy % 2, sec]).astype(jnp.int32)
    par_x = jnp.stack([gx % 2, sec]).astype(jnp.int32)

    sel, tap = table_layout()
    table, proj = call(
        table_kernel, (sds((2 * LANES, KROWS), bf16), sds((out_weight.shape[1], LANES), bf16)), 6, name="table"
    )(
        jnp.asarray(sel), jnp.asarray(tap), soil_embed, geology_embed,
        conv_weight.reshape(9, LANES, LANES), out_weight,
    )

    edge = sds((rows, 2 * LANES), f32)
    ya, yb = call(pack_cols_kernel, (edge, edge), 12, smem=(0,), name="pack_cols")(par_y, *raw)
    ya = lax.ppermute(ya, "gy", swap_pairs(n_gy, 0))
    yb = lax.ppermute(yb, "gy", swap_pairs(n_gy, 1))
    z, cols = call(
        slice_kernel, (sds((4, 4, rows, LANES), f32), sds((7, rows, LANES), f32)), 14,
        scratch=[pltpu.VMEM((4, 7, rows, LANES), f32)], smem=(0,), name="slices",
    )(par_y, *raw, ya, yb)
    z = lax.all_to_all(z, "sec", 0, 0)
    msg = sds((MSG_ROWS, LANES), f32)
    xa, xb = call(pack_rows_kernel, (msg, msg), 3, smem=(0,), name="pack_rows")(par_x, z, cols)
    xa = lax.ppermute(xa, "gx", swap_pairs(n_gx, 1))
    xb = lax.ppermute(xb, "gx", swap_pairs(n_gx, 0))
    grid = (full, 8, LANES)
    out = call(
        main_kernel, sds((4, 2, rows, LANES), f32), 7,
        scratch=[
            pltpu.VMEM((MSG_ROWS, LANES), f32),
            pltpu.VMEM((MSG_ROWS, LANES), f32),
            pltpu.VMEM((6, rows + 2 * CROWS, LANES), f32),
            pltpu.VMEM(grid, f32),
            pltpu.VMEM(grid, f32),
            pltpu.VMEM(grid, f32),
            pltpu.VMEM(grid, f32),
            pltpu.VMEM((8,) + grid, f32),
            pltpu.VMEM(grid, f32),
            pltpu.VMEM((5, full, LANES), f32),
            pltpu.VMEM((full, LANES), f32),
        ],
        smem=(0,), name="cycles",
    )(par_x, z, cols, xa, xb, table, proj)
    out = lax.all_to_all(out, "sec", 0, 0)
    return tuple(
        call(finish_kernel, (sds(pressure.shape, f32), sds((rows, width), f32)), 1, name="finish")(out)
    )


def solution(mesh):
    flat = P("gx", "gy")
    deep = P("sec", "gx", "gy")
    in_specs = (flat,) * 9 + (deep, deep) + (P(),) * 4
    return jax.shard_map(shards, mesh=mesh, in_specs=in_specs, out_specs=(deep, flat), check_vma=False)
```

time: 824 us -> 111 us (0.13)
  starting transfers between devices: 399 us -> 21.8 us
  waiting for transfers between devices: 204 us -> 16 us
  blocking collectives: 161 us -> 10.4 us
  Pallas kernels: 0 us -> 57.3 us
  between operations: 16.3 us -> 0.71 us
  local copies, waits for them, and re-layouts: 13.5 us -> 2.72 us
  other arithmetic: 11.3 us -> 1.24 us
  matrix products: 9.98 us -> 0 us
    ppermute x126 -> x4, starting transfers between devices: 399 us -> 14.5 us  [the longest x1 8.25 us: shards(): xa = lax.ppermute(xa, 'gx', swap_pairs(n_gx, 1))]
    ppermute x126 -> x4, waiting for transfers between devices: 165 us -> 7.76 us  [the longest x1 2.95 us: shards(): yb = lax.ppermute(yb, 'gy', swap_pairs(n_gy, 1))]
    all_gather x8 -> x0, blocking collectives: 105 us -> none  [the longest x4 52.6 us: shards(): lax.all_gather(source_strip, 'sec', axis=0, tiled=True)]
    pallas_call x0 -> x6, Pallas kernels: none -> 57.3 us  [the longest x1 47.6 us: shards(): call(main_kernel, sds((4, 2, rows, LANES), f32), 7, scratch=[pltpu.VMEM((...]
    psum x3 -> x0, blocking collectives: 55.9 us -> none  [spread(): return lax.psum(jnp.where(mine, value, jnp.zeros_like(value)), axis)]
    psum x1 -> x0, waiting for transfers between devices: 39.1 us -> none  [spread(): return lax.psum(jnp.where(mine, value, jnp.zeros_like(value)), axis)]
    all_to_all x0 -> x1, blocking collectives: none -> 10.4 us  [shards(): out = lax.all_to_all(out, 'sec', 0, 0)]
  transfers between devices with their start and end apart: 127 -> 5, of which waited for: 44 -> 4; matrix products, arithmetic and copies ran while one was open for 4% -> 1% of each run, Pallas kernels for 0% -> 2%
where the time goes in v1:
time: 111 us; the launch traced here: 110 us
  Pallas kernels  57.3 us (52%)
  starting transfers between devices  21.8 us (20%)
  waiting for transfers between devices  16 us (14%)
  blocking collectives  10.4 us (9%)
  local copies, waits for them, and re-layouts  2.72 us (2%)
  other arithmetic  1.24 us (1%)
    pallas_call x1, Pallas kernels, shards(): call(main_kernel, sds((4, 2, rows, LANES), f32), 7, scratch=[pltpu.VMEM((...  47.6 us
    all_to_all x1, blocking collectives, shards(): out = lax.all_to_all(out, 'sec', 0, 0)  10.4 us
    ppermute x1, starting transfers between devices, shards(): xa = lax.ppermute(xa, 'gx', swap_pairs(n_gx, 1))  8.25 us
    all_to_all x1, waiting for transfers between devices, shards(): z = lax.all_to_all(z, 'sec', 0, 0)  8.22 us
    all_to_all x1, starting transfers between devices, shards(): z = lax.all_to_all(z, 'sec', 0, 0)  7.26 us
    ppermute x1, waiting for transfers between devices, shards(): yb = lax.ppermute(yb, 'gy', swap_pairs(n_gy, 1))  2.95 us
    unnamed x13, local copies, waits for them, and re-layouts  2.72 us
    ppermute x1, waiting for transfers between devices, shards(): xa = lax.ppermute(xa, 'gx', swap_pairs(n_gx, 1))  2.56 us
  transfers between devices with their start and end apart: 5, of which 4 were waited for; matrix products, arithmetic and copies ran while one was open for 1% of the time, Pallas kernels for 2%

profile of v1, /device:TPU:30, one launch (start us, length us, event | category | flops | bytes accessed | tf_op | source)
XLA Modules:
  0.0 110.1 jit_solution(15149350884972747579)
XLA Ops:
  0.6 0.6 pad_add_fusion.1.par_ref
  1.2 1.8 %pack_cols.1 = (f32[32,256]{1,0:T(8,128)}, f32[32,256]{1,0:T(8,128)}) custom-call(s32[2]{0:T(128)} %pad_add_fusion.1.par_ref, s32[32,256]{1,0:T(8,128)} %soil.3, s32[32,256]{1,0:T(8,128)} %geo.3, s32[32,256]{1,0:T(8,128)} %land.3, s32[32,256]{1,0:T(8,128)} %river.3, f32[32,256]{1,0:T(8,128)} %elev.3, f32[32,256]{1,0:T(8,128)} %rough.3, f32[32,256]{1,0:T(8,128)} %rain.3, ...), custom_call_target="tpu_custom_call" | custom-call | tf_op jit(solution)/shard_map/pack_cols/pallas_call | solution.py:410
  3.0 1.9 %collective-permute-start = (f32[32,256]{1,0:T(8,128)}, f32[32,256]{1,0:T(8,128)S(1)}, u32[]{:S(2)}, u32[]{:S(2)}) collective-permute-start(f32[32,256]{1,0:T(8,128)} %get-tuple-element.10), channel_id=1, source_target_pairs={{0,1},{1,0},{2,3},{3,2},{4,5},{5,4},{6,7},{7,6},{8,9},{9,8},{10,11... | collective-permute-start | bytes 98312 | tf_op jit(solution)/shard_map/ppermute | solution.py:411
  4.9 2.5 %collective-permute-start.1 = (f32[32,256]{1,0:T(8,128)}, f32[32,256]{1,0:T(8,128)S(1)}, u32[]{:S(2)}, u32[]{:S(2)}) collective-permute-start(f32[32,256]{1,0:T(8,128)} %get-tuple-element.11), channel_id=1, source_target_pairs={{1,2},{2,1},{3,4},{4,3},{5,6},{6,5},{7,8},{8,7},{9,10},{10,9},{11,... | collective-permute-start | bytes 98312 | tf_op jit(solution)/shard_map/ppermute | solution.py:412
  7.4 0.0 collective-permute-done.a_ref
  7.4 0.0 copy-start.3
  7.4 3.0 %collective-permute-done.1.b_ref = f32[32,256]{1,0:T(8,128)S(1)} collective-permute-done((f32[32,256]{1,0:T(8,128)}, f32[32,256]{1,0:T(8,128)S(1)}, u32[]{:S(2)}, u32[]{:S(2)}) %collective-permute-start.1) | collective-permute-done | bytes 32800 | tf_op jit(solution)/shard_map/ppermute | solution.py:412
  10.4 0.0 copy-done.3
  10.4 0.0 copy-start.4
  10.4 0.6 copy-done.4
  11.0 2.1 %slices.1 = (f32[4,4,32,128]{3,2,1,0:T(8,128)}, f32[7,32,128]{2,1,0:T(8,128)}) custom-call(s32[2]{0:T(128)} %pad_add_fusion.1.par_ref, s32[32,256]{1,0:T(8,128)} %soil.3, s32[32,256]{1,0:T(8,128)} %geo.3, s32[32,256]{1,0:T(8,128)} %land.3, s32[32,256]{1,0:T(8,128)} %river.3, f32[32,256]{1,0:T(8,128)} %elev.3, f32[32,256]{1,0:T(8,128)} %rough.3, ...), custom_call_target="tpu_custom_call" | custom-call | tf_op jit(solution)/shard_map/slices/pallas_call | solution.py:413
  13.1 7.3 %all-to-all-start = ((f32[4,4,32,128]{3,2,1,0:T(8,128)}), f32[4,4,32,128]{3,2,1,0:T(8,128)S(1)}, u32[]{:S(2)}, u32[]{:S(2)}) async-start(f32[4,4,32,128]{3,2,1,0:T(8,128)} %get-tuple-element.12), calls=%async_computation | async-start | bytes 524288 | tf_op jit(solution)/shard_map/all_to_all | solution.py:417
  20.3 0.7 pad_add_fusion.par_ref
  21.0 8.2 %all-to-all-done.z_ref = f32[4,4,32,128]{3,2,1,0:T(8,128)S(1)} async-done(((f32[4,4,32,128]{3,2,1,0:T(8,128)}), f32[4,4,32,128]{3,2,1,0:T(8,128)S(1)}, u32[]{:S(2)}, u32[]{:S(2)}) %all-to-all-start) | async-done | bytes 262176 | tf_op jit(solution)/shard_map/all_to_all | solution.py:417
  29.2 0.0 copy-start
  29.2 0.7 copy-done
  29.9 1.8 %pack_rows.1 = (f32[384,128]{1,0:T(8,128)}, f32[384,128]{1,0:T(8,128)}) custom-call(s32[2]{0:T(128)} %pad_add_fusion.par_ref, f32[4,4,32,128]{3,2,1,0:T(8,128)} %copy-done, f32[7,32,128]{2,1,0:T(8,128)} %get-tuple-element.13.c_ref), custom_call_target="tpu_custom_call" | custom-call | tf_op jit(solution)/shard_map/pack_rows/pallas_call | solution.py:419
  31.7 0.0 copy-start.5
  31.7 8.3 %collective-permute-start.2 = (f32[384,128]{1,0:T(8,128)}, f32[384,128]{1,0:T(8,128)S(1)}, u32[]{:S(2)}, u32[]{:S(2)}) collective-permute-start(f32[384,128]{1,0:T(8,128)} %get-tuple-element.14), channel_id=1, source_target_pairs={{16,32},{32,16},{48,64},{64,48},{80,96},{96,80},{17,33},{33,17},{4... | collective-permute-start | bytes 589832 | tf_op jit(solution)/shard_map/ppermute | solution.py:420
  40.0 1.9 %collective-permute-start.3 = (f32[384,128]{1,0:T(8,128)}, f32[384,128]{1,0:T(8,128)S(1)}, u32[]{:S(2)}, u32[]{:S(2)}) collective-permute-start(f32[384,128]{1,0:T(8,128)} %get-tuple-element.15), channel_id=1, source_target_pairs={{0,16},{16,0},{32,48},{48,32},{64,80},{80,64},{96,112},{112,96},{1... | collective-permute-start | bytes 589832 | tf_op jit(solution)/shard_map/ppermute | solution.py:421
  41.9 0.0 copy-done.5
  41.9 0.7 copy.19.out_ref
  42.6 2.4 %table.1 = (bf16[256,256]{1,0:T(8,128)(2,1)}, bf16[8,128]{1,0:T(8,128)(2,1)}) custom-call(f32[256,28]{1,0:T(8,128)} %constant.35.clone.sel_ref, s32[256,128]{1,0:T(8,128)} %constant.36.clone.tap_ref, bf16[12,128]{1,0:T(8,128)(2,1)} %soil_ref.1, bf16[16,128]{1,0:T(8,128)(2,1)} %geo_ref.1, bf16[9,128,128]{2,1,0:T(8,128)(2,1)} %bitcast.4, ...), custom_call_target="tpu_custom_call" | custom-call | tf_op jit(solution)/shard_map/table/pallas_call | solution.py:402
  45.0 2.6 %collective-permute-done.2.a_ref = f32[384,128]{1,0:T(8,128)S(1)} collective-permute-done((f32[384,128]{1,0:T(8,128)}, f32[384,128]{1,0:T(8,128)S(1)}, u32[]{:S(2)}, u32[]{:S(2)}) %collective-permute-start.2) | collective-permute-done | bytes 196640 | tf_op jit(solution)/shard_map/ppermute | solution.py:420
  47.6 0.0 copy-start.1
  47.6 2.2 %collective-permute-done.3.b_ref = f32[384,128]{1,0:T(8,128)S(1)} collective-permute-done((f32[384,128]{1,0:T(8,128)}, f32[384,128]{1,0:T(8,128)S(1)}, u32[]{:S(2)}, u32[]{:S(2)}) %collective-permute-start.3) | collective-permute-done | bytes 196640 | tf_op jit(solution)/shard_map/ppermute | solution.py:421
  49.8 0.0 copy-start.2
  49.8 0.0 copy-done.1
  49.8 0.7 copy-done.2
  50.5 47.6 %cycles.1 = f32[4,2,32,128]{3,2,1,0:T(8,128)} custom-call(s32[2]{0:T(128)} %pad_add_fusion.par_ref, f32[4,4,32,128]{3,2,1,0:T(8,128)} %copy-done, f32[7,32,128]{2,1,0:T(8,128)} %get-tuple-element.13.c_ref, f32[384,128]{1,0:T(8,128)} %copy-done.1, f32[384,128]{1,0:T(8,128)} %copy-done.2, bf16[256,256]{1,0:T(8,128)(2,1)} %get-tuple-element.16.table_ref, ...), custom_call_target="tpu_custom_call" | custom-call | tf_op jit(solution)/shard_map/cycles/pallas_call | solution.py:423
  98.1 10.4 %all_to_all.10.z_ref = f32[4,2,32,128]{3,2,1,0:T(8,128)} all-to-all(f32[4,2,32,128]{3,2,1,0:T(8,128)} %cycles.1), channel_id=1, replica_groups=mesh['sec'=4,'gx'=8,'gy'=16] {'sec'}, dimensions={0} | all-to-all | bytes 262144 | tf_op jit(solution)/shard_map/all_to_all | solution.py:440
  108.5 1.6 %finish.1 = (f32[2,32,256]{2,1,0:T(8,128)}, f32[32,256]{1,0:T(8,128)}) custom-call(f32[4,2,32,128]{3,2,1,0:T(8,128)} %all_to_all.10.z_ref), custom_call_target="tpu_custom_call" | custom-call | tf_op jit(solution)/shard_map/finish/pallas_call | solution.py:442
Async XLA Ops:
  3.0 4.4 %collective-permute-start = (f32[32,256]{1,0:T(8,128)}, f32[32,256]{1,0:T(8,128)S(1)}, u32[]{:S(2)}, u32[]{:S(2)}) collective-permute-start(f32[32,256]{1,0:T(8,128)} %get-tuple-element.10), channel_id=1, source_target_pairs={{0,1},{1,0},{2,3},{3,2},{4,5},{5,4},{6,7},{7,6},{8,9},{9,8},{10,11... | collective-permute-start | bytes 98312 | tf_op jit(solution)/shard_map/ppermute | solution.py:411
  4.9 5.4 %collective-permute-start.1 = (f32[32,256]{1,0:T(8,128)}, f32[32,256]{1,0:T(8,128)S(1)}, u32[]{:S(2)}, u32[]{:S(2)}) collective-permute-start(f32[32,256]{1,0:T(8,128)} %get-tuple-element.11), channel_id=1, source_target_pairs={{1,2},{2,1},{3,4},{4,3},{5,6},{6,5},{7,8},{8,7},{9,10},{10,9},{11,... | collective-permute-start | bytes 98312 | tf_op jit(solution)/shard_map/ppermute | solution.py:412
  7.4 3.0 %copy-start.3 = (f32[32,256]{1,0:T(8,128)}, f32[32,256]{1,0:T(8,128)S(1)}, u32[]{:S(2)}) copy-start(f32[32,256]{1,0:T(8,128)S(1)} %collective-permute-done.a_ref) | copy-start | bytes 98308
  10.4 0.6 copy-start.4
  13.1 16.1 %all-to-all-start = ((f32[4,4,32,128]{3,2,1,0:T(8,128)}), f32[4,4,32,128]{3,2,1,0:T(8,128)S(1)}, u32[]{:S(2)}, u32[]{:S(2)}) async-start(f32[4,4,32,128]{3,2,1,0:T(8,128)} %get-tuple-element.12), calls=%async_computation | async-start | bytes 524288 | tf_op jit(solution)/shard_map/all_to_all | solution.py:417
  29.2 0.7 copy-start
  31.7 10.2 %copy-start.5 = (bf16[128,8]{0,1:T(8,128)(2,1)S(1)}, bf16[128,8]{0,1:T(8,128)(2,1)}, u32[]{:S(2)}) copy-start(bf16[128,8]{0,1:T(8,128)(2,1)} %param.31) | copy-start | bytes 6148
  31.7 15.9 %collective-permute-start.2 = (f32[384,128]{1,0:T(8,128)}, f32[384,128]{1,0:T(8,128)S(1)}, u32[]{:S(2)}, u32[]{:S(2)}) collective-permute-start(f32[384,128]{1,0:T(8,128)} %get-tuple-element.14), channel_id=1, source_target_pairs={{16,32},{32,16},{48,64},{64,48},{80,96},{96,80},{17,33},{33,17},{4... | collective-permute-start | bytes 589832 | tf_op jit(solution)/shard_map/ppermute | solution.py:420
  40.0 9.8 %collective-permute-start.3 = (f32[384,128]{1,0:T(8,128)}, f32[384,128]{1,0:T(8,128)S(1)}, u32[]{:S(2)}, u32[]{:S(2)}) collective-permute-start(f32[384,128]{1,0:T(8,128)} %get-tuple-element.15), channel_id=1, source_target_pairs={{0,16},{16,0},{32,48},{48,32},{64,80},{80,64},{96,112},{112,96},{1... | collective-permute-start | bytes 589832 | tf_op jit(solution)/shard_map/ppermute | solution.py:421
  47.6 2.3 %copy-start.1 = (f32[384,128]{1,0:T(8,128)}, f32[384,128]{1,0:T(8,128)S(1)}, u32[]{:S(2)}) copy-start(f32[384,128]{1,0:T(8,128)S(1)} %collective-permute-done.2.a_ref) | copy-start | bytes 589828
  49.8 0.7 copy-start.2

commit v2 on v1

v2 whole, which is shorter than its diff:
```python
import functools

import jax
import jax.numpy as jnp
import numpy as np
from jax import lax
from jax.experimental import pallas as pl
from jax.experimental.pallas import tpu as pltpu
from jax.sharding import PartitionSpec as P

SWEEPS = 4
CYCLES = 4
HALO = SWEEPS * CYCLES
LANES = 128
CHUNK = 64
EDGE = (LANES - CHUNK) // 2
CROWS = 24
NSOIL = 12
NGEO = 16
KSOIL = 9 * NGEO
KROWS = 256

infil_rate = 0.3
lateral = 1.0
vertical = 0.5

VMEM = pl.BlockSpec(memory_space=pltpu.VMEM)
f32 = jnp.float32
bf16 = jnp.bfloat16


def call(kernel, outs, args, scratch=(), name=None, hbm=(), final=False):
    made = outs if final else tuple(pltpu.VMEM(o.shape, o.dtype) for o in outs)
    args = [x if i in hbm else pltpu.with_memory_space_constraint(x, pltpu.VMEM) for i, x in enumerate(args)]
    return pl.pallas_call(
        kernel,
        out_shape=made,
        in_specs=[VMEM] * len(args),
        out_specs=tuple(VMEM for _ in outs),
        scratch_shapes=scratch,
        name=name,
    )(*args)


def swap_pairs(count, first):
    out = []
    for i in range(first, count - 1, 2):
        out += [(i, i + 1), (i + 1, i)]
    return out


def table_layout():
    sel = np.zeros((KROWS, NSOIL + NGEO), np.float32)
    tap = np.full((KROWS, LANES), -1, np.int32)
    for k in range(KSOIL):
        sel[k, NSOIL + k % NGEO] = 1
        tap[k] = k // NGEO
    for j in range(9 * NSOIL):
        sel[KSOIL + j, j % NSOIL] = 1
        tap[KSOIL + j] = j // NSOIL
    return sel, tap


def table_kernel(sel_ref, tap_ref, soil_ref, geo_ref, weight_ref, table_ref):
    sel = sel_ref[...].astype(bf16)
    embed = jnp.dot(sel[:, :NSOIL], soil_ref[...], preferred_element_type=f32)
    embed = embed + jnp.dot(sel[:, NSOIL:], geo_ref[...], preferred_element_type=f32)
    tap = tap_ref[...]
    total = jnp.zeros((LANES, KROWS), f32)
    for t in range(9):
        mine = jnp.where(tap == t, embed, 0.0).astype(bf16)
        total = total + lax.dot_general(
            weight_ref[t], mine, (((0,), (1,)), ((), ())), preferred_element_type=f32
        )
    high = total.astype(bf16)
    table_ref[0:LANES, :] = high
    table_ref[LANES : 2 * LANES, :] = (total - high.astype(f32)).astype(bf16)


def columns(soil, geo, land, river, elev, rough, rain, evap, head):
    landf = land.astype(f32)
    conveyance = landf * (1.0 + river.astype(f32)) * rough
    return (
        [conveyance, rain, evap, elev, head],
        [(soil + 1).astype(f32), (geo + 1).astype(f32)],
    )


def pack_cols_kernel(
    soil, geo, land, river, elev, rough, rain, evap, head, press, stor, a_ref, b_ref
):
    odd = lax.axis_index("gy") % 2 == 1
    plain, classes = columns(
        soil[...], geo[...], land[...], river[...], elev[...], rough[...], rain[...], evap[...], head[...]
    )
    plain = [press[0], press[1], stor[0], stor[1]] + plain
    width = plain[0].shape[1]
    lane = lax.broadcasted_iota(jnp.int32, (plain[0].shape[0], LANES), 1)

    def side(right):
        halves = []
        for half in range(2):
            acc = jnp.zeros((plain[0].shape[0], LANES), f32)
            items = []
            if half == 0:
                items = [(plain[i], 16, 16 * i) for i in range(8)]
            else:
                items = [(plain[8], 16, 0), (classes[0], 32, 32), (classes[1], 32, 64)]
            for value, wide, at in items:
                part = value[:, width - LANES :] if right else value[:, :LANES]
                start = LANES - wide if right else 0
                moved = part if start == at else pltpu.roll(part, (at - start) % LANES, 1)
                acc = jnp.where((lane >= at) & (lane < at + wide), moved, acc)
            halves.append(acc)
        return halves

    left, right = side(False), side(True)
    for half in range(2):
        cols = slice(half * LANES, (half + 1) * LANES)
        a_ref[:, cols] = jnp.where(odd, left[half], right[half])
        b_ref[:, cols] = jnp.where(odd, right[half], left[half])


def slice_kernel(
    soil, geo, land, river, elev, rough, rain, evap, head, press, stor, a_ref, b_ref,
    z_ref, c_ref, work_ref,
):
    odd = lax.axis_index("gy") % 2 == 1
    plain, classes = columns(
        soil[...], geo[...], land[...], river[...], elev[...], rough[...], rain[...], evap[...], head[...]
    )
    plain = [press[0], press[1], stor[0], stor[1]] + plain
    rows, width = plain[0].shape
    lane = lax.broadcasted_iota(jnp.int32, (rows, LANES), 1)
    got_a, got_b = a_ref[...], b_ref[...]
    left = jnp.where(odd, got_a, got_b)
    right = jnp.where(odd, got_b, got_a)

    def slices(value, half, at, wide):
        cols = slice(half * LANES, (half + 1) * LANES)
        lo, hi = left[:, cols], right[:, cols]
        move = (EDGE - wide - at) % LANES
        lo = pltpu.roll(lo, move, 1) if move else lo
        move = (LANES - EDGE - at) % LANES
        hi = pltpu.roll(hi, move, 1) if move else hi
        first, last = value[:, :LANES], value[:, width - LANES :]
        low_r, high_r = pltpu.roll(first, EDGE, 1), pltpu.roll(last, EDGE, 1)
        low_l, high_l = pltpu.roll(first, LANES - EDGE, 1), pltpu.roll(last, LANES - EDGE, 1)
        zero = jnp.zeros_like(lo)
        return [
            jnp.where(lane < EDGE, jnp.where(lane >= EDGE - wide, lo, zero), low_r),
            jnp.where(lane < LANES - EDGE, low_l, high_l),
            jnp.where(lane < EDGE, low_r, high_r),
            jnp.where(lane < LANES - EDGE, high_l, jnp.where(lane < LANES - EDGE + wide, hi, zero)),
        ]

    for i in range(4):
        for d, part in enumerate(slices(plain[i], 0, 16 * i, 16)):
            z_ref[d, i] = part
    spots = [(0, 16 * i, 16) for i in range(4, 8)] + [(1, 0, 16), (1, 32, 32), (1, 64, 32)]
    for j, (value, (half, at, wide)) in enumerate(zip(plain[4:] + classes, spots)):
        for d, part in enumerate(slices(value, half, at, wide)):
            work_ref[d, j] = part
    c_ref[...] = work_ref[lax.axis_index("sec")]


def pack_rows_kernel(z_ref, c_ref, a_ref, b_ref):
    odd = lax.axis_index("gx") % 2 == 1
    rows = z_ref.shape[2]
    low = jnp.where(odd, rows - HALO, 0)
    low_class = jnp.where(odd, rows - CROWS, 0)
    for ref, at, at_class in (
        (a_ref, low, low_class),
        (b_ref, (rows - HALO) - low, (rows - CROWS) - low_class),
    ):
        at = pl.multiple_of(at, 8)
        at_class = pl.multiple_of(at_class, 8)
        for s in range(4):
            for i in range(4):
                k = 8 * (i // 2) + 2 * s + i % 2
                ref[pl.ds(k * HALO, HALO), :] = z_ref[s, i, pl.ds(at, HALO), :]
        for j in range(5):
            ref[pl.ds((16 + j) * HALO, HALO), :] = c_ref[j, pl.ds(at, HALO), :]
        for j in range(2):
            ref[pl.ds(21 * HALO + j * CROWS, CROWS), :] = c_ref[5 + j, pl.ds(at_class, CROWS), :]


MSG_ROWS = 21 * HALO + 2 * CROWS


STEP_S = 8
TRIPS_S = 1
BLOCK_K = 16
UNROLL_C = 3
UNROLL_OWN = 7
OWN = 2


def at_row(r):
    return pl.ds(pl.multiple_of(8 * r + 8, 8), 8)


def place(ref, r):
    return ref.at[at_row(r), :]


def beside(ref, mid, r, step):
    return pltpu.roll(mid, (-step) % 8, 0)


def row_blocks(low, high, size, body):
    assert (high - low) % size == 0

    def step(b, carry):
        for i in range(size):
            body(low + b * size + i)
        return carry

    lax.fori_loop(0, (high - low) // size, step, 0)


def shift_classes(ref, kind, value):
    for dx in (-1, 0, 1):
        ref[3 * kind + dx + 1, :, :] = (pltpu.roll(value, (-dx) % LANES, 1) if dx else value) - 1.0


def one_hot(shift_ref, row):
    sub = lax.broadcasted_iota(jnp.int32, (8, LANES), 0)
    low = sub.astype(f32)
    high = low + 8.0
    mid = jnp.where(sub < 4, sub + 8, sub - 4).astype(f32)
    late = low + 4.0
    first4 = sub < 4

    def spread(kind, t):
        dy, dx = t // 3 - 1, t % 3
        return jnp.broadcast_to(shift_ref[3 * kind + dx, pl.ds(row + dy, 1), :], (8, LANES))

    tiles = []
    for t in range(9):
        value = spread(1, t)
        tiles += [value == low, value == high]
    soils = [spread(0, t) for t in range(9)]
    for t in range(0, 9, 2):
        after = soils[t + 1] if t < 8 else jnp.full((8, LANES), -9.0, f32)
        tiles += [soils[t] == low, jnp.where(first4, soils[t], after) == mid]
        if t < 8:
            tiles.append(after == late)
    pairs = [
        jnp.concatenate([jnp.where(a, 1.0, 0.0), jnp.where(b, 1.0, 0.0)], axis=0).astype(bf16)
        for a, b in zip(tiles[0::2], tiles[1::2])
    ]
    return jnp.concatenate(pairs, axis=0)


def conduct_rows(shift_ref, at, table, proj):
    hot = jnp.concatenate([one_hot(shift_ref, at), one_hot(shift_ref, at + 1)], axis=1)
    both = jnp.dot(table, hot, preferred_element_type=f32)
    hidden = jnp.maximum(both[:LANES] + both[LANES:], 0.0).astype(bf16)
    value = jnp.exp(jnp.dot(proj, hidden, preferred_element_type=f32))
    out = []
    for k in range(2):
        inside = jnp.broadcast_to(shift_ref[1, pl.ds(at + k, 1), :], (8, LANES)) >= 0.0
        out.append(jnp.where(inside, value[:, k * LANES : (k + 1) * LANES], 0.0))
    return out


def own_kernel(c_ref, table_ref, proj_ref, cond_ref, shift_ref):
    rows = c_ref.shape[1]
    for kind in range(2):
        shift_classes(shift_ref, kind, c_ref[5 + kind])
    table, proj = table_ref[...], proj_ref[...]

    def step(i, carry):
        for k, value in enumerate(conduct_rows(shift_ref, 2 * i + OWN, table, proj)):
            cond_ref[pl.ds(pl.multiple_of(8 * (2 * i + k), 8), 8), :] = value
        return carry

    lax.fori_loop(0, rows // 2 - OWN, step, 0, unroll=UNROLL_OWN)


def main_kernel(
    z_ref, c_ref, own_ref, a_ref, b_ref, table_ref, proj_ref, out_ref,
    top_ref, bot_ref, shift_ref, cond_ref, press_ref, press2_ref, stor_ref, coef_ref, rhs_ref, flat_ref, src_ref,
):
    odd = lax.axis_index("gx") % 2 == 1
    rows = z_ref.shape[2]
    full = rows + 2 * HALO
    top_ref[...] = jnp.where(odd, b_ref[...], a_ref[...])
    bot_ref[...] = jnp.where(odd, a_ref[...], b_ref[...])

    for j in range(2):
        at = 21 * HALO + j * CROWS
        value = jnp.concatenate([top_ref[at : at + CROWS, :], c_ref[5 + j], bot_ref[at : at + CROWS, :]], axis=0)
        shift_classes(shift_ref, j, value)

    for j in range(5):
        at = (16 + j) * HALO
        flat_ref[j, 0:HALO, :] = top_ref[at : at + HALO, :]
        flat_ref[j, HALO : HALO + rows, :] = c_ref[j]
        flat_ref[j, HALO + rows : full, :] = bot_ref[at : at + HALO, :]

    for ref in (press_ref, press2_ref):
        ref[0:8, :] = jnp.zeros((8, LANES), f32)
        ref[8 * (full + 1) :, :] = jnp.zeros((8, LANES), f32)
    for f, ref in ((0, press_ref), (1, stor_ref)):
        for r in range(0, full, 8):
            parts = []
            for l in range(8):
                k = 8 * f + l
                if r < HALO:
                    part = top_ref[k * HALO + r : k * HALO + r + 8, :]
                elif r < HALO + rows:
                    part = z_ref[l // 2, 2 * f + l % 2, r - HALO : r - HALO + 8, :]
                else:
                    at = k * HALO + r - HALO - rows
                    part = bot_ref[at : at + 8, :]
                parts.append(part)
            mixed = jnp.swapaxes(jnp.stack(parts), 0, 1).reshape(64, LANES)
            ref[8 * (r + 1) : 8 * (r + 9), :] = mixed

    table, proj = table_ref[...], proj_ref[...]
    cond_ref[8 * (HALO + OWN + 1) : 8 * (HALO + rows - OWN + 1), :] = own_ref[...]
    half = (HALO + OWN) // 2

    def step(i, carry):
        for row in (2 * i, full - 2 * half + 2 * i):
            for k, value in enumerate(conduct_rows(shift_ref, row + CROWS - HALO, table, proj)):
                cond_ref[at_row(row + k), :] = value
        return carry

    lax.fori_loop(0, half, step, 0, unroll=UNROLL_C)
    sub = lax.broadcasted_iota(jnp.int32, (8, LANES), 0)

    def row_coefficients(r):
        mid = cond_ref[at_row(r), :]
        north = 0.5 * lateral * (mid + cond_ref[at_row(r - 1), :])
        south = 0.5 * lateral * (mid + cond_ref[at_row(r + 1), :])
        east = 0.5 * lateral * (mid + pltpu.roll(mid, LANES - 1, 1))
        west = pltpu.roll(east, 1, 1)
        up = 0.5 * vertical * (mid + jnp.where(sub > 0, pltpu.roll(mid, 1, 0), 0.0))
        down = 0.5 * vertical * (mid + jnp.where(sub < 7, pltpu.roll(mid, 7, 0), 0.0))
        store = stor_ref[at_row(r), :]
        diagonal = store + up + down + north + south + east + west
        live = store > 0.0
        inverse = jnp.where(live, 1.0, 0.0) / jnp.where(live, diagonal, 1.0)
        here = at_row(r - 1)
        coef_ref[0, here, :] = jnp.where(sub > 0, up * inverse, 0.0)
        coef_ref[1, here, :] = jnp.where(sub < 7, down * inverse, 0.0)
        coef_ref[2, here, :] = north * inverse
        coef_ref[3, here, :] = south * inverse
        coef_ref[4, here, :] = east * inverse
        coef_ref[5, here, :] = west * inverse
        coef_ref[6, here, :] = store * inverse
        coef_ref[7, here, :] = jnp.where(sub == 0, inverse, 0.0)

    row_blocks(0, full, BLOCK_K, row_coefficients)
    for k in range(8):
        coef_ref[k, 0:8, :] = jnp.zeros((8, LANES), f32)
        coef_ref[k, 8 * (full - 1) : 8 * full, :] = jnp.zeros((8, LANES), f32)

    rough, rain, evap, elev = flat_ref[0], flat_ref[1], flat_ref[2], flat_ref[3]
    head = flat_ref[4]
    land = jnp.where(rough > 0.0, 1.0, 0.0)

    def around(value):
        return (
            pltpu.roll(value, full - 1, 0),
            pltpu.roll(value, 1, 0),
            pltpu.roll(value, LANES - 1, 1),
            pltpu.roll(value, 1, 1),
        )

    faces = [0.5 * (rough + near) for near in around(rough)]
    top_cond = cond_ref[pl.ds(8, full, stride=8), :]
    rate = land * (infil_rate * top_cond / (1.0 + top_cond))
    loss = land * evap
    for cycle in range(CYCLES):
        top = press_ref[pl.ds(8, full, stride=8), :]
        level = head + elev
        flux = jnp.zeros_like(level)
        for face, near in zip(faces, around(level)):
            flux = flux + face * (near - level)
        infil = rate * (head - top)
        src_ref[...] = infil - loss * jax.nn.sigmoid(top)
        head = head + land * (rain - infil + flux)
        done = cycle * SWEEPS

        for sweep in range(SWEEPS):
            old, new = (press_ref, press2_ref) if sweep % 2 == 0 else (press2_ref, press_ref)

            def one_row(r):
                here = at_row(r - 1)
                mid = old[at_row(r), :]
                if sweep == 0:
                    source = jnp.broadcast_to(src_ref[pl.ds(r, 1), :], (8, LANES))
                    rhs = coef_ref[6, here, :] * mid + coef_ref[7, here, :] * source
                    rhs_ref[here, :] = rhs
                else:
                    rhs = rhs_ref[here, :]
                column = coef_ref[0, here, :] * beside(old, mid, r, -1) + coef_ref[1, here, :] * beside(old, mid, r, 1)
                across = coef_ref[2, here, :] * old[at_row(r - 1), :] + coef_ref[3, here, :] * old[at_row(r + 1), :]
                along = coef_ref[4, here, :] * pltpu.roll(mid, LANES - 1, 1) + coef_ref[5, here, :] * pltpu.roll(mid, 1, 1)
                new[at_row(r), :] = (rhs + column) + (across + along)

            first = done + sweep + 1
            low = first // STEP_S * STEP_S
            row_blocks(low, full - low, (full - 2 * low) // TRIPS_S, one_row)

    lane = lax.broadcasted_iota(jnp.int32, (8, LANES), 1)
    for r in range(HALO, HALO + rows, 8):
        layers = jnp.swapaxes(press_ref[8 * (r + 1) : 8 * (r + 9), :].reshape(8, 8, LANES), 0, 1)
        for s in range(4):
            out_ref[s, 0, r - HALO : r - HALO + 8, :] = jnp.where(
                lane < CHUNK,
                pltpu.roll(layers[2 * s], LANES - EDGE, 1),
                pltpu.roll(layers[2 * s + 1], EDGE, 1),
            )
            out_ref[s, 1, r - HALO : r - HALO + 8, :] = pltpu.roll(head[r : r + 8], LANES - EDGE, 1)


def finish_kernel(z_ref, press_ref, head_ref):
    rows = z_ref.shape[2]
    lane = lax.broadcasted_iota(jnp.int32, (rows, LANES), 1)
    for d in range(0, 4, 2):
        cols = slice(d * CHUNK, d * CHUNK + LANES)
        a, b = z_ref[d, 0], z_ref[d + 1, 0]
        press_ref[0, :, cols] = jnp.where(lane < CHUNK, a, pltpu.roll(b, CHUNK, 1))
        press_ref[1, :, cols] = jnp.where(lane < CHUNK, pltpu.roll(a, CHUNK, 1), b)
        head_ref[:, cols] = jnp.where(lane < CHUNK, z_ref[d, 1], pltpu.roll(z_ref[d + 1, 1], CHUNK, 1))


def main_call(rows, args):
    full = rows + 2 * HALO
    grid = (8 * full, LANES)
    framed = (8 * (full + 2), LANES)
    return call(
        main_kernel, (jax.ShapeDtypeStruct((4, 2, rows, LANES), f32),), args,
        scratch=[
            pltpu.VMEM((MSG_ROWS, LANES), f32),
            pltpu.VMEM((MSG_ROWS, LANES), f32),
            pltpu.VMEM((6, rows + 2 * CROWS, LANES), f32),
            pltpu.VMEM(framed, f32),
            pltpu.VMEM(framed, f32),
            pltpu.VMEM(framed, f32),
            pltpu.VMEM(framed, f32),
            pltpu.VMEM((8,) + grid, f32),
            pltpu.VMEM(grid, f32),
            pltpu.VMEM((5, full, LANES), f32),
            pltpu.VMEM((full, LANES), f32),
        ],
        name="cycles",
    )[0]


def shards(
    soil_class, geology_class, land_mask, river_mask, elevation, roughness, rainfall, potential_evap,
    surface_head, pressure, storage, soil_embed, geology_embed, conv_weight, out_weight,
):
    rows, width = soil_class.shape
    n_gx, n_gy = lax.axis_size("gx"), lax.axis_size("gy")
    sds = jax.ShapeDtypeStruct
    raw = (
        soil_class, geology_class, land_mask, river_mask, elevation, roughness, rainfall,
        potential_evap, surface_head, pressure, storage,
    )
    given = tuple(range(len(raw)))

    edge = sds((rows, 2 * LANES), f32)
    ya, yb = call(pack_cols_kernel, (edge, edge), raw, name="pack_cols", hbm=given)
    ya = lax.ppermute(ya, "gy", swap_pairs(n_gy, 0))
    yb = lax.ppermute(yb, "gy", swap_pairs(n_gy, 1))

    sel, tap = table_layout()
    (table,) = call(
        table_kernel, (sds((2 * LANES, KROWS), bf16),),
        (
            jnp.asarray(sel), jnp.asarray(tap), soil_embed, geology_embed,
            conv_weight.reshape(9, LANES, LANES),
        ),
        name="table", hbm=range(5),
    )
    proj = out_weight.T
    ya, yb, table = lax.optimization_barrier((ya, yb, table))

    z, cols = call(
        slice_kernel, (sds((4, 4, rows, LANES), f32), sds((7, rows, LANES), f32)), (*raw, ya, yb),
        scratch=[pltpu.VMEM((4, 7, rows, LANES), f32)], name="slices", hbm=given,
    )
    z = lax.all_to_all(z, "sec", 0, 0)
    (own,) = call(
        own_kernel, (sds((8 * (rows - 2 * OWN), LANES), f32),), (cols, table, proj),
        scratch=[pltpu.VMEM((6, rows, LANES), f32)], name="own_conduct", hbm=(2,),
    )
    z, own = lax.optimization_barrier((z, own))

    msg = sds((MSG_ROWS, LANES), f32)
    xa, xb = call(pack_rows_kernel, (msg, msg), (z, cols), name="pack_rows")
    xa = lax.ppermute(xa, "gx", swap_pairs(n_gx, 1))
    xb = lax.ppermute(xb, "gx", swap_pairs(n_gx, 0))
    out = main_call(rows, (z, cols, own, xa, xb, table, proj))
    out = lax.all_to_all(out, "sec", 0, 0)
    return call(finish_kernel, (sds(pressure.shape, f32), sds((rows, width), f32)), (out,), name="finish", final=True)


def solution(mesh):
    flat = P("gx", "gy")
    deep = P("sec", "gx", "gy")
    in_specs = (flat,) * 9 + (deep, deep) + (P(),) * 4
    return jax.shard_map(shards, mesh=mesh, in_specs=in_specs, out_specs=(deep, flat), check_vma=False)
```

time: 111 us -> 62.4 us (0.56)
  Pallas kernels: 57.3 us -> 15.3 us
  local copies, waits for them, and re-layouts: 2.72 us -> 0.01 us
  waiting for transfers between devices: 16 us -> 14.5 us
  other arithmetic: 1.24 us -> 0 us
    pallas_call x6 -> x7, Pallas kernels: 57.3 us -> 15.3 us  [call(): pl.pallas_call(kernel, out_shape=made, in_specs=[VMEM] * len(args), out_s...]
    ppermute x1, waiting for transfers between devices: 2.56 us -> 5.46 us  [shards(): xa = lax.ppermute(xa, 'gx', swap_pairs(n_gx, 1))]
    unnamed x13 -> x2, local copies, waits for them, and re-layouts: 2.72 us -> 0.01 us
    all_to_all x1, waiting for transfers between devices: 8.22 us -> 5.77 us  [shards(): z = lax.all_to_all(z, 'sec', 0, 0)]
    ppermute x1, waiting for transfers between devices: 2.95 us -> 1.04 us  [shards(): yb = lax.ppermute(yb, 'gy', swap_pairs(n_gy, 1))]
    another operation x2 -> x0, other arithmetic: 1.24 us -> none  [the longest x1 0.67 us: shards(): par_x = jnp.stack([gx % 2, sec]).astype(jnp.int32)]
  transfers between devices with their start and end apart: 5 -> 5, of which waited for: 4 -> 4; matrix products, arithmetic and copies ran while one was open for 1% -> 0% of each run, Pallas kernels for 2% -> 8%
where the time goes in v2:
time: 62.4 us; the launch traced here: 61.9 us
  starting transfers between devices  21.7 us (35%)
  Pallas kernels  15.3 us (25%)
  waiting for transfers between devices  14.5 us (23%)
  blocking collectives  9.7 us (16%)
  between operations  0.71 us (1%)
    pallas_call x7, Pallas kernels, call(): pl.pallas_call(kernel, out_shape=made, in_specs=[VMEM] * len(args), out_s...  15.3 us
    all_to_all x1, blocking collectives, shards(): out = lax.all_to_all(out, 'sec', 0, 0)  9.7 us
    ppermute x1, starting transfers between devices, shards(): xa = lax.ppermute(xa, 'gx', swap_pairs(n_gx, 1))  8.13 us
    all_to_all x1, starting transfers between devices, shards(): z = lax.all_to_all(z, 'sec', 0, 0)  7.26 us
    all_to_all x1, waiting for transfers between devices, shards(): z = lax.all_to_all(z, 'sec', 0, 0)  5.77 us
    ppermute x1, waiting for transfers between devices, shards(): xa = lax.ppermute(xa, 'gx', swap_pairs(n_gx, 1))  5.46 us
    ppermute x1, starting transfers between devices, shards(): yb = lax.ppermute(yb, 'gy', swap_pairs(n_gy, 1))  2.46 us
    ppermute x1, waiting for transfers between devices, shards(): xb = lax.ppermute(xb, 'gx', swap_pairs(n_gx, 0))  2.25 us
  transfers between devices with their start and end apart: 5, of which 4 were waited for; matrix products, arithmetic and copies ran while one was open for 0% of the time, Pallas kernels for 8%

profile of v2, /device:TPU:30, one launch (start us, length us, event | category | flops | bytes accessed | tf_op | source)
XLA Modules:
  0.0 61.9 jit_solution(17709782841030830837)
XLA Ops:
  0.6 1.2 %pack_cols.1 = (f32[32,256]{1,0:T(8,128)S(1)}, f32[32,256]{1,0:T(8,128)S(1)}) custom-call(s32[32,256]{1,0:T(8,128)} %soil.3, s32[32,256]{1,0:T(8,128)} %geo.3, s32[32,256]{1,0:T(8,128)} %land.3, s32[32,256]{1,0:T(8,128)} %river.3, f32[32,256]{1,0:T(8,128)} %elev.3, f32[32,256]{1,0:T(8,128)} %rough.3, f32[32,256]{1,0:T(8,128)} %rain.3, f32[32,256]{1,0:T(8,128)} %evap.3, ...), custom_call_target="tpu_custom_call" | custom-call | tf_op jit(solution)/shard_map/pack_cols/pallas_call | solution.py:35
  1.8 1.9 %collective-permute-start = (f32[32,256]{1,0:T(8,128)S(1)}, f32[32,256]{1,0:T(8,128)S(1)}, u32[]{:S(2)}, u32[]{:S(2)}) collective-permute-start(f32[32,256]{1,0:T(8,128)S(1)} %get-tuple-element.13), channel_id=1, source_target_pairs={{0,1},{1,0},{2,3},{3,2},{4,5},{5,4},{6,7},{7,6},{8,9},{9,8},{10,11... | collective-permute-start | bytes 98312 | tf_op jit(solution)/shard_map/ppermute | solution.py:471
  3.7 2.5 %collective-permute-start.1 = (f32[32,256]{1,0:T(8,128)S(1)}, f32[32,256]{1,0:T(8,128)S(1)}, u32[]{:S(2)}, u32[]{:S(2)}) collective-permute-start(f32[32,256]{1,0:T(8,128)S(1)} %get-tuple-element.14), channel_id=1, source_target_pairs={{1,2},{2,1},{3,4},{4,3},{5,6},{6,5},{7,8},{8,7},{9,10},{10,9},{11,... | collective-permute-start | bytes 98312 | tf_op jit(solution)/shard_map/ppermute | solution.py:472
  6.2 1.7 %table.1.table_ref = bf16[256,256]{1,0:T(8,128)(2,1)S(1)} custom-call(f32[256,28]{1,0:T(8,128)} %constant.4.clone.sel_ref, s32[256,128]{1,0:T(8,128)} %constant.5.clone.tap_ref, bf16[12,128]{1,0:T(8,128)(2,1)} %soil_ref.1, bf16[16,128]{1,0:T(8,128)(2,1)} %geo_ref.1, bf16[9,128,128]{2,1,0:T(8,128)(2,1)} %bitcast.4), custom_call_target="tpu_custom_call" | custom-call | tf_op jit(solution)/shard_map/table/pallas_call | solution.py:35
  7.9 0.0 collective-permute-done.a_ref
  7.9 1.0 %collective-permute-done.1.b_ref = f32[32,256]{1,0:T(8,128)S(1)} collective-permute-done((f32[32,256]{1,0:T(8,128)S(1)}, f32[32,256]{1,0:T(8,128)S(1)}, u32[]{:S(2)}, u32[]{:S(2)}) %collective-permute-start.1) | collective-permute-done | bytes 32800 | tf_op jit(solution)/shard_map/ppermute | solution.py:472
  9.0 2.0 %slices.1 = (f32[4,4,32,128]{3,2,1,0:T(8,128)}, f32[7,32,128]{2,1,0:T(8,128)S(1)}) custom-call(s32[32,256]{1,0:T(8,128)} %soil.3, s32[32,256]{1,0:T(8,128)} %geo.3, s32[32,256]{1,0:T(8,128)} %land.3, s32[32,256]{1,0:T(8,128)} %river.3, f32[32,256]{1,0:T(8,128)} %elev.3, f32[32,256]{1,0:T(8,128)} %rough.3, f32[32,256]{1,0:T(8,128)} %rain.3, f32[32,256]{1,0:T(8,128)} %evap.3, ...), custom_call_target="tpu_custom_call" | custom-call | tf_op jit(solution)/shard_map/slices/pallas_call | solution.py:35
  11.0 7.3 %all-to-all-start = ((f32[4,4,32,128]{3,2,1,0:T(8,128)}), f32[4,4,32,128]{3,2,1,0:T(8,128)S(1)}, u32[]{:S(2)}, u32[]{:S(2)}) async-start(f32[4,4,32,128]{3,2,1,0:T(8,128)} %get-tuple-element.17), calls=%async_computation | async-start | bytes 524288 | tf_op jit(solution)/shard_map/all_to_all | solution.py:490
  18.2 3.1 %own_conduct.1.own_ref = f32[224,128]{1,0:T(8,128)S(1)} custom-call(f32[7,32,128]{2,1,0:T(8,128)S(1)} %get-tuple-element.18.c_ref, bf16[256,256]{1,0:T(8,128)(2,1)S(1)} %table.1.table_ref, bf16[8,128]{1,0:T(8,128)(2,1)} %bitcast.2), custom_call_target="tpu_custom_call" | custom-call | tf_op jit(solution)/shard_map/own_conduct/pallas_call | solution.py:35
  21.4 5.8 %all-to-all-done.z_ref = f32[4,4,32,128]{3,2,1,0:T(8,128)S(1)} async-done(((f32[4,4,32,128]{3,2,1,0:T(8,128)}), f32[4,4,32,128]{3,2,1,0:T(8,128)S(1)}, u32[]{:S(2)}, u32[]{:S(2)}) %all-to-all-start) | async-done | bytes 262176 | tf_op jit(solution)/shard_map/all_to_all | solution.py:490
  27.2 0.0 copy-start
  27.2 8.1 %collective-permute-start.2 = (f32[384,128]{1,0:T(8,128)S(1)}, f32[384,128]{1,0:T(8,128)S(1)}, u32[]{:S(2)}, u32[]{:S(2)}) collective-permute-start(f32[384,128]{1,0:T(8,128)S(1)} %get-tuple-element.22), channel_id=1, source_target_pairs={{16,32},{32,16},{48,64},{64,48},{80,96},{96,80},{17,33},{33,17},{4... | collective-permute-start | bytes 589832 | tf_op jit(solution)/shard_map/ppermute | solution.py:499
  35.3 1.9 %collective-permute-start.3 = (f32[384,128]{1,0:T(8,128)S(1)}, f32[384,128]{1,0:T(8,128)S(1)}, u32[]{:S(2)}, u32[]{:S(2)}) collective-permute-start(f32[384,128]{1,0:T(8,128)S(1)} %get-tuple-element.23), channel_id=1, source_target_pairs={{0,16},{16,0},{32,48},{48,32},{64,80},{80,64},{96,112},{112,96},{1... | collective-permute-start | bytes 589832 | tf_op jit(solution)/shard_map/ppermute | solution.py:500
  37.2 5.5 %collective-permute-done.2.a_ref = f32[384,128]{1,0:T(8,128)S(1)} collective-permute-done((f32[384,128]{1,0:T(8,128)S(1)}, f32[384,128]{1,0:T(8,128)S(1)}, u32[]{:S(2)}, u32[]{:S(2)}) %collective-permute-start.2) | collective-permute-done | bytes 196640 | tf_op jit(solution)/shard_map/ppermute | solution.py:499
  42.7 2.2 %collective-permute-done.3.b_ref = f32[384,128]{1,0:T(8,128)S(1)} collective-permute-done((f32[384,128]{1,0:T(8,128)S(1)}, f32[384,128]{1,0:T(8,128)S(1)}, u32[]{:S(2)}, u32[]{:S(2)}) %collective-permute-start.3) | collective-permute-done | bytes 196640 | tf_op jit(solution)/shard_map/ppermute | solution.py:500
  45.0 0.0 copy-done
  45.0 6.5 %cycles.1 = f32[4,2,32,128]{3,2,1,0:T(8,128)S(1)} custom-call(f32[4,4,32,128]{3,2,1,0:T(8,128)S(1)} %all-to-all-done.z_ref, f32[7,32,128]{2,1,0:T(8,128)S(1)} %get-tuple-element.18.c_ref, f32[224,128]{1,0:T(8,128)S(1)} %own_conduct.1.own_ref, f32[384,128]{1,0:T(8,128)S(1)} %collective-permute-done.2.a_ref, f32[384,128]{1,0:T(8,128)S(1)} %collective-permute-done.3.b_ref, ...), custom_call_target="tpu_custom_call" | custom-call | tf_op jit(solution)/shard_map/cycles/pallas_call | solution.py:35
  51.5 9.7 %all_to_all.10.z_ref = f32[4,2,32,128]{3,2,1,0:T(8,128)S(1)} all-to-all(f32[4,2,32,128]{3,2,1,0:T(8,128)S(1)} %cycles.1), channel_id=1, replica_groups=mesh['sec'=4,'gx'=8,'gy'=16] {'sec'}, dimensions={0} | all-to-all | bytes 262144 | tf_op jit(solution)/shard_map/all_to_all | solution.py:502
  61.2 0.7 %finish.1 = (f32[2,32,256]{2,1,0:T(8,128)}, f32[32,256]{1,0:T(8,128)}) custom-call(f32[4,2,32,128]{3,2,1,0:T(8,128)S(1)} %all_to_all.10.z_ref), custom_call_target="tpu_custom_call" | custom-call | tf_op jit(solution)/shard_map/finish/pallas_call | solution.py:35
  (1 shorter events, 0.0 us)
Async XLA Ops:
  1.8 6.1 %collective-permute-start = (f32[32,256]{1,0:T(8,128)S(1)}, f32[32,256]{1,0:T(8,128)S(1)}, u32[]{:S(2)}, u32[]{:S(2)}) collective-permute-start(f32[32,256]{1,0:T(8,128)S(1)} %get-tuple-element.13), channel_id=1, source_target_pairs={{0,1},{1,0},{2,3},{3,2},{4,5},{5,4},{6,7},{7,6},{8,9},{9,8},{10,11... | collective-permute-start | bytes 98312 | tf_op jit(solution)/shard_map/ppermute | solution.py:471
  3.7 5.2 %collective-permute-start.1 = (f32[32,256]{1,0:T(8,128)S(1)}, f32[32,256]{1,0:T(8,128)S(1)}, u32[]{:S(2)}, u32[]{:S(2)}) collective-permute-start(f32[32,256]{1,0:T(8,128)S(1)} %get-tuple-element.14), channel_id=1, source_target_pairs={{1,2},{2,1},{3,4},{4,3},{5,6},{6,5},{7,8},{8,7},{9,10},{10,9},{11,... | collective-permute-start | bytes 98312 | tf_op jit(solution)/shard_map/ppermute | solution.py:472
  11.0 16.2 %all-to-all-start = ((f32[4,4,32,128]{3,2,1,0:T(8,128)}), f32[4,4,32,128]{3,2,1,0:T(8,128)S(1)}, u32[]{:S(2)}, u32[]{:S(2)}) async-start(f32[4,4,32,128]{3,2,1,0:T(8,128)} %get-tuple-element.17), calls=%async_computation | async-start | bytes 524288 | tf_op jit(solution)/shard_map/all_to_all | solution.py:490
  27.2 17.8 %copy-start = (bf16[128,8]{0,1:T(8,128)(2,1)S(1)}, bf16[128,8]{0,1:T(8,128)(2,1)}, u32[]{:S(2)}) copy-start(bf16[128,8]{0,1:T(8,128)(2,1)} %param.31) | copy-start | bytes 6148
  27.2 15.5 %collective-permute-start.2 = (f32[384,128]{1,0:T(8,128)S(1)}, f32[384,128]{1,0:T(8,128)S(1)}, u32[]{:S(2)}, u32[]{:S(2)}) collective-permute-start(f32[384,128]{1,0:T(8,128)S(1)} %get-tuple-element.22), channel_id=1, source_target_pairs={{16,32},{32,16},{48,64},{64,48},{80,96},{96,80},{17,33},{33,17},{4... | collective-permute-start | bytes 589832 | tf_op jit(solution)/shard_map/ppermute | solution.py:499
  35.3 9.6 %collective-permute-start.3 = (f32[384,128]{1,0:T(8,128)S(1)}, f32[384,128]{1,0:T(8,128)S(1)}, u32[]{:S(2)}, u32[]{:S(2)}) collective-permute-start(f32[384,128]{1,0:T(8,128)S(1)} %get-tuple-element.23), channel_id=1, source_target_pairs={{0,16},{16,0},{32,48},{48,32},{64,80},{80,64},{96,112},{112,96},{1... | collective-permute-start | bytes 589832 | tf_op jit(solution)/shard_map/ppermute | solution.py:500

commit v3 on v2

--- a/solution.py
+++ b/solution.py
@@ -123,7 +123,7 @@
 
 def slice_kernel(
     soil, geo, land, river, elev, rough, rain, evap, head, press, stor, a_ref, b_ref,
-    z_ref, c_ref, work_ref,
+    z_ref, c_ref, ca_ref, cb_ref, work_ref,
 ):
     odd = lax.axis_index("gy") % 2 == 1
     plain, classes = columns(
@@ -162,38 +162,54 @@
         for d, part in enumerate(slices(value, half, at, wide)):
             work_ref[d, j] = part
     c_ref[...] = work_ref[lax.axis_index("sec")]
-
-
-def pack_rows_kernel(z_ref, c_ref, a_ref, b_ref):
+    odd_x = lax.axis_index("gx") % 2 == 1
+    low = jnp.where(odd_x, rows - HALO, 0)
+    low_class = jnp.where(odd_x, rows - CROWS, 0)
+    for ref, at, at_class in (
+        (ca_ref, low, low_class),
+        (cb_ref, (rows - HALO) - low, (rows - CROWS) - low_class),
+    ):
+        for j in range(5):
+            ref[j * HALO : (j + 1) * HALO, :] = c_ref[j, pl.ds(pl.multiple_of(at, 8), HALO), :]
+        for j in range(2):
+            to = 5 * HALO + j * CROWS
+            ref[to : to + CROWS, :] = c_ref[5 + j, pl.ds(pl.multiple_of(at_class, 8), CROWS), :]
+
+
+def pack_rows_kernel(z_ref, a_ref, b_ref):
     odd = lax.axis_index("gx") % 2 == 1
     rows = z_ref.shape[2]
     low = jnp.where(odd, rows - HALO, 0)
-    low_class = jnp.where(odd, rows - CROWS, 0)
-    for ref, at, at_class in (
-        (a_ref, low, low_class),
-        (b_ref, (rows - HALO) - low, (rows - CROWS) - low_class),
-    ):
+    lane = lax.broadcasted_iota(jnp.int32, (HALO, LANES), 1)
+    free = (lane < EDGE - HALO) | (lane >= LANES - EDGE + HALO)
+    for ref, at in ((a_ref, low), (b_ref, (rows - HALO) - low)):
         at = pl.multiple_of(at, 8)
-        at_class = pl.multiple_of(at_class, 8)
         for s in range(4):
-            for i in range(4):
-                k = 8 * (i // 2) + 2 * s + i % 2
-                ref[pl.ds(k * HALO, HALO), :] = z_ref[s, i, pl.ds(at, HALO), :]
-        for j in range(5):
-            ref[pl.ds((16 + j) * HALO, HALO), :] = c_ref[j, pl.ds(at, HALO), :]
-        for j in range(2):
-            ref[pl.ds(21 * HALO + j * CROWS, CROWS), :] = c_ref[5 + j, pl.ds(at_class, CROWS), :]
-
-
-MSG_ROWS = 21 * HALO + 2 * CROWS
+            last = z_ref[s, 3, pl.ds(at, HALO), :]
+            for i in range(3):
+                k = (3 * s + i) * HALO
+                moved = pltpu.roll(last, LANES - EDGE * (i + 1), 1)
+                ref[k : k + HALO, :] = jnp.where(free, moved, z_ref[s, i, pl.ds(at, HALO), :])
+
+
+def unpack(ref, s):
+    lane = lax.broadcasted_iota(jnp.int32, (HALO, LANES), 1)
+    parts = [ref[(3 * s + i) * HALO : (3 * s + i + 1) * HALO, :] for i in range(3)]
+    last = jnp.zeros((HALO, LANES), f32)
+    for i, part in enumerate(parts):
+        start = EDGE - HALO + EDGE * i
+        last = jnp.where((lane >= start) & (lane < start + EDGE), pltpu.roll(part, EDGE * (i + 1), 1), last)
+    return parts + [last]
+
+
+MSG_ROWS = 12 * HALO
+MSG_ROWS_2D = 5 * HALO + 2 * CROWS
 
 
 STEP_S = 8
 TRIPS_S = 1
 BLOCK_K = 16
-UNROLL_C = 3
-UNROLL_OWN = 7
-OWN = 2
+UNROLL_C = 8
 
 
 def at_row(r):
@@ -265,71 +281,65 @@
     return out
 
 
-def own_kernel(c_ref, table_ref, proj_ref, cond_ref, shift_ref):
-    rows = c_ref.shape[1]
+def by_side(a_ref, b_ref):
+    odd = lax.axis_index("gx") % 2 == 1
+    a, b = a_ref[...], b_ref[...]
+    return jnp.where(odd, b, a), jnp.where(odd, a, b)
+
+
+def conduct_kernel(c_ref, ca_ref, cb_ref, table_ref, proj_ref, cond_ref, shift_ref):
+    full = c_ref.shape[1] + 2 * HALO
+    above, below = by_side(ca_ref, cb_ref)
     for kind in range(2):
-        shift_classes(shift_ref, kind, c_ref[5 + kind])
+        at = 5 * HALO + kind * CROWS
+        value = jnp.concatenate([above[at : at + CROWS], c_ref[5 + kind], below[at : at + CROWS]], axis=0)
+        shift_classes(shift_ref, kind, value)
     table, proj = table_ref[...], proj_ref[...]
 
     def step(i, carry):
-        for k, value in enumerate(conduct_rows(shift_ref, 2 * i + OWN, table, proj)):
-            cond_ref[pl.ds(pl.multiple_of(8 * (2 * i + k), 8), 8), :] = value
+        for k, value in enumerate(conduct_rows(shift_ref, 2 * i + CROWS - HALO, table, proj)):
+            cond_ref[at_row(2 * i + k), :] = value
         return carry
 
-    lax.fori_loop(0, rows // 2 - OWN, step, 0, unroll=UNROLL_OWN)
+    lax.fori_loop(0, full // 2, step, 0, unroll=UNROLL_C)
+    cond_ref[0:8, :] = jnp.zeros((8, LANES), f32)
+    cond_ref[8 * (full + 1) :, :] = jnp.zeros((8, LANES), f32)
 
 
 def main_kernel(
-    z_ref, c_ref, own_ref, a_ref, b_ref, table_ref, proj_ref, out_ref,
-    top_ref, bot_ref, shift_ref, cond_ref, press_ref, press2_ref, stor_ref, coef_ref, rhs_ref, flat_ref, src_ref,
+    z_ref, c_ref, ca_ref, cb_ref, a_ref, b_ref, cond_ref, out_ref,
+    press_ref, press2_ref, stor_ref, coef_ref, rhs_ref, flat_ref, src_ref,
 ):
-    odd = lax.axis_index("gx") % 2 == 1
     rows = z_ref.shape[2]
     full = rows + 2 * HALO
-    top_ref[...] = jnp.where(odd, b_ref[...], a_ref[...])
-    bot_ref[...] = jnp.where(odd, a_ref[...], b_ref[...])
-
-    for j in range(2):
-        at = 21 * HALO + j * CROWS
-        value = jnp.concatenate([top_ref[at : at + CROWS, :], c_ref[5 + j], bot_ref[at : at + CROWS, :]], axis=0)
-        shift_classes(shift_ref, j, value)
+    above, below = by_side(ca_ref, cb_ref)
 
     for j in range(5):
-        at = (16 + j) * HALO
-        flat_ref[j, 0:HALO, :] = top_ref[at : at + HALO, :]
+        at = j * HALO
+        flat_ref[j, 0:HALO, :] = above[at : at + HALO]
         flat_ref[j, HALO : HALO + rows, :] = c_ref[j]
-        flat_ref[j, HALO + rows : full, :] = bot_ref[at : at + HALO, :]
+        flat_ref[j, HALO + rows : full, :] = below[at : at + HALO]
 
     for ref in (press_ref, press2_ref):
         ref[0:8, :] = jnp.zeros((8, LANES), f32)
         ref[8 * (full + 1) :, :] = jnp.zeros((8, LANES), f32)
+    north, south = by_side(a_ref, b_ref)
+    sides = [[unpack(side, s) for s in range(4)] for side in (north, south)]
     for f, ref in ((0, press_ref), (1, stor_ref)):
         for r in range(0, full, 8):
             parts = []
             for l in range(8):
-                k = 8 * f + l
+                s, i = l // 2, 2 * f + l % 2
                 if r < HALO:
-                    part = top_ref[k * HALO + r : k * HALO + r + 8, :]
+                    part = sides[0][s][i][r : r + 8]
                 elif r < HALO + rows:
-                    part = z_ref[l // 2, 2 * f + l % 2, r - HALO : r - HALO + 8, :]
+                    part = z_ref[s, i, r - HALO : r - HALO + 8, :]
                 else:
-                    at = k * HALO + r - HALO - rows
-                    part = bot_ref[at : at + 8, :]
+                    at = r - HALO - rows
+                    part = sides[1][s][i][at : at + 8]
                 parts.append(part)
             mixed = jnp.swapaxes(jnp.stack(parts), 0, 1).reshape(64, LANES)
             ref[8 * (r + 1) : 8 * (r + 9), :] = mixed
-
-    table, proj = table_ref[...], proj_ref[...]
-    cond_ref[8 * (HALO + OWN + 1) : 8 * (HALO + rows - OWN + 1), :] = own_ref[...]
-    half = (HALO + OWN) // 2
-
-    def step(i, carry):
-        for row in (2 * i, full - 2 * half + 2 * i):
-            for k, value in enumerate(conduct_rows(shift_ref, row + CROWS - HALO, table, proj)):
-                cond_ref[at_row(row + k), :] = value
-        return carry
-
-    lax.fori_loop(0, half, step, 0, unroll=UNROLL_C)
     sub = lax.broadcasted_iota(jnp.int32, (8, LANES), 0)
 
     def row_coefficients(r):
@@ -437,10 +447,6 @@
     return call(
         main_kernel, (jax.ShapeDtypeStruct((4, 2, rows, LANES), f32),), args,
         scratch=[
-            pltpu.VMEM((MSG_ROWS, LANES), f32),
-            pltpu.VMEM((MSG_ROWS, LANES), f32),
-            pltpu.VMEM((6, rows + 2 * CROWS, LANES), f32),
-            pltpu.VMEM(framed, f32),
             pltpu.VMEM(framed, f32),
             pltpu.VMEM(framed, f32),
             pltpu.VMEM(framed, f32),
@@ -471,6 +477,16 @@
     ya = lax.ppermute(ya, "gy", swap_pairs(n_gy, 0))
     yb = lax.ppermute(yb, "gy", swap_pairs(n_gy, 1))
 
+    plane, edge_2d = sds((7, rows, LANES), f32), sds((MSG_ROWS_2D, LANES), f32)
+    z, cols, ca, cb = call(
+        slice_kernel, (sds((4, 4, rows, LANES), f32), plane, edge_2d, edge_2d), (*raw, ya, yb),
+        scratch=[pltpu.VMEM((4, 7, rows, LANES), f32)], name="slices", hbm=given,
+    )
+    z = lax.all_to_all(z, "sec", 0, 0)
+
+    ca = lax.ppermute(ca, "gx", swap_pairs(n_gx, 1))
+    cb = lax.ppermute(cb, "gx", swap_pairs(n_gx, 0))
+    cols, soil_embed = lax.optimization_barrier((cols, soil_embed))
     sel, tap = table_layout()
     (table,) = call(
         table_kernel, (sds((2 * LANES, KROWS), bf16),),
@@ -480,25 +496,19 @@
         ),
         name="table", hbm=range(5),
     )
-    proj = out_weight.T
-    ya, yb, table = lax.optimization_barrier((ya, yb, table))
-
-    z, cols = call(
-        slice_kernel, (sds((4, 4, rows, LANES), f32), sds((7, rows, LANES), f32)), (*raw, ya, yb),
-        scratch=[pltpu.VMEM((4, 7, rows, LANES), f32)], name="slices", hbm=given,
-    )
-    z = lax.all_to_all(z, "sec", 0, 0)
-    (own,) = call(
-        own_kernel, (sds((8 * (rows - 2 * OWN), LANES), f32),), (cols, table, proj),
-        scratch=[pltpu.VMEM((6, rows, LANES), f32)], name="own_conduct", hbm=(2,),
-    )
-    z, own = lax.optimization_barrier((z, own))
+    z, ca, cb, table = lax.optimization_barrier((z, ca, cb, table))
 
     msg = sds((MSG_ROWS, LANES), f32)
-    xa, xb = call(pack_rows_kernel, (msg, msg), (z, cols), name="pack_rows")
+    xa, xb = call(pack_rows_kernel, (msg, msg), (z,), name="pack_rows")
+    xa, xb, cols = lax.optimization_barrier((xa, xb, cols))
     xa = lax.ppermute(xa, "gx", swap_pairs(n_gx, 1))
     xb = lax.ppermute(xb, "gx", swap_pairs(n_gx, 0))
-    out = main_call(rows, (z, cols, own, xa, xb, table, proj))
+    (cond,) = call(
+        conduct_kernel, (sds((8 * (rows + 2 * HALO + 2), LANES), f32),), (cols, ca, cb, table, out_weight.T),
+        scratch=[pltpu.VMEM((6, rows + 2 * CROWS, LANES), f32)], name="conduct", hbm=(4,),
+    )
+    xa, xb, cond = lax.optimization_barrier((xa, xb, cond))
+    out = main_call(rows, (z, cols, ca, cb, xa, xb, cond))
     out = lax.all_to_all(out, "sec", 0, 0)
     return call(finish_kernel, (sds(pressure.shape, f32), sds((rows, width), f32)), (out,), name="finish", final=True)
 

time: 62.4 us -> 64.4 us (1.032)
  the two profiles are of different devices: /device:TPU:30 before, /device:TPU:36 now
where the time goes in v3:
time: 64.4 us; the launch traced here: 63.9 us
  starting transfers between devices  32.8 us (51%)
  Pallas kernels  15 us (23%)
  blocking collectives  10.8 us (17%)
  waiting for transfers between devices  4.48 us (7%)
  between operations  0.73 us (1%)
    pallas_call x7, Pallas kernels, call(): pl.pallas_call(kernel, out_shape=made, in_specs=[VMEM] * len(args), out_s...  15 us
    all_to_all x1, blocking collectives, shards(): out = lax.all_to_all(out, 'sec', 0, 0)  10.8 us
    ppermute x1, starting transfers between devices, shards(): cb = lax.ppermute(cb, 'gx', swap_pairs(n_gx, 0))  8.79 us
    ppermute x1, starting transfers between devices, shards(): xb = lax.ppermute(xb, 'gx', swap_pairs(n_gx, 0))  8.03 us
    all_to_all x1, starting transfers between devices, shards(): z = lax.all_to_all(z, 'sec', 0, 0)  7.26 us
    ppermute x1, waiting for transfers between devices, shards(): yb = lax.ppermute(yb, 'gy', swap_pairs(n_gy, 1))  3.97 us
    ppermute x1, starting transfers between devices, shards(): yb = lax.ppermute(yb, 'gy', swap_pairs(n_gy, 1))  2.46 us
    ppermute x1, starting transfers between devices, shards(): ca = lax.ppermute(ca, 'gx', swap_pairs(n_gx, 1))  2.43 us
  transfers between devices with their start and end apart: 7, of which 2 were waited for; matrix products, arithmetic and copies ran while one was open for 0% of the time, Pallas kernels for 12%

profile of v3, /device:TPU:36, one launch (start us, length us, event | category | flops | bytes accessed | tf_op | source)
XLA Modules:
  0.0 63.9 jit_solution(13888166269647961044)
XLA Ops:
  0.6 1.2 %pack_cols.1 = (f32[32,256]{1,0:T(8,128)S(1)}, f32[32,256]{1,0:T(8,128)S(1)}) custom-call(s32[32,256]{1,0:T(8,128)} %soil.3, s32[32,256]{1,0:T(8,128)} %geo.3, s32[32,256]{1,0:T(8,128)} %land.3, s32[32,256]{1,0:T(8,128)} %river.3, f32[32,256]{1,0:T(8,128)} %elev.3, f32[32,256]{1,0:T(8,128)} %rough.3, f32[32,256]{1,0:T(8,128)} %rain.3, f32[32,256]{1,0:T(8,128)} %evap.3, ...), custom_call_target="tpu_custom_call" | custom-call | tf_op jit(solution)/shard_map/pack_cols/pallas_call | solution.py:35
  1.8 1.9 %collective-permute-start = (f32[32,256]{1,0:T(8,128)S(1)}, f32[32,256]{1,0:T(8,128)S(1)}, u32[]{:S(2)}, u32[]{:S(2)}) collective-permute-start(f32[32,256]{1,0:T(8,128)S(1)} %get-tuple-element.22), channel_id=1, source_target_pairs={{0,1},{1,0},{2,3},{3,2},{4,5},{5,4},{6,7},{7,6},{8,9},{9,8},{10,11... | collective-permute-start | bytes 98312 | tf_op jit(solution)/shard_map/ppermute | solution.py:477
  3.7 2.5 %collective-permute-start.1 = (f32[32,256]{1,0:T(8,128)S(1)}, f32[32,256]{1,0:T(8,128)S(1)}, u32[]{:S(2)}, u32[]{:S(2)}) collective-permute-start(f32[32,256]{1,0:T(8,128)S(1)} %get-tuple-element.23), channel_id=1, source_target_pairs={{1,2},{2,1},{3,4},{4,3},{5,6},{6,5},{7,8},{8,7},{9,10},{10,9},{11,... | collective-permute-start | bytes 98312 | tf_op jit(solution)/shard_map/ppermute | solution.py:478
  6.2 0.0 collective-permute-done.a_ref
  6.2 4.0 %collective-permute-done.1.b_ref = f32[32,256]{1,0:T(8,128)S(1)} collective-permute-done((f32[32,256]{1,0:T(8,128)S(1)}, f32[32,256]{1,0:T(8,128)S(1)}, u32[]{:S(2)}, u32[]{:S(2)}) %collective-permute-start.1) | collective-permute-done | bytes 32800 | tf_op jit(solution)/shard_map/ppermute | solution.py:478
  10.2 2.0 %slices.1 = (f32[4,4,32,128]{3,2,1,0:T(8,128)}, f32[7,32,128]{2,1,0:T(8,128)S(1)}, f32[128,128]{1,0:T(8,128)S(1)}, f32[128,128]{1,0:T(8,128)S(1)}) custom-call(s32[32,256]{1,0:T(8,128)} %soil.3, s32[32,256]{1,0:T(8,128)} %geo.3, s32[32,256]{1,0:T(8,128)} %land.3, s32[32,256]{1,0:T(8,128)} %river.3, f32[32,256]{1,0:T(8,128)} %elev.3, f32[32,256]{1,0:T(8,128)} %rough.3, ...), custom_call_target="tpu_custom_call" | custom-call | tf_op jit(solution)/shard_map/slices/pallas_call | solution.py:35
  12.2 7.3 %all-to-all-start = ((f32[4,4,32,128]{3,2,1,0:T(8,128)}), f32[4,4,32,128]{3,2,1,0:T(8,128)S(1)}, u32[]{:S(2)}, u32[]{:S(2)}) async-start(f32[4,4,32,128]{3,2,1,0:T(8,128)} %get-tuple-element.24), calls=%async_computation | async-start | bytes 524288 | tf_op jit(solution)/shard_map/all_to_all | solution.py:485
  19.5 2.4 %collective-permute-start.2 = (f32[128,128]{1,0:T(8,128)S(1)}, f32[128,128]{1,0:T(8,128)S(1)}, u32[]{:S(2)}, u32[]{:S(2)}) collective-permute-start(f32[128,128]{1,0:T(8,128)S(1)} %get-tuple-element.25), channel_id=1, source_target_pairs={{16,32},{32,16},{48,64},{64,48},{80,96},{96,80},{17,33},{33,17},{4... | collective-permute-start | bytes 196616 | tf_op jit(solution)/shard_map/ppermute | solution.py:487
  21.9 8.8 %collective-permute-start.3 = (f32[128,128]{1,0:T(8,128)S(1)}, f32[128,128]{1,0:T(8,128)S(1)}, u32[]{:S(2)}, u32[]{:S(2)}) collective-permute-start(f32[128,128]{1,0:T(8,128)S(1)} %get-tuple-element.26), channel_id=1, source_target_pairs={{0,16},{16,0},{32,48},{48,32},{64,80},{80,64},{96,112},{112,96},{1... | collective-permute-start | bytes 196616 | tf_op jit(solution)/shard_map/ppermute | solution.py:488
  30.7 1.7 %table.1.table_ref = bf16[256,256]{1,0:T(8,128)(2,1)S(1)} custom-call(f32[256,28]{1,0:T(8,128)} %constant.4.clone.sel_ref, s32[256,128]{1,0:T(8,128)} %constant.5.clone.tap_ref, bf16[12,128]{1,0:T(8,128)(2,1)} %soil_ref, bf16[16,128]{1,0:T(8,128)(2,1)} %geo_ref.1, bf16[9,128,128]{2,1,0:T(8,128)(2,1)} %bitcast.2), custom_call_target="tpu_custom_call" | custom-call | tf_op jit(solution)/shard_map/table/pallas_call | solution.py:35
  32.4 0.0 collective-permute-done.2.ca_ref
  32.4 0.5 collective-permute-done.3.cb_ref
  33.0 0.0 all-to-all-done.z_ref
  33.0 0.1 pack_rows.1
  33.1 1.9 %collective-permute-start.4 = (f32[192,128]{1,0:T(8,128)S(1)}, f32[192,128]{1,0:T(8,128)S(1)}, u32[]{:S(2)}, u32[]{:S(2)}) collective-permute-start(f32[192,128]{1,0:T(8,128)S(1)} %get-tuple-element.36), channel_id=1, source_target_pairs={{16,32},{32,16},{48,64},{64,48},{80,96},{96,80},{17,33},{33,17},{4... | collective-permute-start | bytes 294920 | tf_op jit(solution)/shard_map/ppermute | solution.py:504
  35.0 8.0 %collective-permute-start.5 = (f32[192,128]{1,0:T(8,128)S(1)}, f32[192,128]{1,0:T(8,128)S(1)}, u32[]{:S(2)}, u32[]{:S(2)}) collective-permute-start(f32[192,128]{1,0:T(8,128)S(1)} %get-tuple-element.37), channel_id=1, source_target_pairs={{0,16},{16,0},{32,48},{48,32},{64,80},{80,64},{96,112},{112,96},{1... | collective-permute-start | bytes 294920 | tf_op jit(solution)/shard_map/ppermute | solution.py:505
  43.0 6.2 %conduct.1.cond_ref = f32[528,128]{1,0:T(8,128)S(1)} custom-call(f32[7,32,128]{2,1,0:T(8,128)S(1)} %get-tuple-element.33.c_ref, f32[128,128]{1,0:T(8,128)S(1)} %collective-permute-done.2.ca_ref, f32[128,128]{1,0:T(8,128)S(1)} %collective-permute-done.3.cb_ref, bf16[256,256]{1,0:T(8,128)(2,1)S(1)} %table.1.table_ref, bf16[8,128]{1,0:T(8,128)(2,1)} %bitcast.3), custom_call_target="tpu_custom_call" | custom-call | tf_op jit(solution)/shard_map/conduct/pallas_call | solution.py:35
  49.3 0.0 collective-permute-done.4.a_ref
  49.3 0.0 collective-permute-done.5.b_ref
  49.3 3.1 %cycles.1 = f32[4,2,32,128]{3,2,1,0:T(8,128)S(1)} custom-call(f32[4,4,32,128]{3,2,1,0:T(8,128)S(1)} %all-to-all-done.z_ref, f32[7,32,128]{2,1,0:T(8,128)S(1)} %get-tuple-element.33.c_ref, f32[128,128]{1,0:T(8,128)S(1)} %collective-permute-done.2.ca_ref, f32[128,128]{1,0:T(8,128)S(1)} %collective-permute-done.3.cb_ref, ...), custom_call_target="tpu_custom_call" | custom-call | tf_op jit(solution)/shard_map/cycles/pallas_call | solution.py:35
  52.4 10.8 %all_to_all.10.z_ref = f32[4,2,32,128]{3,2,1,0:T(8,128)S(1)} all-to-all(f32[4,2,32,128]{3,2,1,0:T(8,128)S(1)} %cycles.1), channel_id=1, replica_groups=mesh['sec'=4,'gx'=8,'gy'=16] {'sec'}, dimensions={0} | all-to-all | bytes 262144 | tf_op jit(solution)/shard_map/all_to_all | solution.py:512
  63.2 0.7 %finish.1 = (f32[2,32,256]{2,1,0:T(8,128)}, f32[32,256]{1,0:T(8,128)}) custom-call(f32[4,2,32,128]{3,2,1,0:T(8,128)S(1)} %all_to_all.10.z_ref), custom_call_target="tpu_custom_call" | custom-call | tf_op jit(solution)/shard_map/finish/pallas_call | solution.py:35
Async XLA Ops:
  1.8 4.4 %collective-permute-start = (f32[32,256]{1,0:T(8,128)S(1)}, f32[32,256]{1,0:T(8,128)S(1)}, u32[]{:S(2)}, u32[]{:S(2)}) collective-permute-start(f32[32,256]{1,0:T(8,128)S(1)} %get-tuple-element.22), channel_id=1, source_target_pairs={{0,1},{1,0},{2,3},{3,2},{4,5},{5,4},{6,7},{7,6},{8,9},{9,8},{10,11... | collective-permute-start | bytes 98312 | tf_op jit(solution)/shard_map/ppermute | solution.py:477
  3.7 6.4 %collective-permute-start.1 = (f32[32,256]{1,0:T(8,128)S(1)}, f32[32,256]{1,0:T(8,128)S(1)}, u32[]{:S(2)}, u32[]{:S(2)}) collective-permute-start(f32[32,256]{1,0:T(8,128)S(1)} %get-tuple-element.23), channel_id=1, source_target_pairs={{1,2},{2,1},{3,4},{4,3},{5,6},{6,5},{7,8},{8,7},{9,10},{10,9},{11,... | collective-permute-start | bytes 98312 | tf_op jit(solution)/shard_map/ppermute | solution.py:478
  12.2 20.7 %all-to-all-start = ((f32[4,4,32,128]{3,2,1,0:T(8,128)}), f32[4,4,32,128]{3,2,1,0:T(8,128)S(1)}, u32[]{:S(2)}, u32[]{:S(2)}) async-start(f32[4,4,32,128]{3,2,1,0:T(8,128)} %get-tuple-element.24), calls=%async_computation | async-start | bytes 524288 | tf_op jit(solution)/shard_map/all_to_all | solution.py:485
  19.5 13.0 %collective-permute-start.2 = (f32[128,128]{1,0:T(8,128)S(1)}, f32[128,128]{1,0:T(8,128)S(1)}, u32[]{:S(2)}, u32[]{:S(2)}) collective-permute-start(f32[128,128]{1,0:T(8,128)S(1)} %get-tuple-element.25), channel_id=1, source_target_pairs={{16,32},{32,16},{48,64},{64,48},{80,96},{96,80},{17,33},{33,17},{4... | collective-permute-start | bytes 196616 | tf_op jit(solution)/shard_map/ppermute | solution.py:487
  21.9 11.0 %collective-permute-start.3 = (f32[128,128]{1,0:T(8,128)S(1)}, f32[128,128]{1,0:T(8,128)S(1)}, u32[]{:S(2)}, u32[]{:S(2)}) collective-permute-start(f32[128,128]{1,0:T(8,128)S(1)} %get-tuple-element.26), channel_id=1, source_target_pairs={{0,16},{16,0},{32,48},{48,32},{64,80},{80,64},{96,112},{112,96},{1... | collective-permute-start | bytes 196616 | tf_op jit(solution)/shard_map/ppermute | solution.py:488
  33.1 16.2 %collective-permute-start.4 = (f32[192,128]{1,0:T(8,128)S(1)}, f32[192,128]{1,0:T(8,128)S(1)}, u32[]{:S(2)}, u32[]{:S(2)}) collective-permute-start(f32[192,128]{1,0:T(8,128)S(1)} %get-tuple-element.36), channel_id=1, source_target_pairs={{16,32},{32,16},{48,64},{64,48},{80,96},{96,80},{17,33},{33,17},{4... | collective-permute-start | bytes 294920 | tf_op jit(solution)/shard_map/ppermute | solution.py:504
  35.0 14.3 %collective-permute-start.5 = (f32[192,128]{1,0:T(8,128)S(1)}, f32[192,128]{1,0:T(8,128)S(1)}, u32[]{:S(2)}, u32[]{:S(2)}) collective-permute-start(f32[192,128]{1,0:T(8,128)S(1)} %get-tuple-element.37), channel_id=1, source_target_pairs={{0,16},{16,0},{32,48},{48,32},{64,80},{80,64},{96,112},{112,96},{1... | collective-permute-start | bytes 294920 | tf_op jit(solution)/shard_map/ppermute | solution.py:505

commit v4 on v3

--- a/solution.py
+++ b/solution.py
@@ -122,46 +122,69 @@
 
 
 def slice_kernel(
-    soil, geo, land, river, elev, rough, rain, evap, head, press, stor, a_ref, b_ref,
-    z_ref, c_ref, ca_ref, cb_ref, work_ref,
+    soil, geo, land, river, elev, rough, rain, evap, head, press, stor, z_ref, c_ref, work_ref
 ):
-    odd = lax.axis_index("gy") % 2 == 1
     plain, classes = columns(
         soil[...], geo[...], land[...], river[...], elev[...], rough[...], rain[...], evap[...], head[...]
     )
     plain = [press[0], press[1], stor[0], stor[1]] + plain
     rows, width = plain[0].shape
+    lane = lax.broadcasted_iota(jnp.int32, (rows, LANES), 1)
+
+    def slices(value):
+        first, last = value[:, :LANES], value[:, width - LANES :]
+        low_r, high_r = pltpu.roll(first, EDGE, 1), pltpu.roll(last, EDGE, 1)
+        low_l, high_l = pltpu.roll(first, LANES - EDGE, 1), pltpu.roll(last, LANES - EDGE, 1)
+        return [
+            jnp.where(lane < EDGE, 0.0, low_r),
+            jnp.where(lane < LANES - EDGE, low_l, high_l),
+            jnp.where(lane < EDGE, low_r, high_r),
+            jnp.where(lane < LANES - EDGE, high_l, 0.0),
+        ]
+
+    for i in range(4):
+        for d, part in enumerate(slices(plain[i])):
+            z_ref[d, i] = part
+    for j, value in enumerate(plain[4:] + classes):
+        for d, part in enumerate(slices(value)):
+            work_ref[d, j] = part
+    c_ref[...] = work_ref[lax.axis_index("sec")]
+
+
+def halo_kernel(z_in, c_in, a_ref, b_ref, z_ref, c_ref, ca_ref, cb_ref):
+    odd = lax.axis_index("gy") % 2 == 1
+    sec = lax.axis_index("sec")
+    rows = c_in.shape[1]
     lane = lax.broadcasted_iota(jnp.int32, (rows, LANES), 1)
     got_a, got_b = a_ref[...], b_ref[...]
     left = jnp.where(odd, got_a, got_b)
     right = jnp.where(odd, got_b, got_a)
 
-    def slices(value, half, at, wide):
+    def halos(half, at, wide):
         cols = slice(half * LANES, (half + 1) * LANES)
         lo, hi = left[:, cols], right[:, cols]
         move = (EDGE - wide - at) % LANES
         lo = pltpu.roll(lo, move, 1) if move else lo
         move = (LANES - EDGE - at) % LANES
         hi = pltpu.roll(hi, move, 1) if move else hi
-        first, last = value[:, :LANES], value[:, width - LANES :]
-        low_r, high_r = pltpu.roll(first, EDGE, 1), pltpu.roll(last, EDGE, 1)
-        low_l, high_l = pltpu.roll(first, LANES - EDGE, 1), pltpu.roll(last, LANES - EDGE, 1)
-        zero = jnp.zeros_like(lo)
-        return [
-            jnp.where(lane < EDGE, jnp.where(lane >= EDGE - wide, lo, zero), low_r),
-            jnp.where(lane < LANES - EDGE, low_l, high_l),
-            jnp.where(lane < EDGE, low_r, high_r),
-            jnp.where(lane < LANES - EDGE, high_l, jnp.where(lane < LANES - EDGE + wide, hi, zero)),
-        ]
-
+        return (
+            jnp.where((lane >= EDGE - wide) & (lane < EDGE), lo, 0.0),
+            jnp.where((lane >= LANES - EDGE) & (lane < LANES - EDGE + wide), hi, 0.0),
+        )
+
+    inner_l, inner_r = lane >= EDGE, lane < LANES - EDGE
     for i in range(4):
-        for d, part in enumerate(slices(plain[i], 0, 16 * i, 16)):
-            z_ref[d, i] = part
+        lo, hi = halos(0, 16 * i, 16)
+        z_ref[0, i] = jnp.where(inner_l, z_in[0, i], lo)
+        z_ref[1, i] = z_in[1, i]
+        z_ref[2, i] = z_in[2, i]
+        z_ref[3, i] = jnp.where(inner_r, z_in[3, i], hi)
     spots = [(0, 16 * i, 16) for i in range(4, 8)] + [(1, 0, 16), (1, 32, 32), (1, 64, 32)]
-    for j, (value, (half, at, wide)) in enumerate(zip(plain[4:] + classes, spots)):
-        for d, part in enumerate(slices(value, half, at, wide)):
-            work_ref[d, j] = part
-    c_ref[...] = work_ref[lax.axis_index("sec")]
+    for j, spot in enumerate(spots):
+        lo, hi = halos(*spot)
+        value = c_in[j]
+        value = jnp.where(inner_l | (sec != 0), value, lo)
+        c_ref[j] = jnp.where(inner_r | (sec != 3), value, hi)
     odd_x = lax.axis_index("gx") % 2 == 1
     low = jnp.where(odd_x, rows - HALO, 0)
     low_class = jnp.where(odd_x, rows - CROWS, 0)
@@ -209,7 +232,6 @@
 STEP_S = 8
 TRIPS_S = 1
 BLOCK_K = 16
-UNROLL_C = 8
 
 
 def at_row(r):
@@ -269,13 +291,13 @@
     return jnp.concatenate(pairs, axis=0)
 
 
-def conduct_rows(shift_ref, at, table, proj):
-    hot = jnp.concatenate([one_hot(shift_ref, at), one_hot(shift_ref, at + 1)], axis=1)
+def conduct_rows(shift_ref, at, count, table, proj):
+    hot = jnp.concatenate([one_hot(shift_ref, at + k) for k in range(count)], axis=1)
     both = jnp.dot(table, hot, preferred_element_type=f32)
     hidden = jnp.maximum(both[:LANES] + both[LANES:], 0.0).astype(bf16)
     value = jnp.exp(jnp.dot(proj, hidden, preferred_element_type=f32))
     out = []
-    for k in range(2):
+    for k in range(count):
         inside = jnp.broadcast_to(shift_ref[1, pl.ds(at + k, 1), :], (8, LANES)) >= 0.0
         out.append(jnp.where(inside, value[:, k * LANES : (k + 1) * LANES], 0.0))
     return out
@@ -296,12 +318,9 @@
         shift_classes(shift_ref, kind, value)
     table, proj = table_ref[...], proj_ref[...]
 
-    def step(i, carry):
-        for k, value in enumerate(conduct_rows(shift_ref, 2 * i + CROWS - HALO, table, proj)):
-            cond_ref[at_row(2 * i + k), :] = value
-        return carry
-
-    lax.fori_loop(0, full // 2, step, 0, unroll=UNROLL_C)
+    for row in range(0, full, full // 2):
+        for k, value in enumerate(conduct_rows(shift_ref, row + CROWS - HALO, full // 2, table, proj)):
+            cond_ref[at_row(row + k), :] = value
     cond_ref[0:8, :] = jnp.zeros((8, LANES), f32)
     cond_ref[8 * (full + 1) :, :] = jnp.zeros((8, LANES), f32)
 
@@ -473,20 +492,33 @@
     given = tuple(range(len(raw)))
 
     edge = sds((rows, 2 * LANES), f32)
+    chunks, plane = sds((4, 4, rows, LANES), f32), sds((7, rows, LANES), f32)
     ya, yb = call(pack_cols_kernel, (edge, edge), raw, name="pack_cols", hbm=given)
+    ya, yb, head = lax.optimization_barrier((ya, yb, surface_head))
     ya = lax.ppermute(ya, "gy", swap_pairs(n_gy, 0))
     yb = lax.ppermute(yb, "gy", swap_pairs(n_gy, 1))
 
-    plane, edge_2d = sds((7, rows, LANES), f32), sds((MSG_ROWS_2D, LANES), f32)
+    z, cols = call(
+        slice_kernel, (chunks, plane), (*raw[:8], head, *raw[9:]),
+        scratch=[pltpu.VMEM((4, 7, rows, LANES), f32)], name="slices", hbm=given,
+    )
+    ya, yb, z, cols = lax.optimization_barrier((ya, yb, z, cols))
+    edge_2d = sds((MSG_ROWS_2D, LANES), f32)
     z, cols, ca, cb = call(
-        slice_kernel, (sds((4, 4, rows, LANES), f32), plane, edge_2d, edge_2d), (*raw, ya, yb),
-        scratch=[pltpu.VMEM((4, 7, rows, LANES), f32)], name="slices", hbm=given,
+        halo_kernel, (chunks, plane, edge_2d, edge_2d), (z, cols, ya, yb), name="halo"
     )
     z = lax.all_to_all(z, "sec", 0, 0)
 
     ca = lax.ppermute(ca, "gx", swap_pairs(n_gx, 1))
     cb = lax.ppermute(cb, "gx", swap_pairs(n_gx, 0))
-    cols, soil_embed = lax.optimization_barrier((cols, soil_embed))
+    z, ca, cb = lax.optimization_barrier((z, ca, cb))
+
+    msg = sds((MSG_ROWS, LANES), f32)
+    xa, xb = call(pack_rows_kernel, (msg, msg), (z,), name="pack_rows")
+    xa, xb, cols, soil_embed = lax.optimization_barrier((xa, xb, cols, soil_embed))
+    xa = lax.ppermute(xa, "gx", swap_pairs(n_gx, 1))
+    xb = lax.ppermute(xb, "gx", swap_pairs(n_gx, 0))
+
     sel, tap = table_layout()
     (table,) = call(
         table_kernel, (sds((2 * LANES, KROWS), bf16),),
@@ -496,13 +528,6 @@
         ),
         name="table", hbm=range(5),
     )
-    z, ca, cb, table = lax.optimization_barrier((z, ca, cb, table))
-
-    msg = sds((MSG_ROWS, LANES), f32)
-    xa, xb = call(pack_rows_kernel, (msg, msg), (z,), name="pack_rows")
-    xa, xb, cols = lax.optimization_barrier((xa, xb, cols))
-    xa = lax.ppermute(xa, "gx", swap_pairs(n_gx, 1))
-    xb = lax.ppermute(xb, "gx", swap_pairs(n_gx, 0))
     (cond,) = call(
         conduct_kernel, (sds((8 * (rows + 2 * HALO + 2), LANES), f32),), (cols, ca, cb, table, out_weight.T),
         scratch=[pltpu.VMEM((6, rows + 2 * CROWS, LANES), f32)], name="conduct", hbm=(4,),

time: 64.4 us -> 61 us (0.947)
  Pallas kernels: 15 us -> 11.2 us
    pallas_call x7 -> x8, Pallas kernels: 15 us -> 11.2 us  [call(): pl.pallas_call(kernel, out_shape=made, in_specs=[VMEM] * len(args), out_s...]
    ppermute x1, waiting for transfers between devices: 0.5 us -> 2.22 us  [shards(): cb = lax.ppermute(cb, 'gx', swap_pairs(n_gx, 0))]
    ppermute x1, waiting for transfers between devices: 3.97 us -> 2.67 us  [shards(): yb = lax.ppermute(yb, 'gy', swap_pairs(n_gy, 1))]
  transfers between devices with their start and end apart: 7 -> 7, of which waited for: 2 -> 2; matrix products, arithmetic and copies ran while one was open for 0% -> 0% of each run, Pallas kernels for 12% -> 9%
where the time goes in v4:
time: 61 us; the launch traced here: 60.5 us
  starting transfers between devices  32.8 us (54%)
  Pallas kernels  11.2 us (18%)
  blocking collectives  10.8 us (18%)
  waiting for transfers between devices  4.9 us (8%)
  between operations  0.75 us (1%)
    pallas_call x8, Pallas kernels, call(): pl.pallas_call(kernel, out_shape=made, in_specs=[VMEM] * len(args), out_s...  11.2 us
    all_to_all x1, blocking collectives, shards(): out = lax.all_to_all(out, 'sec', 0, 0)  10.8 us
    ppermute x1, starting transfers between devices, shards(): cb = lax.ppermute(cb, 'gx', swap_pairs(n_gx, 0))  8.8 us
    ppermute x1, starting transfers between devices, shards(): xb = lax.ppermute(xb, 'gx', swap_pairs(n_gx, 0))  8.03 us
    all_to_all x1, starting transfers between devices, shards(): z = lax.all_to_all(z, 'sec', 0, 0)  7.26 us
    ppermute x1, waiting for transfers between devices, shards(): yb = lax.ppermute(yb, 'gy', swap_pairs(n_gy, 1))  2.67 us
    ppermute x1, starting transfers between devices, shards(): yb = lax.ppermute(yb, 'gy', swap_pairs(n_gy, 1))  2.46 us
    ppermute x1, starting transfers between devices, shards(): ca = lax.ppermute(ca, 'gx', swap_pairs(n_gx, 1))  2.43 us
  transfers between devices with their start and end apart: 7, of which 2 were waited for; matrix products, arithmetic and copies ran while one was open for 0% of the time, Pallas kernels for 9%

profile of v4, /device:TPU:36, one launch (start us, length us, event | category | flops | bytes accessed | tf_op | source)
XLA Modules:
  0.0 60.5 jit_solution(5539034424805579752)
XLA Ops:
  0.6 1.2 %pack_cols.1 = (f32[32,256]{1,0:T(8,128)S(1)}, f32[32,256]{1,0:T(8,128)S(1)}) custom-call(s32[32,256]{1,0:T(8,128)} %soil.3, s32[32,256]{1,0:T(8,128)} %geo.3, s32[32,256]{1,0:T(8,128)} %land.3, s32[32,256]{1,0:T(8,128)} %river.3, f32[32,256]{1,0:T(8,128)} %elev.3, f32[32,256]{1,0:T(8,128)} %rough.3, f32[32,256]{1,0:T(8,128)} %rain.3, f32[32,256]{1,0:T(8,128)} %evap.3, ...), custom_call_target="tpu_custom_call" | custom-call | tf_op jit(solution)/shard_map/pack_cols/pallas_call | solution.py:35
  1.8 1.9 %collective-permute-start = (f32[32,256]{1,0:T(8,128)S(1)}, f32[32,256]{1,0:T(8,128)S(1)}, u32[]{:S(2)}, u32[]{:S(2)}) collective-permute-start(f32[32,256]{1,0:T(8,128)S(1)} %get-tuple-element.31), channel_id=1, source_target_pairs={{0,1},{1,0},{2,3},{3,2},{4,5},{5,4},{6,7},{7,6},{8,9},{9,8},{10,11... | collective-permute-start | bytes 98312 | tf_op jit(solution)/shard_map/ppermute | solution.py:498
  3.7 2.5 %collective-permute-start.1 = (f32[32,256]{1,0:T(8,128)S(1)}, f32[32,256]{1,0:T(8,128)S(1)}, u32[]{:S(2)}, u32[]{:S(2)}) collective-permute-start(f32[32,256]{1,0:T(8,128)S(1)} %get-tuple-element.32), channel_id=1, source_target_pairs={{1,2},{2,1},{3,4},{4,3},{5,6},{6,5},{7,8},{8,7},{9,10},{10,9},{11,... | collective-permute-start | bytes 98312 | tf_op jit(solution)/shard_map/ppermute | solution.py:499
  6.2 1.3 %slices.1 = (f32[4,4,32,128]{3,2,1,0:T(8,128)S(1)}, f32[7,32,128]{2,1,0:T(8,128)S(1)}) custom-call(s32[32,256]{1,0:T(8,128)} %soil.3, s32[32,256]{1,0:T(8,128)} %geo.3, s32[32,256]{1,0:T(8,128)} %land.3, s32[32,256]{1,0:T(8,128)} %river.3, f32[32,256]{1,0:T(8,128)} %elev.3, f32[32,256]{1,0:T(8,128)} %rough.3, f32[32,256]{1,0:T(8,128)} %rain.3, ...), custom_call_target="tpu_custom_call" | custom-call | tf_op jit(solution)/shard_map/slices/pallas_call | solution.py:35
  7.5 0.0 collective-permute-done.a_ref
  7.5 2.7 %collective-permute-done.1.b_ref = f32[32,256]{1,0:T(8,128)S(1)} collective-permute-done((f32[32,256]{1,0:T(8,128)S(1)}, f32[32,256]{1,0:T(8,128)S(1)}, u32[]{:S(2)}, u32[]{:S(2)}) %collective-permute-start.1) | collective-permute-done | bytes 32800 | tf_op jit(solution)/shard_map/ppermute | solution.py:499
  10.2 0.8 %halo.1 = (f32[4,4,32,128]{3,2,1,0:T(8,128)}, f32[7,32,128]{2,1,0:T(8,128)S(1)}, f32[128,128]{1,0:T(8,128)S(1)}, f32[128,128]{1,0:T(8,128)S(1)}) custom-call(f32[4,4,32,128]{3,2,1,0:T(8,128)S(1)} %get-tuple-element.36.z_in, f32[7,32,128]{2,1,0:T(8,128)S(1)} %get-tuple-element.37.c_in, f32[32,256]{1,0:T(8,128)S(1)} %collective-permute-done.a_ref, ...), custom_call_target="tpu_custom_call" | custom-call | tf_op jit(solution)/shard_map/halo/pallas_call | solution.py:35
  11.0 7.3 %all-to-all-start = ((f32[4,4,32,128]{3,2,1,0:T(8,128)}), f32[4,4,32,128]{3,2,1,0:T(8,128)S(1)}, u32[]{:S(2)}, u32[]{:S(2)}) async-start(f32[4,4,32,128]{3,2,1,0:T(8,128)} %get-tuple-element.40), calls=%async_computation | async-start | bytes 524288 | tf_op jit(solution)/shard_map/all_to_all | solution.py:510
  18.3 2.4 %collective-permute-start.2 = (f32[128,128]{1,0:T(8,128)S(1)}, f32[128,128]{1,0:T(8,128)S(1)}, u32[]{:S(2)}, u32[]{:S(2)}) collective-permute-start(f32[128,128]{1,0:T(8,128)S(1)} %get-tuple-element.41), channel_id=1, source_target_pairs={{16,32},{32,16},{48,64},{64,48},{80,96},{96,80},{17,33},{33,17},{4... | collective-permute-start | bytes 196616 | tf_op jit(solution)/shard_map/ppermute | solution.py:512
  20.7 8.8 %collective-permute-start.3 = (f32[128,128]{1,0:T(8,128)S(1)}, f32[128,128]{1,0:T(8,128)S(1)}, u32[]{:S(2)}, u32[]{:S(2)}) collective-permute-start(f32[128,128]{1,0:T(8,128)S(1)} %get-tuple-element.42), channel_id=1, source_target_pairs={{0,16},{16,0},{32,48},{48,32},{64,80},{80,64},{96,112},{112,96},{1... | collective-permute-start | bytes 196616 | tf_op jit(solution)/shard_map/ppermute | solution.py:513
  29.5 0.0 collective-permute-done.2.ca_ref
  29.5 2.2 %collective-permute-done.3.cb_ref = f32[128,128]{1,0:T(8,128)S(1)} collective-permute-done((f32[128,128]{1,0:T(8,128)S(1)}, f32[128,128]{1,0:T(8,128)S(1)}, u32[]{:S(2)}, u32[]{:S(2)}) %collective-permute-start.3) | collective-permute-done | bytes 65568 | tf_op jit(solution)/shard_map/ppermute | solution.py:513
  31.7 0.0 all-to-all-done.z_ref
  31.7 0.1 pack_rows.1
  31.9 1.9 %collective-permute-start.4 = (f32[192,128]{1,0:T(8,128)S(1)}, f32[192,128]{1,0:T(8,128)S(1)}, u32[]{:S(2)}, u32[]{:S(2)}) collective-permute-start(f32[192,128]{1,0:T(8,128)S(1)} %get-tuple-element.50), channel_id=1, source_target_pairs={{16,32},{32,16},{48,64},{64,48},{80,96},{96,80},{17,33},{33,17},{4... | collective-permute-start | bytes 294920 | tf_op jit(solution)/shard_map/ppermute | solution.py:519
  33.8 8.0 %collective-permute-start.5 = (f32[192,128]{1,0:T(8,128)S(1)}, f32[192,128]{1,0:T(8,128)S(1)}, u32[]{:S(2)}, u32[]{:S(2)}) collective-permute-start(f32[192,128]{1,0:T(8,128)S(1)} %get-tuple-element.51), channel_id=1, source_target_pairs={{0,16},{16,0},{32,48},{48,32},{64,80},{80,64},{96,112},{112,96},{1... | collective-permute-start | bytes 294920 | tf_op jit(solution)/shard_map/ppermute | solution.py:520
  41.8 1.7 %table.1.table_ref = bf16[256,256]{1,0:T(8,128)(2,1)S(1)} custom-call(f32[256,28]{1,0:T(8,128)} %constant.4.clone.sel_ref, s32[256,128]{1,0:T(8,128)} %constant.5.clone.tap_ref, bf16[12,128]{1,0:T(8,128)(2,1)} %soil_ref, bf16[16,128]{1,0:T(8,128)(2,1)} %geo_ref.1, bf16[9,128,128]{2,1,0:T(8,128)(2,1)} %bitcast.2), custom_call_target="tpu_custom_call" | custom-call | tf_op jit(solution)/shard_map/table/pallas_call | solution.py:35
  43.5 2.4 %conduct.1.cond_ref = f32[528,128]{1,0:T(8,128)S(1)} custom-call(f32[7,32,128]{2,1,0:T(8,128)S(1)} %get-tuple-element.47.c_ref, f32[128,128]{1,0:T(8,128)S(1)} %collective-permute-done.2.ca_ref, f32[128,128]{1,0:T(8,128)S(1)} %collective-permute-done.3.cb_ref, bf16[256,256]{1,0:T(8,128)(2,1)S(1)} %table.1.table_ref, bf16[8,128]{1,0:T(8,128)(2,1)} %bitcast.3), custom_call_target="tpu_custom_call" | custom-call | tf_op jit(solution)/shard_map/conduct/pallas_call | solution.py:35
  45.9 0.0 collective-permute-done.4.a_ref
  45.9 0.0 collective-permute-done.5.b_ref
  45.9 3.1 %cycles.1 = f32[4,2,32,128]{3,2,1,0:T(8,128)S(1)} custom-call(f32[4,4,32,128]{3,2,1,0:T(8,128)S(1)} %all-to-all-done.z_ref, f32[7,32,128]{2,1,0:T(8,128)S(1)} %get-tuple-element.47.c_ref, f32[128,128]{1,0:T(8,128)S(1)} %collective-permute-done.2.ca_ref, f32[128,128]{1,0:T(8,128)S(1)} %collective-permute-done.3.cb_ref, ...), custom_call_target="tpu_custom_call" | custom-call | tf_op jit(solution)/shard_map/cycles/pallas_call | solution.py:35
  49.0 10.8 %all_to_all.10.z_ref = f32[4,2,32,128]{3,2,1,0:T(8,128)S(1)} all-to-all(f32[4,2,32,128]{3,2,1,0:T(8,128)S(1)} %cycles.1), channel_id=1, replica_groups=mesh['sec'=4,'gx'=8,'gy'=16] {'sec'}, dimensions={0} | all-to-all | bytes 262144 | tf_op jit(solution)/shard_map/all_to_all | solution.py:537
  59.8 0.7 %finish.1 = (f32[2,32,256]{2,1,0:T(8,128)}, f32[32,256]{1,0:T(8,128)}) custom-call(f32[4,2,32,128]{3,2,1,0:T(8,128)S(1)} %all_to_all.10.z_ref), custom_call_target="tpu_custom_call" | custom-call | tf_op jit(solution)/shard_map/finish/pallas_call | solution.py:35
Async XLA Ops:
  1.8 5.7 %collective-permute-start = (f32[32,256]{1,0:T(8,128)S(1)}, f32[32,256]{1,0:T(8,128)S(1)}, u32[]{:S(2)}, u32[]{:S(2)}) collective-permute-start(f32[32,256]{1,0:T(8,128)S(1)} %get-tuple-element.31), channel_id=1, source_target_pairs={{0,1},{1,0},{2,3},{3,2},{4,5},{5,4},{6,7},{7,6},{8,9},{9,8},{10,11... | collective-permute-start | bytes 98312 | tf_op jit(solution)/shard_map/ppermute | solution.py:498
  3.7 6.4 %collective-permute-start.1 = (f32[32,256]{1,0:T(8,128)S(1)}, f32[32,256]{1,0:T(8,128)S(1)}, u32[]{:S(2)}, u32[]{:S(2)}) collective-permute-start(f32[32,256]{1,0:T(8,128)S(1)} %get-tuple-element.32), channel_id=1, source_target_pairs={{1,2},{2,1},{3,4},{4,3},{5,6},{6,5},{7,8},{8,7},{9,10},{10,9},{11,... | collective-permute-start | bytes 98312 | tf_op jit(solution)/shard_map/ppermute | solution.py:499
  11.0 20.7 %all-to-all-start = ((f32[4,4,32,128]{3,2,1,0:T(8,128)}), f32[4,4,32,128]{3,2,1,0:T(8,128)S(1)}, u32[]{:S(2)}, u32[]{:S(2)}) async-start(f32[4,4,32,128]{3,2,1,0:T(8,128)} %get-tuple-element.40), calls=%async_computation | async-start | bytes 524288 | tf_op jit(solution)/shard_map/all_to_all | solution.py:510
  18.3 11.2 %collective-permute-start.2 = (f32[128,128]{1,0:T(8,128)S(1)}, f32[128,128]{1,0:T(8,128)S(1)}, u32[]{:S(2)}, u32[]{:S(2)}) collective-permute-start(f32[128,128]{1,0:T(8,128)S(1)} %get-tuple-element.41), channel_id=1, source_target_pairs={{16,32},{32,16},{48,64},{64,48},{80,96},{96,80},{17,33},{33,17},{4... | collective-permute-start | bytes 196616 | tf_op jit(solution)/shard_map/ppermute | solution.py:512
  20.7 11.0 %collective-permute-start.3 = (f32[128,128]{1,0:T(8,128)S(1)}, f32[128,128]{1,0:T(8,128)S(1)}, u32[]{:S(2)}, u32[]{:S(2)}) collective-permute-start(f32[128,128]{1,0:T(8,128)S(1)} %get-tuple-element.42), channel_id=1, source_target_pairs={{0,16},{16,0},{32,48},{48,32},{64,80},{80,64},{96,112},{112,96},{1... | collective-permute-start | bytes 196616 | tf_op jit(solution)/shard_map/ppermute | solution.py:513
  31.9 14.0 %collective-permute-start.4 = (f32[192,128]{1,0:T(8,128)S(1)}, f32[192,128]{1,0:T(8,128)S(1)}, u32[]{:S(2)}, u32[]{:S(2)}) collective-permute-start(f32[192,128]{1,0:T(8,128)S(1)} %get-tuple-element.50), channel_id=1, source_target_pairs={{16,32},{32,16},{48,64},{64,48},{80,96},{96,80},{17,33},{33,17},{4... | collective-permute-start | bytes 294920 | tf_op jit(solution)/shard_map/ppermute | solution.py:519
  33.8 12.1 %collective-permute-start.5 = (f32[192,128]{1,0:T(8,128)S(1)}, f32[192,128]{1,0:T(8,128)S(1)}, u32[]{:S(2)}, u32[]{:S(2)}) collective-permute-start(f32[192,128]{1,0:T(8,128)S(1)} %get-tuple-element.51), channel_id=1, source_target_pairs={{0,16},{16,0},{32,48},{48,32},{64,80},{80,64},{96,112},{112,96},{1... | collective-permute-start | bytes 294920 | tf_op jit(solution)/shard_map/ppermute | solution.py:520

commit v5 on v4

--- a/solution.py
+++ b/solution.py
@@ -1,5 +1,3 @@
-import functools
-
 import jax
 import jax.numpy as jnp
 import numpy as np
@@ -7,6 +5,7 @@
 from jax.experimental import pallas as pl
 from jax.experimental.pallas import tpu as pltpu
 from jax.sharding import PartitionSpec as P
+
 
 SWEEPS = 4
 CYCLES = 4
@@ -29,16 +28,11 @@
 bf16 = jnp.bfloat16
 
 
-def call(kernel, outs, args, scratch=(), name=None, hbm=(), final=False):
+def call(kernel, outs, args, scratch=(), hbm=(), final=False):
     made = outs if final else tuple(pltpu.VMEM(o.shape, o.dtype) for o in outs)
     args = [x if i in hbm else pltpu.with_memory_space_constraint(x, pltpu.VMEM) for i, x in enumerate(args)]
     return pl.pallas_call(
-        kernel,
-        out_shape=made,
-        in_specs=[VMEM] * len(args),
-        out_specs=tuple(VMEM for _ in outs),
-        scratch_shapes=scratch,
-        name=name,
+        kernel, out_shape=made, in_specs=[VMEM] * len(args), out_specs=tuple(VMEM for _ in outs), scratch_shapes=scratch
     )(*args)
 
 
@@ -238,11 +232,7 @@
     return pl.ds(pl.multiple_of(8 * r + 8, 8), 8)
 
 
-def place(ref, r):
-    return ref.at[at_row(r), :]
-
-
-def beside(ref, mid, r, step):
+def beside(mid, step):
     return pltpu.roll(mid, (-step) % 8, 0)
 
 
@@ -427,7 +417,7 @@
                     rhs_ref[here, :] = rhs
                 else:
                     rhs = rhs_ref[here, :]
-                column = coef_ref[0, here, :] * beside(old, mid, r, -1) + coef_ref[1, here, :] * beside(old, mid, r, 1)
+                column = coef_ref[0, here, :] * beside(mid, -1) + coef_ref[1, here, :] * beside(mid, 1)
                 across = coef_ref[2, here, :] * old[at_row(r - 1), :] + coef_ref[3, here, :] * old[at_row(r + 1), :]
                 along = coef_ref[4, here, :] * pltpu.roll(mid, LANES - 1, 1) + coef_ref[5, here, :] * pltpu.roll(mid, 1, 1)
                 new[at_row(r), :] = (rhs + column) + (across + along)
@@ -474,7 +464,6 @@
             pltpu.VMEM((5, full, LANES), f32),
             pltpu.VMEM((full, LANES), f32),
         ],
-        name="cycles",
     )[0]
 
 
@@ -493,28 +482,25 @@
 
     edge = sds((rows, 2 * LANES), f32)
     chunks, plane = sds((4, 4, rows, LANES), f32), sds((7, rows, LANES), f32)
-    ya, yb = call(pack_cols_kernel, (edge, edge), raw, name="pack_cols", hbm=given)
+    ya, yb = call(pack_cols_kernel, (edge, edge), raw, hbm=given)
     ya, yb, head = lax.optimization_barrier((ya, yb, surface_head))
     ya = lax.ppermute(ya, "gy", swap_pairs(n_gy, 0))
     yb = lax.ppermute(yb, "gy", swap_pairs(n_gy, 1))
 
     z, cols = call(
         slice_kernel, (chunks, plane), (*raw[:8], head, *raw[9:]),
-        scratch=[pltpu.VMEM((4, 7, rows, LANES), f32)], name="slices", hbm=given,
+        scratch=[pltpu.VMEM((4, 7, rows, LANES), f32)], hbm=given,
     )
     ya, yb, z, cols = lax.optimization_barrier((ya, yb, z, cols))
     edge_2d = sds((MSG_ROWS_2D, LANES), f32)
-    z, cols, ca, cb = call(
-        halo_kernel, (chunks, plane, edge_2d, edge_2d), (z, cols, ya, yb), name="halo"
-    )
+    z, cols, ca, cb = call(halo_kernel, (chunks, plane, edge_2d, edge_2d), (z, cols, ya, yb))
     z = lax.all_to_all(z, "sec", 0, 0)
 
+    cb = lax.ppermute(cb, "gx", swap_pairs(n_gx, 0))
     ca = lax.ppermute(ca, "gx", swap_pairs(n_gx, 1))
-    cb = lax.ppermute(cb, "gx", swap_pairs(n_gx, 0))
-    z, ca, cb = lax.optimization_barrier((z, ca, cb))
 
     msg = sds((MSG_ROWS, LANES), f32)
-    xa, xb = call(pack_rows_kernel, (msg, msg), (z,), name="pack_rows")
+    xa, xb = call(pack_rows_kernel, (msg, msg), (z,))
     xa, xb, cols, soil_embed = lax.optimization_barrier((xa, xb, cols, soil_embed))
     xa = lax.ppermute(xa, "gx", swap_pairs(n_gx, 1))
     xb = lax.ppermute(xb, "gx", swap_pairs(n_gx, 0))
@@ -526,16 +512,16 @@
             jnp.asarray(sel), jnp.asarray(tap), soil_embed, geology_embed,
             conv_weight.reshape(9, LANES, LANES),
         ),
-        name="table", hbm=range(5),
+        hbm=range(5),
     )
     (cond,) = call(
         conduct_kernel, (sds((8 * (rows + 2 * HALO + 2), LANES), f32),), (cols, ca, cb, table, out_weight.T),
-        scratch=[pltpu.VMEM((6, rows + 2 * CROWS, LANES), f32)], name="conduct", hbm=(4,),
+        scratch=[pltpu.VMEM((6, rows + 2 * CROWS, LANES), f32)], hbm=(4,),
     )
     xa, xb, cond = lax.optimization_barrier((xa, xb, cond))
     out = main_call(rows, (z, cols, ca, cb, xa, xb, cond))
     out = lax.all_to_all(out, "sec", 0, 0)
-    return call(finish_kernel, (sds(pressure.shape, f32), sds((rows, width), f32)), (out,), name="finish", final=True)
+    return call(finish_kernel, (sds(pressure.shape, f32), sds((rows, width), f32)), (out,), final=True)
 
 
 def solution(mesh):

time: 61 us -> 63.6 us (1.043)
  the two profiles are of different devices: /device:TPU:36 before, /device:TPU:30 now
where the time goes in v5:
time: 63.6 us; the launch traced here: 63.1 us
  blocking collectives  25.4 us (40%)
  starting transfers between devices  21.2 us (33%)
  Pallas kernels  10.6 us (17%)
  waiting for transfers between devices  5.11 us (8%)
  between operations  0.75 us (1%)
    all_to_all x1, blocking collectives, shards(): z = lax.all_to_all(z, 'sec', 0, 0)  16.9 us
    pallas_call x8, Pallas kernels, call(): pl.pallas_call(kernel, out_shape=made, in_specs=[VMEM] * len(args), out_s...  10.6 us
    all_to_all x1, blocking collectives, shards(): out = lax.all_to_all(out, 'sec', 0, 0)  8.56 us
    ppermute x1, starting transfers between devices, shards(): xa = lax.ppermute(xa, 'gx', swap_pairs(n_gx, 1))  8.13 us
    ppermute x1, starting transfers between devices, shards(): ca = lax.ppermute(ca, 'gx', swap_pairs(n_gx, 1))  4.88 us
    ppermute x1, waiting for transfers between devices, shards(): ca = lax.ppermute(ca, 'gx', swap_pairs(n_gx, 1))  3.64 us
    ppermute x1, starting transfers between devices, shards(): yb = lax.ppermute(yb, 'gy', swap_pairs(n_gy, 1))  2.46 us
    ppermute x1, starting transfers between devices, shards(): ya = lax.ppermute(ya, 'gy', swap_pairs(n_gy, 0))  1.92 us
  transfers between devices with their start and end apart: 6, of which 2 were waited for; matrix products, arithmetic and copies ran while one was open for 0% of the time, Pallas kernels for 8%

profile of v5, /device:TPU:30, one launch (start us, length us, event | category | flops | bytes accessed | tf_op | source)
XLA Modules:
  0.0 63.1 jit_solution(1807885470897530036)
XLA Ops:
  0.6 1.2 %shard_map.176 = (f32[32,256]{1,0:T(8,128)S(1)}, f32[32,256]{1,0:T(8,128)S(1)}) custom-call(s32[32,256]{1,0:T(8,128)} %soil.3, s32[32,256]{1,0:T(8,128)} %geo.3, s32[32,256]{1,0:T(8,128)} %land.3, s32[32,256]{1,0:T(8,128)} %river.3, f32[32,256]{1,0:T(8,128)} %elev.3, f32[32,256]{1,0:T(8,128)} %rough.3, f32[32,256]{1,0:T(8,128)} %rain.3, f32[32,256]{1,0:T(8,128)} %evap.3, ...), custom_call_target="tpu_custom_call" | custom-call | tf_op jit(solution)/shard_map/pallas_call | solution.py:34
  1.8 1.9 %collective-permute-start = (f32[32,256]{1,0:T(8,128)S(1)}, f32[32,256]{1,0:T(8,128)S(1)}, u32[]{:S(2)}, u32[]{:S(2)}) collective-permute-start(f32[32,256]{1,0:T(8,128)S(1)} %get-tuple-element.28), channel_id=1, source_target_pairs={{0,1},{1,0},{2,3},{3,2},{4,5},{5,4},{6,7},{7,6},{8,9},{9,8},{10,11... | collective-permute-start | bytes 98312 | tf_op jit(solution)/shard_map/ppermute | solution.py:487
  3.7 2.5 %collective-permute-start.1 = (f32[32,256]{1,0:T(8,128)S(1)}, f32[32,256]{1,0:T(8,128)S(1)}, u32[]{:S(2)}, u32[]{:S(2)}) collective-permute-start(f32[32,256]{1,0:T(8,128)S(1)} %get-tuple-element.29), channel_id=1, source_target_pairs={{1,2},{2,1},{3,4},{4,3},{5,6},{6,5},{7,8},{8,7},{9,10},{10,9},{11,... | collective-permute-start | bytes 98312 | tf_op jit(solution)/shard_map/ppermute | solution.py:488
  6.2 1.3 %shard_map.177 = (f32[4,4,32,128]{3,2,1,0:T(8,128)S(1)}, f32[7,32,128]{2,1,0:T(8,128)S(1)}) custom-call(s32[32,256]{1,0:T(8,128)} %soil.3, s32[32,256]{1,0:T(8,128)} %geo.3, s32[32,256]{1,0:T(8,128)} %land.3, s32[32,256]{1,0:T(8,128)} %river.3, f32[32,256]{1,0:T(8,128)} %elev.3, f32[32,256]{1,0:T(8,128)} %rough.3, f32[32,256]{1,0:T(8,128)} %rain.3, ...), custom_call_target="tpu_custom_call" | custom-call | tf_op jit(solution)/shard_map/pallas_call | solution.py:34
  7.5 0.0 collective-permute-done.a_ref
  7.5 1.5 %collective-permute-done.1.b_ref = f32[32,256]{1,0:T(8,128)S(1)} collective-permute-done((f32[32,256]{1,0:T(8,128)S(1)}, f32[32,256]{1,0:T(8,128)S(1)}, u32[]{:S(2)}, u32[]{:S(2)}) %collective-permute-start.1) | collective-permute-done | bytes 32800 | tf_op jit(solution)/shard_map/ppermute | solution.py:488
  9.0 0.2 shard_map.178
  9.2 16.9 %all_to_all.10.z_ref = f32[4,4,32,128]{3,2,1,0:T(8,128)S(1)} all-to-all(f32[4,4,32,128]{3,2,1,0:T(8,128)S(1)} %get-tuple-element.37), channel_id=1, replica_groups=mesh['sec'=4,'gx'=8,'gy'=16] {'sec'}, dimensions={0} | all-to-all | bytes 524288 | tf_op jit(solution)/shard_map/all_to_all | solution.py:497
  26.0 0.1 shard_map.179
  26.2 8.1 %collective-permute-start.4 = (f32[192,128]{1,0:T(8,128)S(1)}, f32[192,128]{1,0:T(8,128)S(1)}, u32[]{:S(2)}, u32[]{:S(2)}) collective-permute-start(f32[192,128]{1,0:T(8,128)S(1)} %get-tuple-element.44), channel_id=1, source_target_pairs={{16,32},{32,16},{48,64},{64,48},{80,96},{96,80},{17,33},{33,17},{4... | collective-permute-start | bytes 294920 | tf_op jit(solution)/shard_map/ppermute | solution.py:505
  34.3 1.9 %collective-permute-start.5 = (f32[192,128]{1,0:T(8,128)S(1)}, f32[192,128]{1,0:T(8,128)S(1)}, u32[]{:S(2)}, u32[]{:S(2)}) collective-permute-start(f32[192,128]{1,0:T(8,128)S(1)} %get-tuple-element.45), channel_id=1, source_target_pairs={{0,16},{16,0},{32,48},{48,32},{64,80},{80,64},{96,112},{112,96},{1... | collective-permute-start | bytes 294920 | tf_op jit(solution)/shard_map/ppermute | solution.py:506
  36.2 4.9 %collective-permute-start.2 = (f32[128,128]{1,0:T(8,128)S(1)}, f32[128,128]{1,0:T(8,128)S(1)}, u32[]{:S(2)}, u32[]{:S(2)}) collective-permute-start(f32[128,128]{1,0:T(8,128)S(1)} %get-tuple-element.42), channel_id=1, source_target_pairs={{16,32},{32,16},{48,64},{64,48},{80,96},{96,80},{17,33},{33,17},{4... | collective-permute-start | bytes 196616 | tf_op jit(solution)/shard_map/ppermute | solution.py:500
  41.1 1.9 %collective-permute-start.3 = (f32[128,128]{1,0:T(8,128)S(1)}, f32[128,128]{1,0:T(8,128)S(1)}, u32[]{:S(2)}, u32[]{:S(2)}) collective-permute-start(f32[128,128]{1,0:T(8,128)S(1)} %get-tuple-element.43), channel_id=1, source_target_pairs={{0,16},{16,0},{32,48},{48,32},{64,80},{80,64},{96,112},{112,96},{1... | collective-permute-start | bytes 196616 | tf_op jit(solution)/shard_map/ppermute | solution.py:499
  43.0 1.7 %shard_map.180.table_ref = bf16[256,256]{1,0:T(8,128)(2,1)S(1)} custom-call(f32[256,28]{1,0:T(8,128)} %constant.4.clone.sel_ref, s32[256,128]{1,0:T(8,128)} %constant.5.clone.tap_ref, bf16[12,128]{1,0:T(8,128)(2,1)} %soil_ref, bf16[16,128]{1,0:T(8,128)(2,1)} %geo_ref.1, bf16[9,128,128]{2,1,0:T(8,128)(2,1)} %bitcast.2), custom_call_target="tpu_custom_call" | custom-call | tf_op jit(solution)/shard_map/pallas_call | solution.py:34
  44.8 3.6 %collective-permute-done.2.ca_ref = f32[128,128]{1,0:T(8,128)S(1)} collective-permute-done((f32[128,128]{1,0:T(8,128)S(1)}, f32[128,128]{1,0:T(8,128)S(1)}, u32[]{:S(2)}, u32[]{:S(2)}) %collective-permute-start.2) | collective-permute-done | bytes 65568 | tf_op jit(solution)/shard_map/ppermute | solution.py:500
  48.4 0.0 collective-permute-done.3.cb_ref
  48.4 2.4 %shard_map.181.cond_ref = f32[528,128]{1,0:T(8,128)S(1)} custom-call(f32[7,32,128]{2,1,0:T(8,128)S(1)} %get-tuple-element.41.c_ref, f32[128,128]{1,0:T(8,128)S(1)} %collective-permute-done.2.ca_ref, f32[128,128]{1,0:T(8,128)S(1)} %collective-permute-done.3.cb_ref, bf16[256,256]{1,0:T(8,128)(2,1)S(1)} %shard_map.180.table_ref, bf16[8,128]{1,0:T(8,128)(2,1)} %bitcast.3), custom_call_target="tpu_custom_call" | custom-call | tf_op jit(solution)/shard_map/pallas_call | solution.py:34
  50.8 0.0 collective-permute-done.4.a_ref
  50.8 0.0 collective-permute-done.5.b_ref
  50.8 3.1 %shard_map.182 = f32[4,2,32,128]{3,2,1,0:T(8,128)S(1)} custom-call(f32[4,4,32,128]{3,2,1,0:T(8,128)S(1)} %all_to_all.10.z_ref, f32[7,32,128]{2,1,0:T(8,128)S(1)} %get-tuple-element.41.c_ref, f32[128,128]{1,0:T(8,128)S(1)} %collective-permute-done.2.ca_ref, f32[128,128]{1,0:T(8,128)S(1)} %collective-permute-done.3.cb_ref, ...), custom_call_target="tpu_custom_call" | custom-call | tf_op jit(solution)/shard_map/pallas_call | solution.py:34
  53.9 8.6 %all_to_all.11.z_ref = f32[4,2,32,128]{3,2,1,0:T(8,128)S(1)} all-to-all(f32[4,2,32,128]{3,2,1,0:T(8,128)S(1)} %shard_map.182), channel_id=1, replica_groups=mesh['sec'=4,'gx'=8,'gy'=16] {'sec'}, dimensions={0} | all-to-all | bytes 262144 | tf_op jit(solution)/shard_map/all_to_all | solution.py:523
  62.4 0.7 %shard_map.183 = (f32[2,32,256]{2,1,0:T(8,128)}, f32[32,256]{1,0:T(8,128)}) custom-call(f32[4,2,32,128]{3,2,1,0:T(8,128)S(1)} %all_to_all.11.z_ref), custom_call_target="tpu_custom_call" | custom-call | tf_op jit(solution)/shard_map/pallas_call | solution.py:34
Async XLA Ops:
  1.8 5.7 %collective-permute-start = (f32[32,256]{1,0:T(8,128)S(1)}, f32[32,256]{1,0:T(8,128)S(1)}, u32[]{:S(2)}, u32[]{:S(2)}) collective-permute-start(f32[32,256]{1,0:T(8,128)S(1)} %get-tuple-element.28), channel_id=1, source_target_pairs={{0,1},{1,0},{2,3},{3,2},{4,5},{5,4},{6,7},{7,6},{8,9},{9,8},{10,11... | collective-permute-start | bytes 98312 | tf_op jit(solution)/shard_map/ppermute | solution.py:487
  3.7 5.2 %collective-permute-start.1 = (f32[32,256]{1,0:T(8,128)S(1)}, f32[32,256]{1,0:T(8,128)S(1)}, u32[]{:S(2)}, u32[]{:S(2)}) collective-permute-start(f32[32,256]{1,0:T(8,128)S(1)} %get-tuple-element.29), channel_id=1, source_target_pairs={{1,2},{2,1},{3,4},{4,3},{5,6},{6,5},{7,8},{8,7},{9,10},{10,9},{11,... | collective-permute-start | bytes 98312 | tf_op jit(solution)/shard_map/ppermute | solution.py:488
  26.2 24.6 %collective-permute-start.4 = (f32[192,128]{1,0:T(8,128)S(1)}, f32[192,128]{1,0:T(8,128)S(1)}, u32[]{:S(2)}, u32[]{:S(2)}) collective-permute-start(f32[192,128]{1,0:T(8,128)S(1)} %get-tuple-element.44), channel_id=1, source_target_pairs={{16,32},{32,16},{48,64},{64,48},{80,96},{96,80},{17,33},{33,17},{4... | collective-permute-start | bytes 294920 | tf_op jit(solution)/shard_map/ppermute | solution.py:505
  34.3 16.5 %collective-permute-start.5 = (f32[192,128]{1,0:T(8,128)S(1)}, f32[192,128]{1,0:T(8,128)S(1)}, u32[]{:S(2)}, u32[]{:S(2)}) collective-permute-start(f32[192,128]{1,0:T(8,128)S(1)} %get-tuple-element.45), channel_id=1, source_target_pairs={{0,16},{16,0},{32,48},{48,32},{64,80},{80,64},{96,112},{112,96},{1... | collective-permute-start | bytes 294920 | tf_op jit(solution)/shard_map/ppermute | solution.py:506
  36.2 12.2 %collective-permute-start.2 = (f32[128,128]{1,0:T(8,128)S(1)}, f32[128,128]{1,0:T(8,128)S(1)}, u32[]{:S(2)}, u32[]{:S(2)}) collective-permute-start(f32[128,128]{1,0:T(8,128)S(1)} %get-tuple-element.42), channel_id=1, source_target_pairs={{16,32},{32,16},{48,64},{64,48},{80,96},{96,80},{17,33},{33,17},{4... | collective-permute-start | bytes 196616 | tf_op jit(solution)/shard_map/ppermute | solution.py:500
  41.1 7.3 %collective-permute-start.3 = (f32[128,128]{1,0:T(8,128)S(1)}, f32[128,128]{1,0:T(8,128)S(1)}, u32[]{:S(2)}, u32[]{:S(2)}) collective-permute-start(f32[128,128]{1,0:T(8,128)S(1)} %get-tuple-element.43), channel_id=1, source_target_pairs={{0,16},{16,0},{32,48},{48,32},{64,80},{80,64},{96,112},{112,96},{1... | collective-permute-start | bytes 196616 | tf_op jit(solution)/shard_map/ppermute | solution.py:499

commit v6 on v5

--- a/solution.py
+++ b/solution.py
@@ -223,28 +223,8 @@
 MSG_ROWS_2D = 5 * HALO + 2 * CROWS
 
 
-STEP_S = 8
-TRIPS_S = 1
-BLOCK_K = 16
-
-
 def at_row(r):
     return pl.ds(pl.multiple_of(8 * r + 8, 8), 8)
-
-
-def beside(mid, step):
-    return pltpu.roll(mid, (-step) % 8, 0)
-
-
-def row_blocks(low, high, size, body):
-    assert (high - low) % size == 0
-
-    def step(b, carry):
-        for i in range(size):
-            body(low + b * size + i)
-        return carry
-
-    lax.fori_loop(0, (high - low) // size, step, 0)
 
 
 def shift_classes(ref, kind, value):
@@ -315,13 +295,56 @@
     cond_ref[8 * (full + 1) :, :] = jnp.zeros((8, LANES), f32)
 
 
+def face_coefficients(cond_ref, r, store):
+    sub = lax.broadcasted_iota(jnp.int32, (8, LANES), 0)
+    mid = cond_ref[at_row(r), :]
+    north = 0.5 * lateral * (mid + cond_ref[at_row(r - 1), :])
+    south = 0.5 * lateral * (mid + cond_ref[at_row(r + 1), :])
+    east = 0.5 * lateral * (mid + pltpu.roll(mid, LANES - 1, 1))
+    west = pltpu.roll(east, 1, 1)
+    up = 0.5 * vertical * (mid + jnp.where(sub > 0, pltpu.roll(mid, 1, 0), 0.0))
+    down = 0.5 * vertical * (mid + jnp.where(sub < 7, pltpu.roll(mid, 7, 0), 0.0))
+    diagonal = store + up + down + north + south + east + west
+    live = store > 0.0
+    inverse = jnp.where(live, 1.0, 0.0) / jnp.where(live, diagonal, 1.0)
+    return (
+        jnp.where(sub > 0, up * inverse, 0.0),
+        jnp.where(sub < 7, down * inverse, 0.0),
+        north * inverse,
+        south * inverse,
+        east * inverse,
+        west * inverse,
+        store * inverse,
+        jnp.where(sub == 0, inverse, 0.0),
+    )
+
+
+def by_layer(parts):
+    return jnp.swapaxes(jnp.stack(parts), 0, 1).reshape(64, LANES)
+
+
+def own_kernel(z_ref, cond_ref, press_ref, coef_ref):
+    rows = z_ref.shape[2]
+    for r in range(0, rows, 8):
+        press_ref[8 * r : 8 * r + 64, :] = by_layer([z_ref[l // 2, l % 2, r : r + 8, :] for l in range(8)])
+        store = by_layer([z_ref[l // 2, 2 + l % 2, r : r + 8, :] for l in range(8)])
+        for i in range(8):
+            values = face_coefficients(cond_ref, r + i + HALO, store[8 * i : 8 * i + 8])
+            for k, value in enumerate(values):
+                coef_ref[k, 8 * (r + i) : 8 * (r + i) + 8, :] = value
+
+
 def main_kernel(
-    z_ref, c_ref, ca_ref, cb_ref, a_ref, b_ref, cond_ref, out_ref,
-    press_ref, press2_ref, stor_ref, coef_ref, rhs_ref, flat_ref, src_ref,
+    c_ref, ca_ref, cb_ref, a_ref, b_ref, cond_ref, own_press_ref, own_coef_ref, out_ref,
+    press_ref, press2_ref, coef_ref, rhs_ref, flat_ref, src_ref,
 ):
-    rows = z_ref.shape[2]
+    rows = c_ref.shape[1]
     full = rows + 2 * HALO
     above, below = by_side(ca_ref, cb_ref)
+
+    def edge_row(r):
+        at = 8 * (r if r < HALO else r - rows)
+        return slice(at, at + 8)
 
     for j in range(5):
         at = j * HALO
@@ -329,54 +352,24 @@
         flat_ref[j, HALO : HALO + rows, :] = c_ref[j]
         flat_ref[j, HALO + rows : full, :] = below[at : at + HALO]
 
-    for ref in (press_ref, press2_ref):
-        ref[0:8, :] = jnp.zeros((8, LANES), f32)
-        ref[8 * (full + 1) :, :] = jnp.zeros((8, LANES), f32)
-    north, south = by_side(a_ref, b_ref)
-    sides = [[unpack(side, s) for s in range(4)] for side in (north, south)]
-    for f, ref in ((0, press_ref), (1, stor_ref)):
-        for r in range(0, full, 8):
-            parts = []
-            for l in range(8):
-                s, i = l // 2, 2 * f + l % 2
-                if r < HALO:
-                    part = sides[0][s][i][r : r + 8]
-                elif r < HALO + rows:
-                    part = z_ref[s, i, r - HALO : r - HALO + 8, :]
-                else:
-                    at = r - HALO - rows
-                    part = sides[1][s][i][at : at + 8]
-                parts.append(part)
-            mixed = jnp.swapaxes(jnp.stack(parts), 0, 1).reshape(64, LANES)
-            ref[8 * (r + 1) : 8 * (r + 9), :] = mixed
-    sub = lax.broadcasted_iota(jnp.int32, (8, LANES), 0)
-
-    def row_coefficients(r):
-        mid = cond_ref[at_row(r), :]
-        north = 0.5 * lateral * (mid + cond_ref[at_row(r - 1), :])
-        south = 0.5 * lateral * (mid + cond_ref[at_row(r + 1), :])
-        east = 0.5 * lateral * (mid + pltpu.roll(mid, LANES - 1, 1))
-        west = pltpu.roll(east, 1, 1)
-        up = 0.5 * vertical * (mid + jnp.where(sub > 0, pltpu.roll(mid, 1, 0), 0.0))
-        down = 0.5 * vertical * (mid + jnp.where(sub < 7, pltpu.roll(mid, 7, 0), 0.0))
-        store = stor_ref[at_row(r), :]
-        diagonal = store + up + down + north + south + east + west
-        live = store > 0.0
-        inverse = jnp.where(live, 1.0, 0.0) / jnp.where(live, diagonal, 1.0)
-        here = at_row(r - 1)
-        coef_ref[0, here, :] = jnp.where(sub > 0, up * inverse, 0.0)
-        coef_ref[1, here, :] = jnp.where(sub < 7, down * inverse, 0.0)
-        coef_ref[2, here, :] = north * inverse
-        coef_ref[3, here, :] = south * inverse
-        coef_ref[4, here, :] = east * inverse
-        coef_ref[5, here, :] = west * inverse
-        coef_ref[6, here, :] = store * inverse
-        coef_ref[7, here, :] = jnp.where(sub == 0, inverse, 0.0)
-
-    row_blocks(0, full, BLOCK_K, row_coefficients)
-    for k in range(8):
-        coef_ref[k, 0:8, :] = jnp.zeros((8, LANES), f32)
-        coef_ref[k, 8 * (full - 1) : 8 * full, :] = jnp.zeros((8, LANES), f32)
+    press_ref[8 * (HALO + 1) : 8 * (HALO + rows + 1), :] = own_press_ref[...]
+    for side, low in zip(by_side(a_ref, b_ref), (0, HALO + rows)):
+        fields = [unpack(side, s) for s in range(4)]
+        for r in range(0, HALO, 8):
+            at = 8 * (low + r + 1)
+            press_ref[at : at + 64, :] = by_layer([fields[l // 2][l % 2][r : r + 8] for l in range(8)])
+            store = by_layer([fields[l // 2][2 + l % 2][r : r + 8] for l in range(8)])
+            for i in range(8):
+                row = low + r + i
+                if 0 < row < full - 1:
+                    values = face_coefficients(cond_ref, row, store[8 * i : 8 * i + 8])
+                    for k, value in enumerate(values):
+                        coef_ref[k, edge_row(row), :] = value
+
+    def coef(k, r):
+        if HALO <= r < HALO + rows:
+            return own_coef_ref[k, 8 * (r - HALO) : 8 * (r - HALO) + 8, :]
+        return coef_ref[k, edge_row(r), :]
 
     rough, rain, evap, elev = flat_ref[0], flat_ref[1], flat_ref[2], flat_ref[3]
     head = flat_ref[4]
@@ -408,45 +401,52 @@
         for sweep in range(SWEEPS):
             old, new = (press_ref, press2_ref) if sweep % 2 == 0 else (press2_ref, press_ref)
 
-            def one_row(r):
-                here = at_row(r - 1)
+            for r in range(done + sweep + 1, full - done - sweep - 1):
+                here = slice(8 * r, 8 * r + 8)
                 mid = old[at_row(r), :]
                 if sweep == 0:
-                    source = jnp.broadcast_to(src_ref[pl.ds(r, 1), :], (8, LANES))
-                    rhs = coef_ref[6, here, :] * mid + coef_ref[7, here, :] * source
+                    source = jnp.broadcast_to(src_ref[r : r + 1, :], (8, LANES))
+                    rhs = coef(6, r) * mid + coef(7, r) * source
                     rhs_ref[here, :] = rhs
                 else:
                     rhs = rhs_ref[here, :]
-                column = coef_ref[0, here, :] * beside(mid, -1) + coef_ref[1, here, :] * beside(mid, 1)
-                across = coef_ref[2, here, :] * old[at_row(r - 1), :] + coef_ref[3, here, :] * old[at_row(r + 1), :]
-                along = coef_ref[4, here, :] * pltpu.roll(mid, LANES - 1, 1) + coef_ref[5, here, :] * pltpu.roll(mid, 1, 1)
+                column = coef(0, r) * pltpu.roll(mid, 1, 0) + coef(1, r) * pltpu.roll(mid, 7, 0)
+                across = coef(2, r) * old[at_row(r - 1), :] + coef(3, r) * old[at_row(r + 1), :]
+                along = coef(4, r) * pltpu.roll(mid, LANES - 1, 1) + coef(5, r) * pltpu.roll(mid, 1, 1)
                 new[at_row(r), :] = (rhs + column) + (across + along)
-
-            first = done + sweep + 1
-            low = first // STEP_S * STEP_S
-            row_blocks(low, full - low, (full - 2 * low) // TRIPS_S, one_row)
 
     lane = lax.broadcasted_iota(jnp.int32, (8, LANES), 1)
     for r in range(HALO, HALO + rows, 8):
         layers = jnp.swapaxes(press_ref[8 * (r + 1) : 8 * (r + 9), :].reshape(8, 8, LANES), 0, 1)
         for s in range(4):
-            out_ref[s, 0, r - HALO : r - HALO + 8, :] = jnp.where(
+            out_ref[s, r - HALO : r - HALO + 8, :] = jnp.where(
                 lane < CHUNK,
                 pltpu.roll(layers[2 * s], LANES - EDGE, 1),
                 pltpu.roll(layers[2 * s + 1], EDGE, 1),
             )
-            out_ref[s, 1, r - HALO : r - HALO + 8, :] = pltpu.roll(head[r : r + 8], LANES - EDGE, 1)
+    for r in range(HALO, HALO + rows // 2, 8):
+        both = jnp.where(
+            lane < CHUNK,
+            pltpu.roll(head[r : r + 8], LANES - EDGE, 1),
+            pltpu.roll(head[r + rows // 2 : r + rows // 2 + 8], EDGE, 1),
+        )
+        for s in range(4):
+            out_ref[s, rows + r - HALO : rows + r - HALO + 8, :] = both
 
 
 def finish_kernel(z_ref, press_ref, head_ref):
-    rows = z_ref.shape[2]
+    rows = head_ref.shape[0]
+    half = rows // 2
     lane = lax.broadcasted_iota(jnp.int32, (rows, LANES), 1)
+    low = lane[:half] < CHUNK
     for d in range(0, 4, 2):
         cols = slice(d * CHUNK, d * CHUNK + LANES)
-        a, b = z_ref[d, 0], z_ref[d + 1, 0]
+        a, b = z_ref[d, :rows, :], z_ref[d + 1, :rows, :]
         press_ref[0, :, cols] = jnp.where(lane < CHUNK, a, pltpu.roll(b, CHUNK, 1))
         press_ref[1, :, cols] = jnp.where(lane < CHUNK, pltpu.roll(a, CHUNK, 1), b)
-        head_ref[:, cols] = jnp.where(lane < CHUNK, z_ref[d, 1], pltpu.roll(z_ref[d + 1, 1], CHUNK, 1))
+        a, b = z_ref[d, rows:, :], z_ref[d + 1, rows:, :]
+        head_ref[:half, cols] = jnp.where(low, a, pltpu.roll(b, CHUNK, 1))
+        head_ref[half:, cols] = jnp.where(low, pltpu.roll(a, CHUNK, 1), b)
 
 
 def main_call(rows, args):
@@ -454,12 +454,11 @@
     grid = (8 * full, LANES)
     framed = (8 * (full + 2), LANES)
     return call(
-        main_kernel, (jax.ShapeDtypeStruct((4, 2, rows, LANES), f32),), args,
+        main_kernel, (jax.ShapeDtypeStruct((4, rows + rows // 2, LANES), f32),), args,
         scratch=[
             pltpu.VMEM(framed, f32),
             pltpu.VMEM(framed, f32),
-            pltpu.VMEM(framed, f32),
-            pltpu.VMEM((8,) + grid, f32),
+            pltpu.VMEM((8, 8 * 2 * HALO, LANES), f32),
             pltpu.VMEM(grid, f32),
             pltpu.VMEM((5, full, LANES), f32),
             pltpu.VMEM((full, LANES), f32),
@@ -518,8 +517,9 @@
         conduct_kernel, (sds((8 * (rows + 2 * HALO + 2), LANES), f32),), (cols, ca, cb, table, out_weight.T),
         scratch=[pltpu.VMEM((6, rows + 2 * CROWS, LANES), f32)], hbm=(4,),
     )
-    xa, xb, cond = lax.optimization_barrier((xa, xb, cond))
-    out = main_call(rows, (z, cols, ca, cb, xa, xb, cond))
+    own_press, own_coef = call(own_kernel, (sds((8 * rows, LANES), f32), sds((8, 8 * rows, LANES), f32)), (z, cond))
+    xa, xb, own_press, own_coef = lax.optimization_barrier((xa, xb, own_press, own_coef))
+    out = main_call(rows, (cols, ca, cb, xa, xb, cond, own_press, own_coef))
     out = lax.all_to_all(out, "sec", 0, 0)
     return call(finish_kernel, (sds(pressure.shape, f32), sds((rows, width), f32)), (out,), final=True)
 

time: 63.6 us -> 62.9 us (0.989)
    pallas_call x8 -> x9, Pallas kernels: 10.6 us -> 10 us  [call(): pl.pallas_call(kernel, out_shape=made, in_specs=[VMEM] * len(args), out_s...]
  transfers between devices with their start and end apart: 6 -> 6, of which waited for: 2 -> 2; matrix products, arithmetic and copies ran while one was open for 0% -> 0% of each run, Pallas kernels for 8% -> 9%
where the time goes in v6:
time: 62.9 us; the launch traced here: 62.5 us
  blocking collectives  25.4 us (40%)
  starting transfers between devices  21.2 us (34%)
  Pallas kernels  10 us (16%)
  waiting for transfers between devices  5.11 us (8%)
  between operations  0.76 us (1%)
    all_to_all x1, blocking collectives, shards(): z = lax.all_to_all(z, 'sec', 0, 0)  16.9 us
    pallas_call x9, Pallas kernels, call(): pl.pallas_call(kernel, out_shape=made, in_specs=[VMEM] * len(args), out_s...  10 us
    all_to_all x1, blocking collectives, shards(): out = lax.all_to_all(out, 'sec', 0, 0)  8.47 us
    ppermute x1, starting transfers between devices, shards(): xa = lax.ppermute(xa, 'gx', swap_pairs(n_gx, 1))  8.13 us
    ppermute x1, starting transfers between devices, shards(): ca = lax.ppermute(ca, 'gx', swap_pairs(n_gx, 1))  4.88 us
    ppermute x1, waiting for transfers between devices, shards(): ca = lax.ppermute(ca, 'gx', swap_pairs(n_gx, 1))  3.64 us
    ppermute x1, starting transfers between devices, shards(): yb = lax.ppermute(yb, 'gy', swap_pairs(n_gy, 1))  2.46 us
    ppermute x1, starting transfers between devices, shards(): ya = lax.ppermute(ya, 'gy', swap_pairs(n_gy, 0))  1.92 us
  transfers between devices with their start and end apart: 6, of which 2 were waited for; matrix products, arithmetic and copies ran while one was open for 0% of the time, Pallas kernels for 9%

profile of v6, /device:TPU:30, one launch (start us, length us, event | category | flops | bytes accessed | tf_op | source)
XLA Modules:
  0.0 62.5 jit_solution(12643634773120479672)
XLA Ops:
  0.6 1.2 %shard_map.176 = (f32[32,256]{1,0:T(8,128)S(1)}, f32[32,256]{1,0:T(8,128)S(1)}) custom-call(s32[32,256]{1,0:T(8,128)} %soil.3, s32[32,256]{1,0:T(8,128)} %geo.3, s32[32,256]{1,0:T(8,128)} %land.3, s32[32,256]{1,0:T(8,128)} %river.3, f32[32,256]{1,0:T(8,128)} %elev.3, f32[32,256]{1,0:T(8,128)} %rough.3, f32[32,256]{1,0:T(8,128)} %rain.3, f32[32,256]{1,0:T(8,128)} %evap.3, ...), custom_call_target="tpu_custom_call" | custom-call | tf_op jit(solution)/shard_map/pallas_call | solution.py:34
  1.8 1.9 %collective-permute-start = (f32[32,256]{1,0:T(8,128)S(1)}, f32[32,256]{1,0:T(8,128)S(1)}, u32[]{:S(2)}, u32[]{:S(2)}) collective-permute-start(f32[32,256]{1,0:T(8,128)S(1)} %get-tuple-element.31), channel_id=1, source_target_pairs={{0,1},{1,0},{2,3},{3,2},{4,5},{5,4},{6,7},{7,6},{8,9},{9,8},{10,11... | collective-permute-start | bytes 98312 | tf_op jit(solution)/shard_map/ppermute | solution.py:486
  3.7 2.5 %collective-permute-start.1 = (f32[32,256]{1,0:T(8,128)S(1)}, f32[32,256]{1,0:T(8,128)S(1)}, u32[]{:S(2)}, u32[]{:S(2)}) collective-permute-start(f32[32,256]{1,0:T(8,128)S(1)} %get-tuple-element.32), channel_id=1, source_target_pairs={{1,2},{2,1},{3,4},{4,3},{5,6},{6,5},{7,8},{8,7},{9,10},{10,9},{11,... | collective-permute-start | bytes 98312 | tf_op jit(solution)/shard_map/ppermute | solution.py:487
  6.2 1.3 %shard_map.177 = (f32[4,4,32,128]{3,2,1,0:T(8,128)S(1)}, f32[7,32,128]{2,1,0:T(8,128)S(1)}) custom-call(s32[32,256]{1,0:T(8,128)} %soil.3, s32[32,256]{1,0:T(8,128)} %geo.3, s32[32,256]{1,0:T(8,128)} %land.3, s32[32,256]{1,0:T(8,128)} %river.3, f32[32,256]{1,0:T(8,128)} %elev.3, f32[32,256]{1,0:T(8,128)} %rough.3, f32[32,256]{1,0:T(8,128)} %rain.3, ...), custom_call_target="tpu_custom_call" | custom-call | tf_op jit(solution)/shard_map/pallas_call | solution.py:34
  7.5 0.0 collective-permute-done.a_ref
  7.5 1.5 %collective-permute-done.1.b_ref = f32[32,256]{1,0:T(8,128)S(1)} collective-permute-done((f32[32,256]{1,0:T(8,128)S(1)}, f32[32,256]{1,0:T(8,128)S(1)}, u32[]{:S(2)}, u32[]{:S(2)}) %collective-permute-start.1) | collective-permute-done | bytes 32800 | tf_op jit(solution)/shard_map/ppermute | solution.py:487
  9.0 0.2 shard_map.178
  9.2 16.9 %all_to_all.10.z_ref = f32[4,4,32,128]{3,2,1,0:T(8,128)S(1)} all-to-all(f32[4,4,32,128]{3,2,1,0:T(8,128)S(1)} %get-tuple-element.40), channel_id=1, replica_groups=mesh['sec'=4,'gx'=8,'gy'=16] {'sec'}, dimensions={0} | all-to-all | bytes 524288 | tf_op jit(solution)/shard_map/all_to_all | solution.py:496
  26.0 0.1 shard_map.179
  26.2 8.1 %collective-permute-start.4 = (f32[192,128]{1,0:T(8,128)S(1)}, f32[192,128]{1,0:T(8,128)S(1)}, u32[]{:S(2)}, u32[]{:S(2)}) collective-permute-start(f32[192,128]{1,0:T(8,128)S(1)} %get-tuple-element.47), channel_id=1, source_target_pairs={{16,32},{32,16},{48,64},{64,48},{80,96},{96,80},{17,33},{33,17},{4... | collective-permute-start | bytes 294920 | tf_op jit(solution)/shard_map/ppermute | solution.py:504
  34.3 1.9 %collective-permute-start.5 = (f32[192,128]{1,0:T(8,128)S(1)}, f32[192,128]{1,0:T(8,128)S(1)}, u32[]{:S(2)}, u32[]{:S(2)}) collective-permute-start(f32[192,128]{1,0:T(8,128)S(1)} %get-tuple-element.48), channel_id=1, source_target_pairs={{0,16},{16,0},{32,48},{48,32},{64,80},{80,64},{96,112},{112,96},{1... | collective-permute-start | bytes 294920 | tf_op jit(solution)/shard_map/ppermute | solution.py:505
  36.2 4.9 %collective-permute-start.2 = (f32[128,128]{1,0:T(8,128)S(1)}, f32[128,128]{1,0:T(8,128)S(1)}, u32[]{:S(2)}, u32[]{:S(2)}) collective-permute-start(f32[128,128]{1,0:T(8,128)S(1)} %get-tuple-element.45), channel_id=1, source_target_pairs={{16,32},{32,16},{48,64},{64,48},{80,96},{96,80},{17,33},{33,17},{4... | collective-permute-start | bytes 196616 | tf_op jit(solution)/shard_map/ppermute | solution.py:499
  41.1 1.9 %collective-permute-start.3 = (f32[128,128]{1,0:T(8,128)S(1)}, f32[128,128]{1,0:T(8,128)S(1)}, u32[]{:S(2)}, u32[]{:S(2)}) collective-permute-start(f32[128,128]{1,0:T(8,128)S(1)} %get-tuple-element.46), channel_id=1, source_target_pairs={{0,16},{16,0},{32,48},{48,32},{64,80},{80,64},{96,112},{112,96},{1... | collective-permute-start | bytes 196616 | tf_op jit(solution)/shard_map/ppermute | solution.py:498
  43.0 1.7 %shard_map.180.table_ref = bf16[256,256]{1,0:T(8,128)(2,1)S(1)} custom-call(f32[256,28]{1,0:T(8,128)} %constant.4.clone.sel_ref, s32[256,128]{1,0:T(8,128)} %constant.5.clone.tap_ref, bf16[12,128]{1,0:T(8,128)(2,1)} %soil_ref, bf16[16,128]{1,0:T(8,128)(2,1)} %geo_ref.1, bf16[9,128,128]{2,1,0:T(8,128)(2,1)} %bitcast.2), custom_call_target="tpu_custom_call" | custom-call | tf_op jit(solution)/shard_map/pallas_call | solution.py:34
  44.8 3.6 %collective-permute-done.2.ca_ref = f32[128,128]{1,0:T(8,128)S(1)} collective-permute-done((f32[128,128]{1,0:T(8,128)S(1)}, f32[128,128]{1,0:T(8,128)S(1)}, u32[]{:S(2)}, u32[]{:S(2)}) %collective-permute-start.2) | collective-permute-done | bytes 65568 | tf_op jit(solution)/shard_map/ppermute | solution.py:499
  48.4 0.0 collective-permute-done.3.cb_ref
  48.4 2.4 %shard_map.181.cond_ref = f32[528,128]{1,0:T(8,128)S(1)} custom-call(f32[7,32,128]{2,1,0:T(8,128)S(1)} %get-tuple-element.44.c_ref, f32[128,128]{1,0:T(8,128)S(1)} %collective-permute-done.2.ca_ref, f32[128,128]{1,0:T(8,128)S(1)} %collective-permute-done.3.cb_ref, bf16[256,256]{1,0:T(8,128)(2,1)S(1)} %shard_map.180.table_ref, bf16[8,128]{1,0:T(8,128)(2,1)} %bitcast.3), custom_call_target="tpu_custom_call" | custom-call | tf_op jit(solution)/shard_map/pallas_call | solution.py:34
  50.8 0.3 shard_map.182
  51.0 0.0 collective-permute-done.4.a_ref
  51.1 0.0 collective-permute-done.5.b_ref
  51.1 2.2 %shard_map.183 = f32[4,48,128]{2,1,0:T(8,128)S(1)} custom-call(f32[7,32,128]{2,1,0:T(8,128)S(1)} %get-tuple-element.44.c_ref, f32[128,128]{1,0:T(8,128)S(1)} %collective-permute-done.2.ca_ref, f32[128,128]{1,0:T(8,128)S(1)} %collective-permute-done.3.cb_ref, f32[192,128]{1,0:T(8,128)S(1)} %collective-permute-done.4.a_ref, ...), custom_call_target="tpu_custom_call" | custom-call | tf_op jit(solution)/shard_map/pallas_call | solution.py:34
  53.3 8.5 %all_to_all.11.z_ref = f32[4,48,128]{2,1,0:T(8,128)S(1)} all-to-all(f32[4,48,128]{2,1,0:T(8,128)S(1)} %shard_map.183), channel_id=1, replica_groups=mesh['sec'=4,'gx'=8,'gy'=16] {'sec'}, dimensions={0} | all-to-all | bytes 196608 | tf_op jit(solution)/shard_map/all_to_all | solution.py:523
  61.7 0.7 %shard_map.184 = (f32[2,32,256]{2,1,0:T(8,128)}, f32[32,256]{1,0:T(8,128)}) custom-call(f32[4,48,128]{2,1,0:T(8,128)S(1)} %all_to_all.11.z_ref), custom_call_target="tpu_custom_call" | custom-call | tf_op jit(solution)/shard_map/pallas_call | solution.py:34
Async XLA Ops:
  1.8 5.7 %collective-permute-start = (f32[32,256]{1,0:T(8,128)S(1)}, f32[32,256]{1,0:T(8,128)S(1)}, u32[]{:S(2)}, u32[]{:S(2)}) collective-permute-start(f32[32,256]{1,0:T(8,128)S(1)} %get-tuple-element.31), channel_id=1, source_target_pairs={{0,1},{1,0},{2,3},{3,2},{4,5},{5,4},{6,7},{7,6},{8,9},{9,8},{10,11... | collective-permute-start | bytes 98312 | tf_op jit(solution)/shard_map/ppermute | solution.py:486
  3.7 5.2 %collective-permute-start.1 = (f32[32,256]{1,0:T(8,128)S(1)}, f32[32,256]{1,0:T(8,128)S(1)}, u32[]{:S(2)}, u32[]{:S(2)}) collective-permute-start(f32[32,256]{1,0:T(8,128)S(1)} %get-tuple-element.32), channel_id=1, source_target_pairs={{1,2},{2,1},{3,4},{4,3},{5,6},{6,5},{7,8},{8,7},{9,10},{10,9},{11,... | collective-permute-start | bytes 98312 | tf_op jit(solution)/shard_map/ppermute | solution.py:487
  26.2 24.9 %collective-permute-start.4 = (f32[192,128]{1,0:T(8,128)S(1)}, f32[192,128]{1,0:T(8,128)S(1)}, u32[]{:S(2)}, u32[]{:S(2)}) collective-permute-start(f32[192,128]{1,0:T(8,128)S(1)} %get-tuple-element.47), channel_id=1, source_target_pairs={{16,32},{32,16},{48,64},{64,48},{80,96},{96,80},{17,33},{33,17},{4... | collective-permute-start | bytes 294920 | tf_op jit(solution)/shard_map/ppermute | solution.py:504
  34.3 16.8 %collective-permute-start.5 = (f32[192,128]{1,0:T(8,128)S(1)}, f32[192,128]{1,0:T(8,128)S(1)}, u32[]{:S(2)}, u32[]{:S(2)}) collective-permute-start(f32[192,128]{1,0:T(8,128)S(1)} %get-tuple-element.48), channel_id=1, source_target_pairs={{0,16},{16,0},{32,48},{48,32},{64,80},{80,64},{96,112},{112,96},{1... | collective-permute-start | bytes 294920 | tf_op jit(solution)/shard_map/ppermute | solution.py:505
  36.2 12.2 %collective-permute-start.2 = (f32[128,128]{1,0:T(8,128)S(1)}, f32[128,128]{1,0:T(8,128)S(1)}, u32[]{:S(2)}, u32[]{:S(2)}) collective-permute-start(f32[128,128]{1,0:T(8,128)S(1)} %get-tuple-element.45), channel_id=1, source_target_pairs={{16,32},{32,16},{48,64},{64,48},{80,96},{96,80},{17,33},{33,17},{4... | collective-permute-start | bytes 196616 | tf_op jit(solution)/shard_map/ppermute | solution.py:499
  41.1 7.3 %collective-permute-start.3 = (f32[128,128]{1,0:T(8,128)S(1)}, f32[128,128]{1,0:T(8,128)S(1)}, u32[]{:S(2)}, u32[]{:S(2)}) collective-permute-start(f32[128,128]{1,0:T(8,128)S(1)} %get-tuple-element.46), channel_id=1, source_target_pairs={{0,16},{16,0},{32,48},{48,32},{64,80},{80,64},{96,112},{112,96},{1... | collective-permute-start | bytes 196616 | tf_op jit(solution)/shard_map/ppermute | solution.py:498

commit v7 on v6

--- a/solution.py
+++ b/solution.py
@@ -167,12 +167,17 @@
         )
 
     inner_l, inner_r = lane >= EDGE, lane < LANES - EDGE
+    fields = []
     for i in range(4):
         lo, hi = halos(0, 16 * i, 16)
-        z_ref[0, i] = jnp.where(inner_l, z_in[0, i], lo)
-        z_ref[1, i] = z_in[1, i]
-        z_ref[2, i] = z_in[2, i]
-        z_ref[3, i] = jnp.where(inner_r, z_in[3, i], hi)
+        fields.append(
+            (jnp.where(inner_l, z_in[0, i], lo), z_in[1, i], z_in[2, i], jnp.where(inner_r, z_in[3, i], hi))
+        )
+    free = (lane < EDGE - HALO) | (lane >= LANES - EDGE + HALO)
+    for d in range(4):
+        for i in range(3):
+            moved = pltpu.roll(fields[3][d], LANES - EDGE * (i + 1), 1)
+            z_ref[d, i] = jnp.where(free, moved, fields[i][d])
     spots = [(0, 16 * i, 16) for i in range(4, 8)] + [(1, 0, 16), (1, 32, 32), (1, 64, 32)]
     for j, spot in enumerate(spots):
         lo, hi = halos(*spot)
@@ -197,22 +202,17 @@
     odd = lax.axis_index("gx") % 2 == 1
     rows = z_ref.shape[2]
     low = jnp.where(odd, rows - HALO, 0)
-    lane = lax.broadcasted_iota(jnp.int32, (HALO, LANES), 1)
-    free = (lane < EDGE - HALO) | (lane >= LANES - EDGE + HALO)
     for ref, at in ((a_ref, low), (b_ref, (rows - HALO) - low)):
         at = pl.multiple_of(at, 8)
         for s in range(4):
-            last = z_ref[s, 3, pl.ds(at, HALO), :]
             for i in range(3):
                 k = (3 * s + i) * HALO
-                moved = pltpu.roll(last, LANES - EDGE * (i + 1), 1)
-                ref[k : k + HALO, :] = jnp.where(free, moved, z_ref[s, i, pl.ds(at, HALO), :])
-
-
-def unpack(ref, s):
-    lane = lax.broadcasted_iota(jnp.int32, (HALO, LANES), 1)
-    parts = [ref[(3 * s + i) * HALO : (3 * s + i + 1) * HALO, :] for i in range(3)]
-    last = jnp.zeros((HALO, LANES), f32)
+                ref[k : k + HALO, :] = z_ref[s, i, pl.ds(at, HALO), :]
+
+
+def unpack(parts):
+    lane = lax.broadcasted_iota(jnp.int32, parts[0].shape, 1)
+    last = jnp.zeros_like(parts[0])
     for i, part in enumerate(parts):
         start = EDGE - HALO + EDGE * i
         last = jnp.where((lane >= start) & (lane < start + EDGE), pltpu.roll(part, EDGE * (i + 1), 1), last)
@@ -326,8 +326,9 @@
 def own_kernel(z_ref, cond_ref, press_ref, coef_ref):
     rows = z_ref.shape[2]
     for r in range(0, rows, 8):
-        press_ref[8 * r : 8 * r + 64, :] = by_layer([z_ref[l // 2, l % 2, r : r + 8, :] for l in range(8)])
-        store = by_layer([z_ref[l // 2, 2 + l % 2, r : r + 8, :] for l in range(8)])
+        fields = [unpack([z_ref[s, i, r : r + 8, :] for i in range(3)]) for s in range(4)]
+        press_ref[8 * r : 8 * r + 64, :] = by_layer([fields[l // 2][l % 2] for l in range(8)])
+        store = by_layer([fields[l // 2][2 + l % 2] for l in range(8)])
         for i in range(8):
             values = face_coefficients(cond_ref, r + i + HALO, store[8 * i : 8 * i + 8])
             for k, value in enumerate(values):
@@ -354,7 +355,7 @@
 
     press_ref[8 * (HALO + 1) : 8 * (HALO + rows + 1), :] = own_press_ref[...]
     for side, low in zip(by_side(a_ref, b_ref), (0, HALO + rows)):
-        fields = [unpack(side, s) for s in range(4)]
+        fields = [unpack([side[(3 * s + i) * HALO : (3 * s + i + 1) * HALO] for i in range(3)]) for s in range(4)]
         for r in range(0, HALO, 8):
             at = 8 * (low + r + 1)
             press_ref[at : at + 64, :] = by_layer([fields[l // 2][l % 2][r : r + 8] for l in range(8)])
@@ -492,7 +493,7 @@
     )
     ya, yb, z, cols = lax.optimization_barrier((ya, yb, z, cols))
     edge_2d = sds((MSG_ROWS_2D, LANES), f32)
-    z, cols, ca, cb = call(halo_kernel, (chunks, plane, edge_2d, edge_2d), (z, cols, ya, yb))
+    z, cols, ca, cb = call(halo_kernel, (sds((4, 3, rows, LANES), f32), plane, edge_2d, edge_2d), (z, cols, ya, yb))
     z = lax.all_to_all(z, "sec", 0, 0)
 
     cb = lax.ppermute(cb, "gx", swap_pairs(n_gx, 0))

time: 62.9 us -> 61.8 us (0.983)
  blocking collectives: 25.4 us -> 23.7 us
    all_to_all x1, blocking collectives: 16.9 us -> 14.7 us  [shards(): z = lax.all_to_all(z, 'sec', 0, 0)]
where the time goes in v7:
time: 61.8 us; the launch traced here: 61.3 us
  blocking collectives  23.7 us (38%)
  starting transfers between devices  21.2 us (34%)
  Pallas kernels  10 us (16%)
  waiting for transfers between devices  5.61 us (9%)
  between operations  0.75 us (1%)
    all_to_all x1, blocking collectives, shards(): z = lax.all_to_all(z, 'sec', 0, 0)  14.7 us
    pallas_call x9, Pallas kernels, call(): pl.pallas_call(kernel, out_shape=made, in_specs=[VMEM] * len(args), out_s...  10 us
    all_to_all x1, blocking collectives, shards(): out = lax.all_to_all(out, 'sec', 0, 0)  8.99 us
    ppermute x1, starting transfers between devices, shards(): xa = lax.ppermute(xa, 'gx', swap_pairs(n_gx, 1))  8.13 us
    ppermute x1, starting transfers between devices, shards(): ca = lax.ppermute(ca, 'gx', swap_pairs(n_gx, 1))  4.88 us
    ppermute x1, waiting for transfers between devices, shards(): ca = lax.ppermute(ca, 'gx', swap_pairs(n_gx, 1))  4.14 us
    ppermute x1, starting transfers between devices, shards(): yb = lax.ppermute(yb, 'gy', swap_pairs(n_gy, 1))  2.46 us
    ppermute x1, starting transfers between devices, shards(): ya = lax.ppermute(ya, 'gy', swap_pairs(n_gy, 0))  1.92 us
  transfers between devices with their start and end apart: 6, of which 2 were waited for; matrix products, arithmetic and copies ran while one was open for 0% of the time, Pallas kernels for 9%

profile of v7, /device:TPU:30, one launch (start us, length us, event | category | flops | bytes accessed | tf_op | source)
XLA Modules:
  0.0 61.3 jit_solution(5383804819369610255)
XLA Ops:
  0.6 1.2 %shard_map.176 = (f32[32,256]{1,0:T(8,128)S(1)}, f32[32,256]{1,0:T(8,128)S(1)}) custom-call(s32[32,256]{1,0:T(8,128)} %soil.3, s32[32,256]{1,0:T(8,128)} %geo.3, s32[32,256]{1,0:T(8,128)} %land.3, s32[32,256]{1,0:T(8,128)} %river.3, f32[32,256]{1,0:T(8,128)} %elev.3, f32[32,256]{1,0:T(8,128)} %rough.3, f32[32,256]{1,0:T(8,128)} %rain.3, f32[32,256]{1,0:T(8,128)} %evap.3, ...), custom_call_target="tpu_custom_call" | custom-call | tf_op jit(solution)/shard_map/pallas_call | solution.py:34
  1.8 1.9 %collective-permute-start = (f32[32,256]{1,0:T(8,128)S(1)}, f32[32,256]{1,0:T(8,128)S(1)}, u32[]{:S(2)}, u32[]{:S(2)}) collective-permute-start(f32[32,256]{1,0:T(8,128)S(1)} %get-tuple-element.31), channel_id=1, source_target_pairs={{0,1},{1,0},{2,3},{3,2},{4,5},{5,4},{6,7},{7,6},{8,9},{9,8},{10,11... | collective-permute-start | bytes 98312 | tf_op jit(solution)/shard_map/ppermute | solution.py:487
  3.7 2.5 %collective-permute-start.1 = (f32[32,256]{1,0:T(8,128)S(1)}, f32[32,256]{1,0:T(8,128)S(1)}, u32[]{:S(2)}, u32[]{:S(2)}) collective-permute-start(f32[32,256]{1,0:T(8,128)S(1)} %get-tuple-element.32), channel_id=1, source_target_pairs={{1,2},{2,1},{3,4},{4,3},{5,6},{6,5},{7,8},{8,7},{9,10},{10,9},{11,... | collective-permute-start | bytes 98312 | tf_op jit(solution)/shard_map/ppermute | solution.py:488
  6.2 1.3 %shard_map.177 = (f32[4,4,32,128]{3,2,1,0:T(8,128)S(1)}, f32[7,32,128]{2,1,0:T(8,128)S(1)}) custom-call(s32[32,256]{1,0:T(8,128)} %soil.3, s32[32,256]{1,0:T(8,128)} %geo.3, s32[32,256]{1,0:T(8,128)} %land.3, s32[32,256]{1,0:T(8,128)} %river.3, f32[32,256]{1,0:T(8,128)} %elev.3, f32[32,256]{1,0:T(8,128)} %rough.3, f32[32,256]{1,0:T(8,128)} %rain.3, ...), custom_call_target="tpu_custom_call" | custom-call | tf_op jit(solution)/shard_map/pallas_call | solution.py:34
  7.5 0.0 collective-permute-done.a_ref
  7.5 1.5 %collective-permute-done.1.b_ref = f32[32,256]{1,0:T(8,128)S(1)} collective-permute-done((f32[32,256]{1,0:T(8,128)S(1)}, f32[32,256]{1,0:T(8,128)S(1)}, u32[]{:S(2)}, u32[]{:S(2)}) %collective-permute-start.1) | collective-permute-done | bytes 32800 | tf_op jit(solution)/shard_map/ppermute | solution.py:488
  9.0 0.3 shard_map.178
  9.2 14.7 %all_to_all.10.z_ref = f32[4,3,32,128]{3,2,1,0:T(8,128)S(1)} all-to-all(f32[4,3,32,128]{3,2,1,0:T(8,128)S(1)} %get-tuple-element.40), channel_id=1, replica_groups=mesh['sec'=4,'gx'=8,'gy'=16] {'sec'}, dimensions={0} | all-to-all | bytes 393216 | tf_op jit(solution)/shard_map/all_to_all | solution.py:497
  24.0 8.1 %collective-permute-start.4 = (f32[192,128]{1,0:T(8,128)S(1)}, f32[192,128]{1,0:T(8,128)S(1)}, u32[]{:S(2)}, u32[]{:S(2)}) collective-permute-start(f32[192,128]{1,0:T(8,128)S(1)} %get-tuple-element.47), channel_id=1, source_target_pairs={{16,32},{32,16},{48,64},{64,48},{80,96},{96,80},{17,33},{33,17},{4... | collective-permute-start | bytes 294920 | tf_op jit(solution)/shard_map/ppermute | solution.py:505
  32.1 1.9 %collective-permute-start.5 = (f32[192,128]{1,0:T(8,128)S(1)}, f32[192,128]{1,0:T(8,128)S(1)}, u32[]{:S(2)}, u32[]{:S(2)}) collective-permute-start(f32[192,128]{1,0:T(8,128)S(1)} %get-tuple-element.48), channel_id=1, source_target_pairs={{0,16},{16,0},{32,48},{48,32},{64,80},{80,64},{96,112},{112,96},{1... | collective-permute-start | bytes 294920 | tf_op jit(solution)/shard_map/ppermute | solution.py:506
  34.0 4.9 %collective-permute-start.2 = (f32[128,128]{1,0:T(8,128)S(1)}, f32[128,128]{1,0:T(8,128)S(1)}, u32[]{:S(2)}, u32[]{:S(2)}) collective-permute-start(f32[128,128]{1,0:T(8,128)S(1)} %get-tuple-element.45), channel_id=1, source_target_pairs={{16,32},{32,16},{48,64},{64,48},{80,96},{96,80},{17,33},{33,17},{4... | collective-permute-start | bytes 196616 | tf_op jit(solution)/shard_map/ppermute | solution.py:500
  38.9 1.9 %collective-permute-start.3 = (f32[128,128]{1,0:T(8,128)S(1)}, f32[128,128]{1,0:T(8,128)S(1)}, u32[]{:S(2)}, u32[]{:S(2)}) collective-permute-start(f32[128,128]{1,0:T(8,128)S(1)} %get-tuple-element.46), channel_id=1, source_target_pairs={{0,16},{16,0},{32,48},{48,32},{64,80},{80,64},{96,112},{112,96},{1... | collective-permute-start | bytes 196616 | tf_op jit(solution)/shard_map/ppermute | solution.py:499
  40.8 1.7 %shard_map.180.table_ref = bf16[256,256]{1,0:T(8,128)(2,1)S(1)} custom-call(f32[256,28]{1,0:T(8,128)} %constant.4.clone.sel_ref, s32[256,128]{1,0:T(8,128)} %constant.5.clone.tap_ref, bf16[12,128]{1,0:T(8,128)(2,1)} %soil_ref, bf16[16,128]{1,0:T(8,128)(2,1)} %geo_ref.1, bf16[9,128,128]{2,1,0:T(8,128)(2,1)} %bitcast.2), custom_call_target="tpu_custom_call" | custom-call | tf_op jit(solution)/shard_map/pallas_call | solution.py:34
  42.6 4.1 %collective-permute-done.2.ca_ref = f32[128,128]{1,0:T(8,128)S(1)} collective-permute-done((f32[128,128]{1,0:T(8,128)S(1)}, f32[128,128]{1,0:T(8,128)S(1)}, u32[]{:S(2)}, u32[]{:S(2)}) %collective-permute-start.2) | collective-permute-done | bytes 65568 | tf_op jit(solution)/shard_map/ppermute | solution.py:500
  46.7 0.0 collective-permute-done.3.cb_ref
  46.7 2.3 %shard_map.181.cond_ref = f32[528,128]{1,0:T(8,128)S(1)} custom-call(f32[7,32,128]{2,1,0:T(8,128)S(1)} %get-tuple-element.44.c_ref, f32[128,128]{1,0:T(8,128)S(1)} %collective-permute-done.2.ca_ref, f32[128,128]{1,0:T(8,128)S(1)} %collective-permute-done.3.cb_ref, bf16[256,256]{1,0:T(8,128)(2,1)S(1)} %shard_map.180.table_ref, bf16[8,128]{1,0:T(8,128)(2,1)} %bitcast.3), custom_call_target="tpu_custom_call" | custom-call | tf_op jit(solution)/shard_map/pallas_call | solution.py:34
  49.1 0.3 shard_map.182
  49.4 0.0 collective-permute-done.4.a_ref
  49.4 0.0 collective-permute-done.5.b_ref
  49.4 2.2 %shard_map.183 = f32[4,48,128]{2,1,0:T(8,128)S(1)} custom-call(f32[7,32,128]{2,1,0:T(8,128)S(1)} %get-tuple-element.44.c_ref, f32[128,128]{1,0:T(8,128)S(1)} %collective-permute-done.2.ca_ref, f32[128,128]{1,0:T(8,128)S(1)} %collective-permute-done.3.cb_ref, f32[192,128]{1,0:T(8,128)S(1)} %collective-permute-done.4.a_ref, ...), custom_call_target="tpu_custom_call" | custom-call | tf_op jit(solution)/shard_map/pallas_call | solution.py:34
  51.6 9.0 %all_to_all.11.z_ref = f32[4,48,128]{2,1,0:T(8,128)S(1)} all-to-all(f32[4,48,128]{2,1,0:T(8,128)S(1)} %shard_map.183), channel_id=1, replica_groups=mesh['sec'=4,'gx'=8,'gy'=16] {'sec'}, dimensions={0} | all-to-all | bytes 196608 | tf_op jit(solution)/shard_map/all_to_all | solution.py:524
  60.6 0.7 %shard_map.184 = (f32[2,32,256]{2,1,0:T(8,128)}, f32[32,256]{1,0:T(8,128)}) custom-call(f32[4,48,128]{2,1,0:T(8,128)S(1)} %all_to_all.11.z_ref), custom_call_target="tpu_custom_call" | custom-call | tf_op jit(solution)/shard_map/pallas_call | solution.py:34
  (1 shorter events, 0.0 us)
Async XLA Ops:
  1.8 5.7 %collective-permute-start = (f32[32,256]{1,0:T(8,128)S(1)}, f32[32,256]{1,0:T(8,128)S(1)}, u32[]{:S(2)}, u32[]{:S(2)}) collective-permute-start(f32[32,256]{1,0:T(8,128)S(1)} %get-tuple-element.31), channel_id=1, source_target_pairs={{0,1},{1,0},{2,3},{3,2},{4,5},{5,4},{6,7},{7,6},{8,9},{9,8},{10,11... | collective-permute-start | bytes 98312 | tf_op jit(solution)/shard_map/ppermute | solution.py:487
  3.7 5.2 %collective-permute-start.1 = (f32[32,256]{1,0:T(8,128)S(1)}, f32[32,256]{1,0:T(8,128)S(1)}, u32[]{:S(2)}, u32[]{:S(2)}) collective-permute-start(f32[32,256]{1,0:T(8,128)S(1)} %get-tuple-element.32), channel_id=1, source_target_pairs={{1,2},{2,1},{3,4},{4,3},{5,6},{6,5},{7,8},{8,7},{9,10},{10,9},{11,... | collective-permute-start | bytes 98312 | tf_op jit(solution)/shard_map/ppermute | solution.py:488
  24.0 25.4 %collective-permute-start.4 = (f32[192,128]{1,0:T(8,128)S(1)}, f32[192,128]{1,0:T(8,128)S(1)}, u32[]{:S(2)}, u32[]{:S(2)}) collective-permute-start(f32[192,128]{1,0:T(8,128)S(1)} %get-tuple-element.47), channel_id=1, source_target_pairs={{16,32},{32,16},{48,64},{64,48},{80,96},{96,80},{17,33},{33,17},{4... | collective-permute-start | bytes 294920 | tf_op jit(solution)/shard_map/ppermute | solution.py:505
  32.1 17.3 %collective-permute-start.5 = (f32[192,128]{1,0:T(8,128)S(1)}, f32[192,128]{1,0:T(8,128)S(1)}, u32[]{:S(2)}, u32[]{:S(2)}) collective-permute-start(f32[192,128]{1,0:T(8,128)S(1)} %get-tuple-element.48), channel_id=1, source_target_pairs={{0,16},{16,0},{32,48},{48,32},{64,80},{80,64},{96,112},{112,96},{1... | collective-permute-start | bytes 294920 | tf_op jit(solution)/shard_map/ppermute | solution.py:506
  34.0 12.7 %collective-permute-start.2 = (f32[128,128]{1,0:T(8,128)S(1)}, f32[128,128]{1,0:T(8,128)S(1)}, u32[]{:S(2)}, u32[]{:S(2)}) collective-permute-start(f32[128,128]{1,0:T(8,128)S(1)} %get-tuple-element.45), channel_id=1, source_target_pairs={{16,32},{32,16},{48,64},{64,48},{80,96},{96,80},{17,33},{33,17},{4... | collective-permute-start | bytes 196616 | tf_op jit(solution)/shard_map/ppermute | solution.py:500
  38.9 7.8 %collective-permute-start.3 = (f32[128,128]{1,0:T(8,128)S(1)}, f32[128,128]{1,0:T(8,128)S(1)}, u32[]{:S(2)}, u32[]{:S(2)}) collective-permute-start(f32[128,128]{1,0:T(8,128)S(1)} %get-tuple-element.46), channel_id=1, source_target_pairs={{0,16},{16,0},{32,48},{48,32},{64,80},{80,64},{96,112},{112,96},{1... | collective-permute-start | bytes 196616 | tf_op jit(solution)/shard_map/ppermute | solution.py:499
